TPU v7x, 128 devices: a whole 4x4x4 slice. The times are simulated.
128 devices in a mesh: gx: 4 (over y), gy: 8 (over x, core), gz: 4 (over z).
Axes of the slice: x: 4, y: 4, z: 4, core: 2. Of those that a mesh axis runs over, the one named last changes fastest.
Arguments:
- volume: bfloat16 [48, 64, 65536], P(None, 'gz', ('gx', 'gy')), may hold values from -6 to 6
- tissue: int32 [32, 32, 4], replicated, may hold values 0 or 1
- w_down1: bfloat16 [8, 64, 48], replicated, may hold values from -0.4375 to 0.4375
- b_down1: float32 [64], replicated, may hold values from -1.5 to 1.5
- w_conv1a: bfloat16 [27, 64, 64], replicated, may hold values from -0.21875 to 0.21875
- b_conv1a: float32 [64], replicated, may hold values from -1.5 to 1.5
- w_conv1b: bfloat16 [27, 64, 64], replicated, may hold values from -0.21875 to 0.21875
- b_conv1b: float32 [64], replicated, may hold values from -1.5 to 1.5
- w_down2: bfloat16 [8, 96, 64], replicated, may hold values from -0.375 to 0.375
- b_down2: float32 [96], replicated, may hold values from -1.5 to 1.5
- w_conv2a: bfloat16 [27, 96, 96], replicated, may hold values from -0.15625 to 0.15625
- b_conv2a: float32 [96], replicated, may hold values from -1.5 to 1.5
- w_conv2b: bfloat16 [27, 96, 96], replicated, may hold values from -0.15625 to 0.15625
- b_conv2b: float32 [96], replicated, may hold values from -1.5 to 1.5
Outputs:
- level_one: bfloat16 [64, 32, 16384], P(None, 'gz', ('gx', 'gy'))
- level_two: bfloat16 [96, 16, 4096], P(None, 'gz', ('gx', 'gy'))
All inputs are finite; a program needn't handle non-finite values.
Results may differ from a plain program's by a relative error of at most 0.012.
Values may be sent and summed in bfloat16 or wider, within the bound.
A program may use at most 128 MiB of HBM per device.

v0:
```python
import functools

import jax
import jax.numpy as jnp
from jax import lax
from jax.experimental import pallas as pl
from jax.experimental.pallas import tpu as pltpu
from jax.sharding import PartitionSpec as P

CX = 64
CY = 32
AXES = ("gx", "gy", "gz")
MESH = pl.DeviceIdType.MESH
DIRS = [
    (dx, dy, dz)
    for dx in (-1, 0, 1)
    for dy in (-1, 0, 1)
    for dz in (-1, 0, 1)
    if (dx, dy, dz) != (0, 0, 0)
]


def rim_kernel(width, f_ref, p_ref, local_sem, send_sem, recv_sem):
    size_z, size_y, size_x, _ = f_ref.shape
    sizes = (size_x, size_y, size_z)
    index = [lax.axis_index(a) for a in AXES]
    count = [lax.axis_size(a) for a in AXES]

    def exists(d):
        ok = True
        for a in range(3):
            if d[a] == -1:
                ok = jnp.logical_and(ok, index[a] > 0)
            elif d[a] == 1:
                ok = jnp.logical_and(ok, index[a] < count[a] - 1)
        return ok

    def device(d):
        return tuple(index[a] + d[a] for a in range(3))

    def source(a, step):
        s = sizes[a]
        if step == -1:
            return slice(0, width)
        if step == 1:
            return slice(s - width, s)
        return slice(0, s)

    def side(a, step):
        s = sizes[a]
        if step == -1:
            return slice(0, width)
        if step == 1:
            return slice(s + width, s + 2 * width)
        return slice(width, width + s)

    barrier = pltpu.get_barrier_semaphore()
    for d in DIRS:
        @pl.when(exists(d))
        def _():
            pl.semaphore_signal(barrier, inc=1, device_id=device(d), device_id_type=MESH)

    local = pltpu.make_async_copy(
        f_ref, p_ref.at[width:width + size_z, width:width + size_y, width:width + size_x, :],
        local_sem.at[0])
    local.start()

    for d in DIRS:
        @pl.when(jnp.logical_not(exists(d)))
        def _():
            sx, sy, sz = (side(a, d[a]) for a in range(3))
            region = p_ref.at[sz, sy, sx, :]
            region[...] = jnp.zeros(region.shape, region.dtype)

    peers = 1
    for a in range(3):
        below = (index[a] + count[a] - 1) // count[a]
        above = (2 * count[a] - 2 - index[a]) // count[a]
        peers = peers * (1 + below + above)
    pl.semaphore_wait(barrier, peers - 1)

    copies = []
    for k, d in enumerate(DIRS):
        sx, sy, sz = (source(a, d[a]) for a in range(3))
        tx, ty, tz = (side(a, -d[a]) for a in range(3))
        copy = pltpu.make_async_remote_copy(
            src_ref=f_ref.at[sz, sy, sx, :],
            dst_ref=p_ref.at[tz, ty, tx, :],
            send_sem=send_sem.at[k],
            recv_sem=recv_sem.at[k],
            device_id=device(d),
            device_id_type=MESH,
        )
        copies.append((d, copy))

        @pl.when(exists(d))
        def _():
            copy.start()

    local.wait()
    for d, copy in copies:
        @pl.when(exists(d))
        def _():
            copy.wait_send()

        @pl.when(exists(tuple(-v for v in d)))
        def _():
            copy.wait_recv()


def with_rim(field, width, collective_id):
    size_z, size_y, size_x, chans = field.shape
    return pl.pallas_call(
        functools.partial(rim_kernel, width),
        out_shape=jax.ShapeDtypeStruct(
            (size_z + 2 * width, size_y + 2 * width, size_x + 2 * width, chans), field.dtype),
        in_specs=[pl.BlockSpec(memory_space=pltpu.VMEM)],
        out_specs=pl.BlockSpec(memory_space=pltpu.VMEM),
        scratch_shapes=[
            pltpu.SemaphoreType.DMA((1,)),
            pltpu.SemaphoreType.DMA((len(DIRS),)),
            pltpu.SemaphoreType.DMA((len(DIRS),)),
        ],
        compiler_params=pltpu.CompilerParams(collective_id=collective_id, has_side_effects=True),
    )(field)


def region_mask(tissue, repeats, block_starts, extents, margin):
    padded = jnp.pad(tissue, 1)
    counts = [extents[d] // repeats[d] + 2 for d in range(3)]
    starts = [jnp.asarray(block_starts[d], dtype=jnp.int32) for d in range(3)]
    table = lax.dynamic_slice(padded, starts, counts)
    for d in range(3):
        table = jnp.repeat(table, repeats[d], axis=d)
    table = table[
        repeats[0] - margin : repeats[0] + extents[0] + margin,
        repeats[1] - margin : repeats[1] + extents[1] + margin,
        repeats[2] - margin : repeats[2] + extents[2] + margin,
    ]
    return table.astype(jnp.float32).transpose(2, 1, 0)[..., None]


def finish(summed, offsets, tissue_mask):
    return (jnp.maximum(summed + offsets, 0.0) * tissue_mask).astype(jnp.bfloat16)


def conv_taps(padded, weights):
    size_z = padded.shape[0] - 2
    stacked = jnp.concatenate([padded[k:k + size_z] for k in range(3)], axis=-1)
    kernel = weights.reshape(3, 3, 3, weights.shape[1], weights.shape[2]).transpose(1, 0, 2, 4, 3)
    kernel = kernel.reshape(3, 3, 3 * weights.shape[2], weights.shape[1])
    return lax.conv_general_dilated(
        stacked, kernel, (1, 1), "VALID",
        dimension_numbers=("NHWC", "HWIO", "NHWC"), preferred_element_type=jnp.float32)


def down_first(grid, weights):
    channels, size_z, size_y, size_x = grid.shape
    split = grid.reshape(channels, size_z // 2, 2, size_y // 2, 2, size_x // 2, 2)
    grouped = weights.reshape(2, 2, 2, weights.shape[1], weights.shape[2])
    return jnp.einsum("abkoi,izkybxa->zyxo", grouped, split, preferred_element_type=jnp.float32)


def down_cells(field, weights):
    size_z, size_y, size_x, channels = field.shape
    split = field.reshape(size_z // 2, 2, size_y // 2, 2, size_x // 2, 2, channels)
    grouped = weights.reshape(2, 2, 2, weights.shape[1], weights.shape[2])
    return jnp.einsum("abkoi,zkybxai->zyxo", grouped, split, preferred_element_type=jnp.float32)


def packed(field):
    size_z, size_y, size_x, chans = field.shape
    return field.transpose(3, 0, 1, 2).reshape(chans, size_z, size_y * size_x)


def local(volume, tissue, w_down1, b_down1, w_conv1a, b_conv1a, w_conv1b, b_conv1b,
          w_down2, b_down2, w_conv2a, b_conv2a, w_conv2b, b_conv2b):
    index_x = lax.axis_index("gx")
    index_y = lax.axis_index("gy")
    index_z = lax.axis_index("gz")
    grid_zero = volume.reshape(volume.shape[0], volume.shape[1], CY, CX)
    first_x = CX // 2
    first_y = CY // 2
    first_z = volume.shape[1] // 2
    first_blocks = (index_x * (first_x // 4), index_y * (first_y // 4), index_z * (first_z // 8))
    mask_one = region_mask(tissue, (4, 4, 8), first_blocks, (first_x, first_y, first_z), 0)
    mask_one_wide = region_mask(tissue, (4, 4, 8), first_blocks, (first_x, first_y, first_z), 1)
    down_one = finish(down_first(grid_zero, w_down1), b_down1, mask_one)
    inner_one = finish(conv_taps(with_rim(down_one, 2, 0), w_conv1a), b_conv1a, mask_one_wide)
    feat_one = finish(conv_taps(inner_one, w_conv1b), b_conv1b, mask_one)
    second_x = first_x // 2
    second_y = first_y // 2
    second_z = first_z // 2
    second_blocks = (index_x * (second_x // 2), index_y * (second_y // 2), index_z * (second_z // 4))
    mask_two = region_mask(tissue, (2, 2, 4), second_blocks, (second_x, second_y, second_z), 0)
    mask_two_wide = region_mask(tissue, (2, 2, 4), second_blocks, (second_x, second_y, second_z), 1)
    down_two = finish(down_cells(feat_one, w_down2), b_down2, mask_two)
    middle = finish(conv_taps(with_rim(down_two, 2, 1), w_conv2a), b_conv2a, mask_two_wide)
    feat_two = finish(conv_taps(middle, w_conv2b), b_conv2b, mask_two)
    return (packed(feat_one), packed(feat_two))


def solution(mesh):
    return jax.shard_map(
        local,
        mesh=mesh,
        in_specs=(P(None, "gz", ("gx", "gy")),) + (P(),) * 13,
        out_specs=(P(None, "gz", ("gx", "gy")), P(None, "gz", ("gx", "gy"))),
        check_vma=False,
    )
```

profile of v0, /device:TPU:1, one launch (start us, length us, event | category | flops | bytes accessed | tf_op | source)
XLA Modules:
  0.0 94.4 jit_solution(13183707039826713953)
XLA Ops:
  0.6 0.0 copy-start
  0.7 0.9 pad_dynamic-slice_fusion
  1.5 0.1 copy.33
  1.7 0.1 fusion.58
  1.8 0.0 copy-start.7
  1.8 0.0 copy-start.10
  1.8 0.0 copy-start.11
  1.8 8.7 %copy.30 = bf16[48,16,2048]{0,2,1:T(8,128)(2,1)} copy(bf16[48,16,2048]{2,1,0:T(8,128)(2,1)} %param.14) | data formatting | bytes 6291456 | tf_op args[0]
  10.5 0.0 copy-done.10
  10.5 6.6 %fusion.18.f_ref = bf16[8,16,32,64]{3,2,1,0:T(8,128)(2,1)} fusion(bf16[2,2,2,64,48,1,1]{3,4,2,1,0,6,5:T(8,128)(2,1)S(1)} %bitcast.136, bf16[48,8,2,16,2,32,2]{0,6,5,4,3,2,1:T(2,128)(2,1)} %bitcast.115, f32[8,16,32]{2,1,0:T(8,128)S(1)} %fusion.58, f32[64]{0:T(128)S(1)} %copy-done.11), kind=kOutput, calls=%fused_computation.23 | convolution fusion | flops 202375168 | bytes 3735808 | tf_op jit(solution)/shard_map/abkoi,izkybxa->zyxo/dot_general | solution.py:161
  17.1 17.5 %shard_map.149 = bf16[12,20,36,64]{3,2,1,0:T(8,128)(2,1)} custom-call(bf16[8,16,32,64]{3,2,1,0:T(8,128)(2,1)} %fusion.18.f_ref), custom_call_target="tpu_custom_call" | custom-call | tf_op jit(solution)/shard_map/pallas_call | solution.py:113
  34.6 3.9 %fusion.63 = (bf16[10,20,36,64]{3,2,1,0:T(8,128)(2,1)S(1)}, bf16[10,20,36,64]{3,2,1,0:T(8,128)(2,1)S(1)}, bf16[10,20,36,64]{3,2,1,0:T(8,128)(2,1)S(1)}) fusion(bf16[12,20,36,64]{3,2,1,0:T(8,128)(2,1)} %shard_map.149), kind=kLoop, calls=%fused_computation.63 | loop fusion | bytes 5529600 | tf_op jit(solution)/shard_map/slice | solution.py:149
  38.4 0.0 copy-start.5
  38.5 0.0 copy-start.12
  38.5 3.5 %pad_maximum_fusion = bf16[10,20,36,192]{3,2,1,0:T(8,128)(2,1)} fusion(bf16[10,20,36,64]{3,2,1,0:T(8,128)(2,1)S(1)} %get-tuple-element.10, bf16[10,20,36,64]{3,2,1,0:T(8,128)(2,1)S(1)} %get-tuple-element.11, bf16[10,20,36,64]{3,2,1,0:T(8,128)(2,1)S(1)} %get-tuple-element.9), kind=kLoop, calls=%fused_computation.7 | loop fusion | flops 8294400 | bytes 5529600 | tf_op jit(solution)/shard_map/concatenate | solution.py:149
  41.9 0.1 fusion.57
  42.1 0.2 copy.36
  42.3 0.3 copy.34
  42.6 12.4 %multiply_convert_fusion = bf16[10,18,34,64]{3,0,2,1:T(8,128)(2,1)S(1)} fusion(f32[10,18,34]{0,2,1:T(8,128)S(1)} %copy.36, f32[64]{0:T(128)S(1)} %copy-done.12, bf16[3,3,192,64]{3,2,1,0:T(8,128)(2,1)S(1)} %bitcast.131, bf16[10,20,36,192]{3,2,1,0:T(8,128)(2,1)} %pad_maximum_fusion), kind=kOutput, calls=%fused_computation.6 | convolution fusion | flops 1355212800 | bytes 3794080 | tf_op jit(solution)/shard_map/conv_general_dilated | solution.py:152
  54.9 0.0 copy-start.6
  55.0 1.7 %fusion.62 = (bf16[8,18,34,64]{3,0,2,1:T(8,128)(2,1)S(1)}, bf16[8,18,34,64]{3,0,2,1:T(8,128)(2,1)S(1)}, bf16[8,18,34,64]{3,0,2,1:T(8,128)(2,1)}) fusion(bf16[10,18,34,64]{3,0,2,1:T(8,128)(2,1)S(1)} %multiply_convert_fusion), kind=kLoop, calls=%fused_computation.62 | loop fusion | bytes 3760128 | tf_op jit(solution)/shard_map/slice | solution.py:149
  56.7 0.2 copy.37
  56.9 0.0 copy-start.8
  57.0 0.0 copy-start.9
  57.0 6.8 %fusion.6 = f32[8,16,32,64]{3,0,2,1:T(8,128)S(1)} fusion(bf16[3,3,192,64]{3,2,1,0:T(8,128)(2,1)S(1)} %bitcast.130, bf16[8,18,34,64]{3,0,2,1:T(8,128)(2,1)S(1)} %get-tuple-element.7, bf16[8,18,34,64]{3,0,2,1:T(8,128)(2,1)} %get-tuple-element.8, bf16[8,18,34,64]{3,0,2,1:T(8,128)(2,1)S(1)} %get-tuple-element.6), kind=kOutput, calls=%fused_computation.9 | convolution fusion | flops 911609856 | bytes 3149824 | tf_op jit(solution)/shard_map/conv_general_dilated | solution.py:152
  63.8 0.0 copy-start.13
  63.8 0.7 fusion.21
  64.6 0.1 copy.41
  64.8 0.1 fusion.60
  64.9 1.0 %fusion.51.f_ref = bf16[4,8,16,96]{3,2,1,0:T(8,128)(2,1)} fusion(bf16[2,2,2,96,64,1,1]{3,4,2,1,0,6,5:T(8,128)(2,1)S(1)} %bitcast.114, bf16[4,2,8,2,16,2,64]{6,5,4,3,2,1,0:T(2,128)(2,1)S(1)} %bitcast.118, f32[4,8,16]{2,1,0:T(8,128)S(1)} %fusion.60, f32[96]{0:T(128)S(1)} %copy-done.13), kind=kOutput, calls=%fused_computation.43 | convolution fusion | flops 50528256 | bytes 723328 | tf_op jit(solution)/shard_map/abkoi,zkybxai->zyxo/dot_general | solution.py:168
  65.9 8.9 %shard_map.150 = bf16[8,12,20,96]{3,2,1,0:T(8,128)(2,1)} custom-call(bf16[4,8,16,96]{3,2,1,0:T(8,128)(2,1)} %fusion.51.f_ref), custom_call_target="tpu_custom_call" | custom-call | tf_op jit(solution)/shard_map/pallas_call | solution.py:113
  74.8 1.6 %fusion.64 = (bf16[6,12,20,96]{3,2,1,0:T(8,128)(2,1)S(1)}, bf16[6,12,20,96]{3,2,1,0:T(8,128)(2,1)S(1)}, bf16[6,12,20,96]{3,2,1,0:T(8,128)(2,1)S(1)}) fusion(bf16[8,12,20,96]{3,2,1,0:T(8,128)(2,1)} %shard_map.150), kind=kLoop, calls=%fused_computation.64 | loop fusion | bytes 1658880 | tf_op jit(solution)/shard_map/slice | solution.py:149
  76.4 0.7 maximum_bitcast_fusion
  77.1 0.1 copy.59
  77.3 0.2 pad.8.clone
  77.5 1.0 %reshape.98 = bf16[12,6,8,3,288]{4,3,2,1,0:T(4,128)(2,1)S(1)} reshape(bf16[12,6,24,288]{3,2,1,0:T(8,128)(2,1)S(1)} %pad.8.clone) | data formatting | bytes 1990656 | tf_op jit(solution)/shard_map/conv_general_dilated | solution.py:152
  78.4 0.5 slice.74
  79.0 0.0 copy-start.3
  79.0 0.0 copy-start.14
  79.0 0.0 copy-start.17
  79.0 3.3 %fusion.5 = bf16[12,6,8,5,288]{4,3,2,1,0:T(8,128)(2,1)} fusion(bf16[12,6,7,2,288]{4,3,2,1,0:T(2,128)(2,1)S(1)} %slice.74, bf16[12,6,8,3,288]{4,3,2,1,0:T(4,128)(2,1)S(1)} %reshape.98), kind=kLoop, calls=%fused_computation.8 | loop fusion | flops 4976640 | bytes 3234816 | tf_op jit(solution)/shard_map/conv_general_dilated | solution.py:152
  82.3 0.3 copy.44
  82.7 4.3 %fusion.32 = f32[10,48,3,96]{3,1,2,0:T(8,128)S(1)} fusion(bf16[3,3,288,96]{3,2,1,0:T(8,128)(2,1)S(1)} %bitcast.125, bf16[12,6,8,5,288]{4,3,2,1,0:T(8,128)(2,1)} %fusion.5, f32[96]{0:T(128)S(1)} %copy-done.14, pred[48,3]{0,1:T(4,128)(4,1)S(1)} %copy-done.17), kind=kOutput, calls=%fused_computation.31 | convolution fusion | flops 717050880 | bytes 2710032 | tf_op jit(solution)/shard_map/conv_general_dilated | solution.py:152
  87.0 0.4 copy.45
  87.3 0.3 reshape.102
  87.7 0.1 fusion.59
  87.8 0.3 fusion.54
  88.1 0.1 fusion.65
  88.2 0.4 maximum_bitcast_fusion.1
  88.6 0.2 copy.60
  88.8 0.0 copy-start.4
  88.8 0.3 pad.10.clone
  89.1 0.0 copy-start.15
  89.1 0.0 copy-start.16
  89.1 0.1 slice.80
  89.3 0.6 fusion.35
  89.9 0.0 copy-done.4
  89.9 0.3 copy.49
  90.2 1.3 %fusion.45 = f32[8,32,3,96]{3,1,2,0:T(8,128)S(1)} fusion(bf16[3,3,288,96]{3,2,1,0:T(8,128)(2,1)S(1)} %bitcast.126, bf16[10,4,8,5,288]{4,1,3,2,0:T(4,128)(2,1)S(1)} %fusion.35, f32[96]{0:T(128)S(1)} %copy-done.15, pred[32,3]{0,1:T(4,128)(4,1)S(1)} %copy-done.16), kind=kOutput, calls=%fused_computation.38 | convolution fusion | flops 382427136 | bytes 1714656 | tf_op jit(solution)/shard_map/conv_general_dilated | solution.py:152
  91.5 0.2 copy.50
  91.8 0.1 copy.51
  91.9 0.1 fusion.56
  92.0 0.8 copy.54
  92.8 1.6 %copy.53 = bf16[64,8,512]{2,1,0:T(8,128)(2,1)} copy(bf16[64,8,512]{0,2,1:T(8,128)(2,1)S(1)} %bitcast.119) | data formatting | bytes 1048576
  (29 shorter events, 0.2 us)
Async XLA Ops:
  0.6 64.2 %copy-start = (bf16[8,96,64]{1,2,0:T(8,128)(2,1)S(1)}, bf16[8,96,64]{1,2,0:T(8,128)(2,1)}, u32[]{:S(2)}) copy-start(bf16[8,96,64]{1,2,0:T(8,128)(2,1)} %param.22) | copy-start | bytes 294916
  1.8 8.7 %copy-start.7 = (f32[8,16,32]{2,1,0:T(8,128)}, f32[8,16,32]{2,1,0:T(8,128)S(1)}, u32[]{:S(2)}) copy-start(f32[8,16,32]{2,1,0:T(8,128)S(1)} %fusion.58) | copy-start | bytes 49156
  1.8 8.7 %copy-start.10 = (bf16[8,64,48]{1,2,0:T(8,128)(2,1)S(1)}, bf16[8,64,48]{1,2,0:T(8,128)(2,1)}, u32[]{:S(2)}) copy-start(bf16[8,64,48]{1,2,0:T(8,128)(2,1)} %param.16) | copy-start | bytes 147460
  1.8 8.7 %copy-start.11 = (f32[64]{0:T(128)S(1)}, f32[64]{0:T(128)}, u32[]{:S(2)}) copy-start(f32[64]{0:T(128)} %param.17) | copy-start | bytes 772
  38.4 3.9 %copy-start.5 = (bf16[27,64,64]{2,1,0:T(8,128)(2,1)S(1)}, bf16[27,64,64]{2,1,0:T(8,128)(2,1)}, u32[]{:S(2)}) copy-start(bf16[27,64,64]{2,1,0:T(8,128)(2,1)} %param.18) | copy-start | bytes 663556
  38.5 4.1 %copy-start.12 = (f32[64]{0:T(128)S(1)}, f32[64]{0:T(128)}, u32[]{:S(2)}) copy-start(f32[64]{0:T(128)} %param.19) | copy-start | bytes 772
  54.9 1.8 %copy-start.6 = (bf16[27,64,64]{2,1,0:T(8,128)(2,1)S(1)}, bf16[27,64,64]{2,1,0:T(8,128)(2,1)}, u32[]{:S(2)}) copy-start(bf16[27,64,64]{2,1,0:T(8,128)(2,1)} %param.20) | copy-start | bytes 663556
  56.9 6.8 %copy-start.8 = (f32[8,16,32]{2,1,0:T(8,128)S(1)}, f32[8,16,32]{2,1,0:T(8,128)}, u32[]{:S(2)}) copy-start(f32[8,16,32]{2,1,0:T(8,128)} %copy-done.7) | copy-start | bytes 49156
  57.0 6.8 %copy-start.9 = (f32[64]{0:T(128)S(1)}, f32[64]{0:T(128)}, u32[]{:S(2)}) copy-start(f32[64]{0:T(128)} %param.21) | copy-start | bytes 772
  63.8 1.1 %copy-start.13 = (f32[96]{0:T(128)S(1)}, f32[96]{0:T(128)}, u32[]{:S(2)}) copy-start(f32[96]{0:T(128)} %param.23) | copy-start | bytes 1156
  64.6 11.8 %copy-start.1 = (bf16[8,16,32,64]{3,2,1,0:T(8,128)(2,1)}, bf16[8,16,32,64]{3,2,1,0:T(8,128)(2,1)S(1)}, u32[]{:S(2)}) copy-start(bf16[8,16,32,64]{3,2,1,0:T(8,128)(2,1)S(1)} %fusion.21) | copy-start | bytes 1572868
  79.0 3.4 %copy-start.3 = (bf16[27,96,96]{2,1,0:T(8,128)(2,1)S(1)}, bf16[27,96,96]{2,1,0:T(8,128)(2,1)}, u32[]{:S(2)}) copy-start(bf16[27,96,96]{2,1,0:T(8,128)(2,1)} %param.24) | copy-start | bytes 1492996
  79.0 3.7 %copy-start.14 = (f32[96]{0:T(128)S(1)}, f32[96]{0:T(128)}, u32[]{:S(2)}) copy-start(f32[96]{0:T(128)} %param.25) | copy-start | bytes 1156
  79.0 3.7 %copy-start.17 = (pred[48,3]{0,1:T(4,128)(4,1)S(1)}, pred[48,3]{0,1:T(4,128)(4,1)}, u32[]{:S(2)}) copy-start(pred[48,3]{0,1:T(4,128)(4,1)} %constant.39) | copy-start | bytes 436
  88.8 1.1 %copy-start.4 = (bf16[27,96,96]{2,1,0:T(8,128)(2,1)S(1)}, bf16[27,96,96]{2,1,0:T(8,128)(2,1)}, u32[]{:S(2)}) copy-start(bf16[27,96,96]{2,1,0:T(8,128)(2,1)} %param.26) | copy-start | bytes 1492996
  89.1 1.1 %copy-start.15 = (f32[96]{0:T(128)S(1)}, f32[96]{0:T(128)}, u32[]{:S(2)}) copy-start(f32[96]{0:T(128)} %param.27) | copy-start | bytes 1156
  89.1 1.1 %copy-start.16 = (pred[32,3]{0,1:T(4,128)(4,1)S(1)}, pred[32,3]{0,1:T(4,128)(4,1)}, u32[]{:S(2)}) copy-start(pred[32,3]{0,1:T(4,128)(4,1)} %constant.38) | copy-start | bytes 292
  91.5 1.3 %copy-start.2 = (bf16[8,16,32,64]{3,2,1,0:T(8,128)(2,1)S(1)}, bf16[8,16,32,64]{3,2,1,0:T(8,128)(2,1)}, u32[]{:S(2)}) copy-start(bf16[8,16,32,64]{3,2,1,0:T(8,128)(2,1)} %copy-done.1) | copy-start | bytes 1572868
where the time goes:
time: 94.9 us; the launch traced here: 94.4 us
  matrix products  32.3 us (34%)
  Pallas kernels  26.4 us (28%)
  local copies, waits for them, and re-layouts  24.6 us (26%)
  other arithmetic  9.98 us (11%)
  between operations  1.12 us (1%)
    pallas_call x2, Pallas kernels, with_rim(): pl.pallas_call(functools.partial(rim_kernel, width), out_shape=jax.ShapeD...  26.4 us
    conv_general_dilated x4, matrix products, conv_taps(): lax.conv_general_dilated(stacked, kernel, (1, 1), 'VALID', dimension_numb...  24.7 us
    unnamed x41, local copies, waits for them, and re-layouts  11.6 us
    slice x4, local copies, waits for them, and re-layouts, conv_taps(): stacked = jnp.concatenate([padded[k:k + size_z] for k in range(3)], axis=-1)  7.28 us
    dot_general x1, matrix products, down_first(): jnp.einsum('abkoi,izkybxa->zyxo', grouped, split, preferred_element_type=...  6.56 us
    concatenate x3, other arithmetic, conv_taps(): stacked = jnp.concatenate([padded[k:k + size_z] for k in range(3)], axis=-1)  4.62 us
    conv_general_dilated x2, other arithmetic, conv_taps(): lax.conv_general_dilated(stacked, kernel, (1, 1), 'VALID', dimension_numb...  3.87 us

commit v1 on v0

--- a/solution.py
+++ b/solution.py
@@ -20,7 +20,7 @@
 ]
 
 
-def rim_kernel(width, f_ref, p_ref, local_sem, send_sem, recv_sem):
+def rim_kernel(width, f_ref, p_ref, send_sem, recv_sem):
     size_z, size_y, size_x, _ = f_ref.shape
     sizes = (size_x, size_y, size_z)
     index = [lax.axis_index(a) for a in AXES]
@@ -60,10 +60,7 @@
         def _():
             pl.semaphore_signal(barrier, inc=1, device_id=device(d), device_id_type=MESH)
 
-    local = pltpu.make_async_copy(
-        f_ref, p_ref.at[width:width + size_z, width:width + size_y, width:width + size_x, :],
-        local_sem.at[0])
-    local.start()
+    p_ref[width:width + size_z, width:width + size_y, width:width + size_x, :] = f_ref[...]
 
     for d in DIRS:
         @pl.when(jnp.logical_not(exists(d)))
@@ -97,7 +94,6 @@
         def _():
             copy.start()
 
-    local.wait()
     for d, copy in copies:
         @pl.when(exists(d))
         def _():
@@ -117,7 +113,6 @@
         in_specs=[pl.BlockSpec(memory_space=pltpu.VMEM)],
         out_specs=pl.BlockSpec(memory_space=pltpu.VMEM),
         scratch_shapes=[
-            pltpu.SemaphoreType.DMA((1,)),
             pltpu.SemaphoreType.DMA((len(DIRS),)),
             pltpu.SemaphoreType.DMA((len(DIRS),)),
         ],

time: 94.9 us -> 94.9 us (level)
  no operation moved by 1% of the time
where the time goes in v1:
time: 94.9 us; the launch traced here: 94.4 us
  matrix products  32.3 us (34%)
  Pallas kernels  26.4 us (28%)
  local copies, waits for them, and re-layouts  24.6 us (26%)
  other arithmetic  9.98 us (11%)
  between operations  1.12 us (1%)
    pallas_call x2, Pallas kernels, with_rim(): pl.pallas_call(functools.partial(rim_kernel, width), out_shape=jax.ShapeD...  26.4 us
    conv_general_dilated x4, matrix products, conv_taps(): lax.conv_general_dilated(stacked, kernel, (1, 1), 'VALID', dimension_numb...  24.7 us
    unnamed x41, local copies, waits for them, and re-layouts  11.6 us
    slice x4, local copies, waits for them, and re-layouts, conv_taps(): stacked = jnp.concatenate([padded[k:k + size_z] for k in range(3)], axis=-1)  7.28 us
    dot_general x1, matrix products, down_first(): jnp.einsum('abkoi,izkybxa->zyxo', grouped, split, preferred_element_type=...  6.56 us
    concatenate x3, other arithmetic, conv_taps(): stacked = jnp.concatenate([padded[k:k + size_z] for k in range(3)], axis=-1)  4.62 us
    conv_general_dilated x2, other arithmetic, conv_taps(): lax.conv_general_dilated(stacked, kernel, (1, 1), 'VALID', dimension_numb...  3.87 us

profile of v1, /device:TPU:1, one launch (start us, length us, event | category | flops | bytes accessed | tf_op | source)
XLA Modules:
  0.0 94.4 jit_solution(15471899307425497070)
XLA Ops:
  0.6 0.0 copy-start
  0.7 0.9 pad_dynamic-slice_fusion
  1.5 0.1 copy.33
  1.7 0.1 fusion.58
  1.8 0.0 copy-start.7
  1.8 0.0 copy-start.10
  1.8 0.0 copy-start.11
  1.8 8.7 %copy.30 = bf16[48,16,2048]{0,2,1:T(8,128)(2,1)} copy(bf16[48,16,2048]{2,1,0:T(8,128)(2,1)} %param.14) | data formatting | bytes 6291456 | tf_op args[0]
  10.5 0.0 copy-done.10
  10.5 6.6 %fusion.18.f_ref = bf16[8,16,32,64]{3,2,1,0:T(8,128)(2,1)} fusion(bf16[2,2,2,64,48,1,1]{3,4,2,1,0,6,5:T(8,128)(2,1)S(1)} %bitcast.136, bf16[48,8,2,16,2,32,2]{0,6,5,4,3,2,1:T(2,128)(2,1)} %bitcast.115, f32[8,16,32]{2,1,0:T(8,128)S(1)} %fusion.58, f32[64]{0:T(128)S(1)} %copy-done.11), kind=kOutput, calls=%fused_computation.23 | convolution fusion | flops 202375168 | bytes 3735808 | tf_op jit(solution)/shard_map/abkoi,izkybxa->zyxo/dot_general | solution.py:156
  17.1 17.5 %shard_map.149 = bf16[12,20,36,64]{3,2,1,0:T(8,128)(2,1)} custom-call(bf16[8,16,32,64]{3,2,1,0:T(8,128)(2,1)} %fusion.18.f_ref), custom_call_target="tpu_custom_call" | custom-call | tf_op jit(solution)/shard_map/pallas_call | solution.py:109
  34.6 3.9 %fusion.63 = (bf16[10,20,36,64]{3,2,1,0:T(8,128)(2,1)S(1)}, bf16[10,20,36,64]{3,2,1,0:T(8,128)(2,1)S(1)}, bf16[10,20,36,64]{3,2,1,0:T(8,128)(2,1)S(1)}) fusion(bf16[12,20,36,64]{3,2,1,0:T(8,128)(2,1)} %shard_map.149), kind=kLoop, calls=%fused_computation.63 | loop fusion | bytes 5529600 | tf_op jit(solution)/shard_map/slice | solution.py:144
  38.4 0.0 copy-start.5
  38.4 0.0 copy-start.12
  38.5 3.5 %pad_maximum_fusion = bf16[10,20,36,192]{3,2,1,0:T(8,128)(2,1)} fusion(bf16[10,20,36,64]{3,2,1,0:T(8,128)(2,1)S(1)} %get-tuple-element.10, bf16[10,20,36,64]{3,2,1,0:T(8,128)(2,1)S(1)} %get-tuple-element.11, bf16[10,20,36,64]{3,2,1,0:T(8,128)(2,1)S(1)} %get-tuple-element.9), kind=kLoop, calls=%fused_computation.7 | loop fusion | flops 8294400 | bytes 5529600 | tf_op jit(solution)/shard_map/concatenate | solution.py:144
  41.9 0.1 fusion.57
  42.0 0.2 copy.36
  42.3 0.3 copy.34
  42.6 12.4 %multiply_convert_fusion = bf16[10,18,34,64]{3,0,2,1:T(8,128)(2,1)S(1)} fusion(f32[10,18,34]{0,2,1:T(8,128)S(1)} %copy.36, f32[64]{0:T(128)S(1)} %copy-done.12, bf16[3,3,192,64]{3,2,1,0:T(8,128)(2,1)S(1)} %bitcast.131, bf16[10,20,36,192]{3,2,1,0:T(8,128)(2,1)} %pad_maximum_fusion), kind=kOutput, calls=%fused_computation.6 | convolution fusion | flops 1355212800 | bytes 3794080 | tf_op jit(solution)/shard_map/conv_general_dilated | solution.py:147
  54.9 0.0 copy-start.6
  54.9 1.7 %fusion.62 = (bf16[8,18,34,64]{3,0,2,1:T(8,128)(2,1)S(1)}, bf16[8,18,34,64]{3,0,2,1:T(8,128)(2,1)S(1)}, bf16[8,18,34,64]{3,0,2,1:T(8,128)(2,1)}) fusion(bf16[10,18,34,64]{3,0,2,1:T(8,128)(2,1)S(1)} %multiply_convert_fusion), kind=kLoop, calls=%fused_computation.62 | loop fusion | bytes 3760128 | tf_op jit(solution)/shard_map/slice | solution.py:144
  56.7 0.2 copy.37
  56.9 0.0 copy-start.8
  56.9 0.0 copy-start.9
  57.0 6.8 %fusion.6 = f32[8,16,32,64]{3,0,2,1:T(8,128)S(1)} fusion(bf16[3,3,192,64]{3,2,1,0:T(8,128)(2,1)S(1)} %bitcast.130, bf16[8,18,34,64]{3,0,2,1:T(8,128)(2,1)S(1)} %get-tuple-element.7, bf16[8,18,34,64]{3,0,2,1:T(8,128)(2,1)} %get-tuple-element.8, bf16[8,18,34,64]{3,0,2,1:T(8,128)(2,1)S(1)} %get-tuple-element.6), kind=kOutput, calls=%fused_computation.9 | convolution fusion | flops 911609856 | bytes 3149824 | tf_op jit(solution)/shard_map/conv_general_dilated | solution.py:147
  63.8 0.0 copy-start.13
  63.8 0.7 fusion.21
  64.6 0.1 copy.41
  64.8 0.1 fusion.60
  64.9 1.0 %fusion.51.f_ref = bf16[4,8,16,96]{3,2,1,0:T(8,128)(2,1)} fusion(bf16[2,2,2,96,64,1,1]{3,4,2,1,0,6,5:T(8,128)(2,1)S(1)} %bitcast.114, bf16[4,2,8,2,16,2,64]{6,5,4,3,2,1,0:T(2,128)(2,1)S(1)} %bitcast.118, f32[4,8,16]{2,1,0:T(8,128)S(1)} %fusion.60, f32[96]{0:T(128)S(1)} %copy-done.13), kind=kOutput, calls=%fused_computation.43 | convolution fusion | flops 50528256 | bytes 723328 | tf_op jit(solution)/shard_map/abkoi,zkybxai->zyxo/dot_general | solution.py:163
  65.9 8.9 %shard_map.150 = bf16[8,12,20,96]{3,2,1,0:T(8,128)(2,1)} custom-call(bf16[4,8,16,96]{3,2,1,0:T(8,128)(2,1)} %fusion.51.f_ref), custom_call_target="tpu_custom_call" | custom-call | tf_op jit(solution)/shard_map/pallas_call | solution.py:109
  74.8 1.6 %fusion.64 = (bf16[6,12,20,96]{3,2,1,0:T(8,128)(2,1)S(1)}, bf16[6,12,20,96]{3,2,1,0:T(8,128)(2,1)S(1)}, bf16[6,12,20,96]{3,2,1,0:T(8,128)(2,1)S(1)}) fusion(bf16[8,12,20,96]{3,2,1,0:T(8,128)(2,1)} %shard_map.150), kind=kLoop, calls=%fused_computation.64 | loop fusion | bytes 1658880 | tf_op jit(solution)/shard_map/slice | solution.py:144
  76.4 0.7 maximum_bitcast_fusion
  77.1 0.1 copy.59
  77.3 0.2 pad.8.clone
  77.4 1.0 %reshape.98 = bf16[12,6,8,3,288]{4,3,2,1,0:T(4,128)(2,1)S(1)} reshape(bf16[12,6,24,288]{3,2,1,0:T(8,128)(2,1)S(1)} %pad.8.clone) | data formatting | bytes 1990656 | tf_op jit(solution)/shard_map/conv_general_dilated | solution.py:147
  78.4 0.5 slice.74
  79.0 0.0 copy-start.3
  79.0 0.0 copy-start.14
  79.0 0.0 copy-start.17
  79.0 3.3 %fusion.5 = bf16[12,6,8,5,288]{4,3,2,1,0:T(8,128)(2,1)} fusion(bf16[12,6,7,2,288]{4,3,2,1,0:T(2,128)(2,1)S(1)} %slice.74, bf16[12,6,8,3,288]{4,3,2,1,0:T(4,128)(2,1)S(1)} %reshape.98), kind=kLoop, calls=%fused_computation.8 | loop fusion | flops 4976640 | bytes 3234816 | tf_op jit(solution)/shard_map/conv_general_dilated | solution.py:147
  82.3 0.3 copy.44
  82.7 4.3 %fusion.32 = f32[10,48,3,96]{3,1,2,0:T(8,128)S(1)} fusion(bf16[3,3,288,96]{3,2,1,0:T(8,128)(2,1)S(1)} %bitcast.125, bf16[12,6,8,5,288]{4,3,2,1,0:T(8,128)(2,1)} %fusion.5, f32[96]{0:T(128)S(1)} %copy-done.14, pred[48,3]{0,1:T(4,128)(4,1)S(1)} %copy-done.17), kind=kOutput, calls=%fused_computation.31 | convolution fusion | flops 717050880 | bytes 2710032 | tf_op jit(solution)/shard_map/conv_general_dilated | solution.py:147
  86.9 0.4 copy.45
  87.3 0.3 reshape.102
  87.7 0.1 fusion.59
  87.8 0.3 fusion.54
  88.0 0.1 fusion.65
  88.1 0.4 maximum_bitcast_fusion.1
  88.6 0.2 copy.60
  88.8 0.0 copy-start.4
  88.8 0.3 pad.10.clone
  89.1 0.0 copy-start.15
  89.1 0.0 copy-start.16
  89.1 0.1 slice.80
  89.3 0.6 fusion.35
  89.8 0.0 copy-done.4
  89.9 0.3 copy.49
  90.2 1.3 %fusion.45 = f32[8,32,3,96]{3,1,2,0:T(8,128)S(1)} fusion(bf16[3,3,288,96]{3,2,1,0:T(8,128)(2,1)S(1)} %bitcast.126, bf16[10,4,8,5,288]{4,1,3,2,0:T(4,128)(2,1)S(1)} %fusion.35, f32[96]{0:T(128)S(1)} %copy-done.15, pred[32,3]{0,1:T(4,128)(4,1)S(1)} %copy-done.16), kind=kOutput, calls=%fused_computation.38 | convolution fusion | flops 382427136 | bytes 1714656 | tf_op jit(solution)/shard_map/conv_general_dilated | solution.py:147
  91.5 0.2 copy.50
  91.8 0.1 copy.51
  91.8 0.1 fusion.56
  92.0 0.8 copy.54
  92.8 1.6 %copy.53 = bf16[64,8,512]{2,1,0:T(8,128)(2,1)} copy(bf16[64,8,512]{0,2,1:T(8,128)(2,1)S(1)} %bitcast.119) | data formatting | bytes 1048576
  (29 shorter events, 0.2 us)
Async XLA Ops:
  0.6 64.2 %copy-start = (bf16[8,96,64]{1,2,0:T(8,128)(2,1)S(1)}, bf16[8,96,64]{1,2,0:T(8,128)(2,1)}, u32[]{:S(2)}) copy-start(bf16[8,96,64]{1,2,0:T(8,128)(2,1)} %param.22) | copy-start | bytes 294916
  1.8 8.7 %copy-start.7 = (f32[8,16,32]{2,1,0:T(8,128)}, f32[8,16,32]{2,1,0:T(8,128)S(1)}, u32[]{:S(2)}) copy-start(f32[8,16,32]{2,1,0:T(8,128)S(1)} %fusion.58) | copy-start | bytes 49156
  1.8 8.7 %copy-start.10 = (bf16[8,64,48]{1,2,0:T(8,128)(2,1)S(1)}, bf16[8,64,48]{1,2,0:T(8,128)(2,1)}, u32[]{:S(2)}) copy-start(bf16[8,64,48]{1,2,0:T(8,128)(2,1)} %param.16) | copy-start | bytes 147460
  1.8 8.7 %copy-start.11 = (f32[64]{0:T(128)S(1)}, f32[64]{0:T(128)}, u32[]{:S(2)}) copy-start(f32[64]{0:T(128)} %param.17) | copy-start | bytes 772
  38.4 3.9 %copy-start.5 = (bf16[27,64,64]{2,1,0:T(8,128)(2,1)S(1)}, bf16[27,64,64]{2,1,0:T(8,128)(2,1)}, u32[]{:S(2)}) copy-start(bf16[27,64,64]{2,1,0:T(8,128)(2,1)} %param.18) | copy-start | bytes 663556
  38.4 4.1 %copy-start.12 = (f32[64]{0:T(128)S(1)}, f32[64]{0:T(128)}, u32[]{:S(2)}) copy-start(f32[64]{0:T(128)} %param.19) | copy-start | bytes 772
  54.9 1.8 %copy-start.6 = (bf16[27,64,64]{2,1,0:T(8,128)(2,1)S(1)}, bf16[27,64,64]{2,1,0:T(8,128)(2,1)}, u32[]{:S(2)}) copy-start(bf16[27,64,64]{2,1,0:T(8,128)(2,1)} %param.20) | copy-start | bytes 663556
  56.9 6.9 %copy-start.8 = (f32[8,16,32]{2,1,0:T(8,128)S(1)}, f32[8,16,32]{2,1,0:T(8,128)}, u32[]{:S(2)}) copy-start(f32[8,16,32]{2,1,0:T(8,128)} %copy-done.7) | copy-start | bytes 49156
  56.9 6.9 %copy-start.9 = (f32[64]{0:T(128)S(1)}, f32[64]{0:T(128)}, u32[]{:S(2)}) copy-start(f32[64]{0:T(128)} %param.21) | copy-start | bytes 772
  63.8 1.1 %copy-start.13 = (f32[96]{0:T(128)S(1)}, f32[96]{0:T(128)}, u32[]{:S(2)}) copy-start(f32[96]{0:T(128)} %param.23) | copy-start | bytes 1156
  64.6 11.8 %copy-start.1 = (bf16[8,16,32,64]{3,2,1,0:T(8,128)(2,1)}, bf16[8,16,32,64]{3,2,1,0:T(8,128)(2,1)S(1)}, u32[]{:S(2)}) copy-start(bf16[8,16,32,64]{3,2,1,0:T(8,128)(2,1)S(1)} %fusion.21) | copy-start | bytes 1572868
  79.0 3.4 %copy-start.3 = (bf16[27,96,96]{2,1,0:T(8,128)(2,1)S(1)}, bf16[27,96,96]{2,1,0:T(8,128)(2,1)}, u32[]{:S(2)}) copy-start(bf16[27,96,96]{2,1,0:T(8,128)(2,1)} %param.24) | copy-start | bytes 1492996
  79.0 3.7 %copy-start.14 = (f32[96]{0:T(128)S(1)}, f32[96]{0:T(128)}, u32[]{:S(2)}) copy-start(f32[96]{0:T(128)} %param.25) | copy-start | bytes 1156
  79.0 3.7 %copy-start.17 = (pred[48,3]{0,1:T(4,128)(4,1)S(1)}, pred[48,3]{0,1:T(4,128)(4,1)}, u32[]{:S(2)}) copy-start(pred[48,3]{0,1:T(4,128)(4,1)} %constant.39) | copy-start | bytes 436
  88.8 1.1 %copy-start.4 = (bf16[27,96,96]{2,1,0:T(8,128)(2,1)S(1)}, bf16[27,96,96]{2,1,0:T(8,128)(2,1)}, u32[]{:S(2)}) copy-start(bf16[27,96,96]{2,1,0:T(8,128)(2,1)} %param.26) | copy-start | bytes 1492996
  89.1 1.1 %copy-start.15 = (f32[96]{0:T(128)S(1)}, f32[96]{0:T(128)}, u32[]{:S(2)}) copy-start(f32[96]{0:T(128)} %param.27) | copy-start | bytes 1156
  89.1 1.1 %copy-start.16 = (pred[32,3]{0,1:T(4,128)(4,1)S(1)}, pred[32,3]{0,1:T(4,128)(4,1)}, u32[]{:S(2)}) copy-start(pred[32,3]{0,1:T(4,128)(4,1)} %constant.38) | copy-start | bytes 292
  91.5 1.3 %copy-start.2 = (bf16[8,16,32,64]{3,2,1,0:T(8,128)(2,1)S(1)}, bf16[8,16,32,64]{3,2,1,0:T(8,128)(2,1)}, u32[]{:S(2)}) copy-start(bf16[8,16,32,64]{3,2,1,0:T(8,128)(2,1)} %copy-done.1) | copy-start | bytes 1572868

commit v2 on v1

--- a/solution.py
+++ b/solution.py
@@ -141,12 +141,14 @@
 
 def conv_taps(padded, weights):
     size_z = padded.shape[0] - 2
-    stacked = jnp.concatenate([padded[k:k + size_z] for k in range(3)], axis=-1)
-    kernel = weights.reshape(3, 3, 3, weights.shape[1], weights.shape[2]).transpose(1, 0, 2, 4, 3)
-    kernel = kernel.reshape(3, 3, 3 * weights.shape[2], weights.shape[1])
-    return lax.conv_general_dilated(
-        stacked, kernel, (1, 1), "VALID",
-        dimension_numbers=("NHWC", "HWIO", "NHWC"), preferred_element_type=jnp.float32)
+    kernel = weights.reshape(3, 3, 3, weights.shape[1], weights.shape[2]).transpose(2, 1, 0, 4, 3)
+    total = None
+    for k in range(3):
+        term = lax.conv_general_dilated(
+            padded[k:k + size_z], kernel[k], (1, 1), "VALID",
+            dimension_numbers=("NHWC", "HWIO", "NHWC"), preferred_element_type=jnp.float32)
+        total = term if total is None else total + term
+    return total
 
 
 def down_first(grid, weights):

time: 94.9 us -> 108 us (1.14)
  matrix products: 32.3 us -> 43 us
  local copies, waits for them, and re-layouts: 24.6 us -> 28.8 us
  other arithmetic: 9.98 us -> 8.28 us
    conv_general_dilated x4 -> x12, matrix products: 24.7 us -> 35.5 us  [conv_taps(): lax.conv_general_dilated(padded[k:k + size_z], kernel[k], (1, 1), 'VALID'...]
    concatenate x3 -> x0, other arithmetic: 4.62 us -> none  [conv_taps(): stacked = jnp.concatenate([padded[k:k + size_z] for k in range(3)], axis=-1)]
    reshape x2 -> x4, local copies, waits for them, and re-layouts: 0.5 us -> 3.11 us  [conv_taps(): weights.reshape(3, 3, 3, weights.shape[1], weights.shape[2])]
    conv_general_dilated x2 -> x6, other arithmetic: 3.87 us -> 5.8 us  [conv_taps(): lax.conv_general_dilated(padded[k:k + size_z], kernel[k], (1, 1), 'VALID'...]
    unnamed x41 -> x49, local copies, waits for them, and re-layouts: 11.6 us -> 12.7 us
    slice x4 -> x9, local copies, waits for them, and re-layouts: 7.28 us -> 8.29 us  [conv_taps(): padded[k:k + size_z]]
where the time goes in v2:
time: 108 us
  matrix products  43 us (40%)
  local copies, waits for them, and re-layouts  28.8 us (27%)
  Pallas kernels  26.4 us (24%)
  other arithmetic  8.28 us (8%)
  between operations  1.24 us (1%)
    conv_general_dilated x12, matrix products, conv_taps(): lax.conv_general_dilated(padded[k:k + size_z], kernel[k], (1, 1), 'VALID'...  35.5 us
    pallas_call x2, Pallas kernels, with_rim(): pl.pallas_call(functools.partial(rim_kernel, width), out_shape=jax.ShapeD...  26.4 us
    unnamed x49, local copies, waits for them, and re-layouts  12.7 us
    slice x9, local copies, waits for them, and re-layouts, conv_taps(): padded[k:k + size_z]  8.29 us
    dot_general x1, matrix products, down_first(): jnp.einsum('abkoi,izkybxa->zyxo', grouped, split, preferred_element_type=...  6.54 us
    conv_general_dilated x6, other arithmetic, conv_taps(): lax.conv_general_dilated(padded[k:k + size_z], kernel[k], (1, 1), 'VALID'...  5.8 us
    reshape x4, local copies, waits for them, and re-layouts, conv_taps(): weights.reshape(3, 3, 3, weights.shape[1], weights.shape[2])  3.11 us

profile of v2, /device:TPU:1, one launch (start us, length us, event | category | flops | bytes accessed | tf_op | source)
XLA Modules:
  0.0 107.7 jit_solution(6981062161592415661)
XLA Ops:
  0.7 0.9 pad_dynamic-slice_fusion
  1.5 0.1 copy.35
  1.7 0.1 fusion.67
  1.8 8.7 %copy.32 = bf16[48,16,2048]{0,2,1:T(8,128)(2,1)} copy(bf16[48,16,2048]{2,1,0:T(8,128)(2,1)} %param.14) | data formatting | bytes 6291456 | tf_op args[0]
  10.5 6.5 %fusion.13.f_ref = bf16[8,16,32,64]{3,2,1,0:T(8,128)(2,1)} fusion(bf16[2,2,2,64,48,1,1]{3,4,2,1,0,6,5:T(8,128)(2,1)S(1)} %bitcast.186, bf16[48,8,2,16,2,32,2]{0,6,5,4,3,2,1:T(2,128)(2,1)} %bitcast.153, f32[8,16,32]{2,1,0:T(8,128)S(1)} %fusion.67, f32[64]{0:T(128)S(1)} %copy-done.12), kind=kOutput, calls=%fused_computation.16 | convolution fusion | flops 202375168 | bytes 3735808 | tf_op jit(solution)/shard_map/abkoi,izkybxa->zyxo/dot_general | solution.py:158
  17.1 17.5 %shard_map.149 = bf16[12,20,36,64]{3,2,1,0:T(8,128)(2,1)} custom-call(bf16[8,16,32,64]{3,2,1,0:T(8,128)(2,1)} %fusion.13.f_ref), custom_call_target="tpu_custom_call" | custom-call | tf_op jit(solution)/shard_map/pallas_call | solution.py:109
  34.6 6.0 %fusion.70 = (bf16[10,20,36,64]{3,2,1,0:T(8,128)(2,1)S(1)}, bf16[10,20,36,64]{3,2,1,0:T(8,128)(2,1)}, bf16[10,20,36,64]{3,2,1,0:T(8,128)(2,1)}) fusion(bf16[12,20,36,64]{3,2,1,0:T(8,128)(2,1)} %shard_map.149), kind=kLoop, calls=%fused_computation.104 | loop fusion | bytes 5529600 | tf_op jit(solution)/shard_map/slice | solution.py:148
  40.5 0.2 copy.36
  40.8 7.5 %fusion.2 = f32[10,18,34,64]{3,0,2,1:T(8,128)} fusion(bf16[10,20,36,64]{3,2,1,0:T(8,128)(2,1)} %get-tuple-element.7, bf16[3,3,3,64,64]{4,3,2,1,0:T(8,128)(2,1)S(1)} %bitcast.176), kind=kOutput, calls=%fused_computation.3 | convolution fusion | flops 451215360 | bytes 2635776 | tf_op jit(solution)/shard_map/conv_general_dilated | solution.py:147
  48.3 6.6 %fusion.4 = f32[10,18,34,64]{3,0,2,1:T(8,128)} fusion(bf16[10,20,36,64]{3,2,1,0:T(8,128)(2,1)S(1)} %copy-done.1, bf16[3,3,3,64,64]{4,3,2,1,0:T(8,128)(2,1)S(1)} %bitcast.177), kind=kOutput, calls=%fused_computation.5 | convolution fusion | flops 451215360 | bytes 3762176 | tf_op jit(solution)/shard_map/conv_general_dilated | solution.py:147
  54.8 0.1 fusion.66
  54.9 1.0 copy.40
  55.9 8.0 %multiply_convert_fusion = bf16[10,18,34,64]{3,0,2,1:T(8,128)(2,1)} fusion(f32[10,18,34,64]{3,0,2,1:T(8,128)} %fusion.2, f32[10,18,34,64]{3,0,2,1:T(8,128)} %fusion.4, f32[10,18,34]{0,2,1:T(8,128)} %copy.40, f32[64]{0:T(128)S(1)} %copy-done.13, bf16[10,20,36,64]{3,2,1,0:T(8,128)(2,1)S(1)} %get-tuple-element.6, bf16[3,3,3,64,64]{4,3,2,1,0:T(8,128)(2,1)S(1)} %bitcast.178), kind=kOutput, calls=%fused_computation.2 | convolution fusion | flops 453565440 | bytes 6137248 | tf_op jit(solution)/shard_map/conv_general_dilated | solution.py:147
  63.9 0.2 copy.41
  64.2 3.6 %fusion.26 = f32[8,16,32,64]{3,0,2,1:T(8,128)S(1)} fusion(bf16[10,18,34,64]{3,0,2,1:T(8,128)(2,1)} %multiply_convert_fusion, bf16[3,3,3,64,64]{4,3,2,1,0:T(8,128)(2,1)S(1)} %bitcast.179), kind=kOutput, calls=%fused_computation.30 | convolution fusion | flops 301989888 | bytes 2449408 | tf_op jit(solution)/shard_map/conv_general_dilated | solution.py:147
  67.8 1.7 %fusion.28 = f32[8,16,32,64]{3,0,2,1:T(8,128)S(1)} fusion(bf16[10,18,34,64]{3,0,2,1:T(8,128)(2,1)S(1)} %copy-done.19, bf16[3,3,3,64,64]{4,3,2,1,0:T(8,128)(2,1)S(1)} %bitcast.180), kind=kOutput, calls=%fused_computation.32 | convolution fusion | flops 301989888 | bytes 2449408 | tf_op jit(solution)/shard_map/conv_general_dilated | solution.py:147
  69.5 1.6 %fusion.30 = f32[8,16,32,64]{3,0,2,1:T(8,128)S(1)} fusion(bf16[10,18,34,64]{3,0,2,1:T(8,128)(2,1)S(1)} %copy-done.19, bf16[3,3,3,64,64]{4,3,2,1,0:T(8,128)(2,1)S(1)} %bitcast.181), kind=kOutput, calls=%fused_computation.34 | convolution fusion | flops 301989888 | bytes 2449408 | tf_op jit(solution)/shard_map/conv_general_dilated | solution.py:147
  71.2 1.7 %fusion.17 = bf16[8,16,32,64]{3,2,1,0:T(8,128)(2,1)S(1)} fusion(f32[8,16,32,64]{3,0,2,1:T(8,128)S(1)} %fusion.26, f32[8,16,32,64]{3,0,2,1:T(8,128)S(1)} %fusion.28, f32[8,16,32,64]{3,0,2,1:T(8,128)S(1)} %fusion.30, f32[64]{0:T(128)S(1)} %copy-done.10, f32[8,16,32]{2,1,0:T(8,128)S(1)} %fusion.67), kind=kLoop, calls=%fused_computation.21 | loop fusion | flops 1572864 | bytes 3686656 | tf_op jit(solution)/shard_map/convert_element_type | solution.py:139
  73.0 0.1 copy.47
  73.2 0.6 copy-done.8
  73.8 0.1 fusion.69
  73.9 1.0 fusion.42.f_ref
  74.9 8.9 %shard_map.150 = bf16[8,12,20,96]{3,2,1,0:T(8,128)(2,1)} custom-call(bf16[4,8,16,96]{3,2,1,0:T(8,128)(2,1)} %fusion.42.f_ref), custom_call_target="tpu_custom_call" | custom-call | tf_op jit(solution)/shard_map/pallas_call | solution.py:109
  83.8 1.6 %slice_bitcast_fusion.1 = (bf16[12,6,20,96]{3,2,0,1:T(8,128)(2,1)S(1)}, bf16[12,6,20,96]{3,2,0,1:T(8,128)(2,1)S(1)}, bf16[12,6,20,96]{3,2,0,1:T(8,128)(2,1)S(1)}) fusion(bf16[8,12,20,96]{3,2,1,0:T(8,128)(2,1)} %shard_map.150), kind=kLoop, calls=%fused_computation.65 | loop fusion | bytes 1658880 | tf_op jit(solution)/shard_map/slice | solution.py:148
  85.5 0.1 pad.12.clone
  85.6 0.3 reshape.92
  85.9 0.2 slice.136
  86.1 1.8 %fusion.38 = bf16[12,6,8,5,96]{4,3,2,1,0:T(8,128)(2,1)} fusion(bf16[12,6,7,2,96]{4,3,2,1,0:T(2,128)(2,1)S(1)} %slice.136, bf16[12,6,8,3,96]{4,3,2,1,0:T(4,128)(2,1)S(1)} %reshape.92), kind=kLoop, calls=%fused_computation.45 | loop fusion | flops 1658880 | bytes 1078272 | tf_op jit(solution)/shard_map/conv_general_dilated | solution.py:147
  87.9 0.1 pad.10.clone
  88.0 0.3 reshape.87
  88.3 0.2 slice.134
  88.5 1.8 %fusion.37 = bf16[12,6,8,5,96]{4,3,2,1,0:T(8,128)(2,1)} fusion(bf16[12,6,7,2,96]{4,3,2,1,0:T(2,128)(2,1)S(1)} %slice.134, bf16[12,6,8,3,96]{4,3,2,1,0:T(4,128)(2,1)S(1)} %reshape.87), kind=kLoop, calls=%fused_computation.44 | loop fusion | flops 1658880 | bytes 1078272 | tf_op jit(solution)/shard_map/conv_general_dilated | solution.py:147
  90.3 0.1 pad.8.clone
  90.4 0.3 reshape.82
  90.7 0.2 slice.132
  90.9 0.8 fusion.36
  91.7 2.3 %copy.50 = bf16[3,3,3,96,96]{3,4,0,1,2:T(8,128)(2,1)} copy(bf16[3,3,3,96,96]{4,3,2,1,0:T(8,128)(2,1)} %bitcast.165) | data formatting | bytes 995328 | tf_op jit(solution)/shard_map/reshape | solution.py:144
  94.0 1.9 %convolution_select_fusion.2 = f32[10,48,3,96]{3,1,2,0:T(8,128)S(1)} fusion(bf16[12,6,8,5,96]{4,3,2,1,0:T(8,128)(2,1)S(1)} %fusion.36, pred[48,3]{0,1:T(4,128)(4,1)} %constant.55, bf16[3,3,3,96,96]{4,3,2,1,0:T(8,128)(2,1)} %bitcast.170), kind=kOutput, calls=%fused_computation.29 | convolution fusion | flops 239016960 | bytes 1327616 | tf_op jit(solution)/shard_map/conv_general_dilated | solution.py:147
  96.0 0.9 fusion.25
  96.9 0.3 copy-done.2
  97.2 0.9 fusion.24
  98.1 0.4 copy.55
  98.5 0.3 reshape.96
  98.9 0.1 copy-done.9
  99.0 0.1 fusion.68
  99.1 0.3 fusion.48
  99.4 0.1 slice_bitcast_fusion.7
  99.5 0.1 copy.76
  99.6 0.1 pad.14.clone
  99.8 0.2 fusion.55
  100.0 0.1 copy.77
  100.1 0.1 pad.16.clone
  100.3 1.0 fusion.56
  101.2 0.3 copy.59
  101.6 1.6 %convolution_select_fusion.4 = f32[8,32,3,96]{3,1,2,0:T(8,128)S(1)} fusion(bf16[10,4,8,5,96]{4,1,3,2,0:T(4,128)(2,1)} %fusion.56, bf16[3,3,3,96,96]{4,3,2,1,0:T(8,128)(2,1)S(1)} %bitcast.167, pred[32,3]{0,1:T(4,128)(4,1)S(1)} %copy-done.17), kind=kOutput, calls=%fused_computation.37 | convolution fusion | flops 127475712 | bytes 823808 | tf_op jit(solution)/shard_map/conv_general_dilated | solution.py:147
  103.2 0.1 pad.18.clone
  103.4 0.2 fusion.57
  103.6 0.6 convolution_select_fusion.3
  104.2 0.6 fusion.35
  104.8 0.2 copy.64
  105.1 0.1 copy.65
  105.1 0.1 fusion.65
  105.3 0.8 copy.68
  106.1 1.6 %copy.67 = bf16[64,8,512]{2,1,0:T(8,128)(2,1)} copy(bf16[64,8,512]{0,2,1:T(8,128)(2,1)S(1)} %bitcast.155) | data formatting | bytes 1048576
  (55 shorter events, 0.6 us)
Async XLA Ops:
  0.6 73.3 %copy-start = (bf16[8,96,64]{1,2,0:T(8,128)(2,1)S(1)}, bf16[8,96,64]{1,2,0:T(8,128)(2,1)}, u32[]{:S(2)}) copy-start(bf16[8,96,64]{1,2,0:T(8,128)(2,1)} %param.22) | copy-start | bytes 294916
  1.8 8.8 %copy-start.11 = (bf16[8,64,48]{1,2,0:T(8,128)(2,1)S(1)}, bf16[8,64,48]{1,2,0:T(8,128)(2,1)}, u32[]{:S(2)}) copy-start(bf16[8,64,48]{1,2,0:T(8,128)(2,1)} %param.16) | copy-start | bytes 147460
  1.8 8.8 %copy-start.12 = (f32[64]{0:T(128)S(1)}, f32[64]{0:T(128)}, u32[]{:S(2)}) copy-start(f32[64]{0:T(128)} %param.17) | copy-start | bytes 772
  34.6 6.0 %copy-start.6 = (bf16[27,64,64]{2,1,0:T(8,128)(2,1)S(1)}, bf16[27,64,64]{2,1,0:T(8,128)(2,1)}, u32[]{:S(2)}) copy-start(bf16[27,64,64]{2,1,0:T(8,128)(2,1)} %param.18) | copy-start | bytes 663556
  40.8 7.5 %copy-start.1 = (bf16[10,20,36,64]{3,2,1,0:T(8,128)(2,1)S(1)}, bf16[10,20,36,64]{3,2,1,0:T(8,128)(2,1)}, u32[]{:S(2)}) copy-start(bf16[10,20,36,64]{3,2,1,0:T(8,128)(2,1)} %get-tuple-element.8) | copy-start | bytes 2764804
  48.2 7.6 %copy-start.13 = (f32[64]{0:T(128)S(1)}, f32[64]{0:T(128)}, u32[]{:S(2)}) copy-start(f32[64]{0:T(128)} %param.19) | copy-start | bytes 772
  55.9 8.0 %copy-start.7 = (bf16[27,64,64]{2,1,0:T(8,128)(2,1)S(1)}, bf16[27,64,64]{2,1,0:T(8,128)(2,1)}, u32[]{:S(2)}) copy-start(bf16[27,64,64]{2,1,0:T(8,128)(2,1)} %param.20) | copy-start | bytes 663556
  64.2 3.6 %copy-start.19 = (bf16[10,18,34,64]{3,0,2,1:T(8,128)(2,1)S(1)}, bf16[10,18,34,64]{3,0,2,1:T(8,128)(2,1)}, u32[]{:S(2)}) copy-start(bf16[10,18,34,64]{3,0,2,1:T(8,128)(2,1)} %multiply_convert_fusion) | copy-start | bytes 2350084
  69.5 1.7 %copy-start.10 = (f32[64]{0:T(128)S(1)}, f32[64]{0:T(128)}, u32[]{:S(2)}) copy-start(f32[64]{0:T(128)} %param.21) | copy-start | bytes 772
  71.2 2.7 %copy-start.14 = (f32[96]{0:T(128)S(1)}, f32[96]{0:T(128)}, u32[]{:S(2)}) copy-start(f32[96]{0:T(128)} %param.23) | copy-start | bytes 1156
  73.2 0.6 copy-start.8
  91.7 4.2 %copy-start.3 = (bf16[12,6,8,5,96]{4,3,2,1,0:T(8,128)(2,1)S(1)}, bf16[12,6,8,5,96]{4,3,2,1,0:T(8,128)(2,1)}, u32[]{:S(2)}) copy-start(bf16[12,6,8,5,96]{4,3,2,1,0:T(8,128)(2,1)} %fusion.37) | copy-start | bytes 1658884
  94.0 1.9 %copy-start.5 = (bf16[3,3,3,96,96]{3,4,0,1,2:T(8,128)(2,1)S(1)}, bf16[3,3,3,96,96]{3,4,0,1,2:T(8,128)(2,1)}, u32[]{:S(2)}) copy-start(bf16[3,3,3,96,96]{3,4,0,1,2:T(8,128)(2,1)} %copy.50) | copy-start | bytes 1492996
  94.0 1.9 %copy-start.18 = (pred[48,3]{0,1:T(4,128)(4,1)S(1)}, pred[48,3]{0,1:T(4,128)(4,1)}, u32[]{:S(2)}) copy-start(pred[48,3]{0,1:T(4,128)(4,1)} %constant.55) | copy-start | bytes 436
  95.9 1.3 %copy-start.2 = (bf16[12,6,8,5,96]{4,3,2,1,0:T(8,128)(2,1)S(1)}, bf16[12,6,8,5,96]{4,3,2,1,0:T(8,128)(2,1)}, u32[]{:S(2)}) copy-start(bf16[12,6,8,5,96]{4,3,2,1,0:T(8,128)(2,1)} %fusion.38) | copy-start | bytes 1658884
  95.9 1.3 %copy-start.15 = (f32[96]{0:T(128)S(1)}, f32[96]{0:T(128)}, u32[]{:S(2)}) copy-start(f32[96]{0:T(128)} %param.25) | copy-start | bytes 1156
  98.1 0.9 copy-start.9
  99.5 1.7 %copy-start.4 = (bf16[27,96,96]{2,1,0:T(8,128)(2,1)S(1)}, bf16[27,96,96]{2,1,0:T(8,128)(2,1)}, u32[]{:S(2)}) copy-start(bf16[27,96,96]{2,1,0:T(8,128)(2,1)} %param.26) | copy-start | bytes 1492996
  99.8 1.8 %copy-start.17 = (pred[32,3]{0,1:T(4,128)(4,1)S(1)}, pred[32,3]{0,1:T(4,128)(4,1)}, u32[]{:S(2)}) copy-start(pred[32,3]{0,1:T(4,128)(4,1)} %constant.54) | copy-start | bytes 292
  103.2 1.1 %copy-start.16 = (f32[96]{0:T(128)S(1)}, f32[96]{0:T(128)}, u32[]{:S(2)}) copy-start(f32[96]{0:T(128)} %param.27) | copy-start | bytes 1156

commit v3 on v0

--- a/solution.py
+++ b/solution.py
@@ -20,9 +20,8 @@
 ]
 
 
-def rim_kernel(width, f_ref, p_ref, local_sem, send_sem, recv_sem):
-    size_z, size_y, size_x, _ = f_ref.shape
-    sizes = (size_x, size_y, size_z)
+def rim_kernel(width, owners, f_ref, p_ref, local_sem, send_sem, recv_sem):
+    sizes = f_ref.shape[:3]
     index = [lax.axis_index(a) for a in AXES]
     count = [lax.axis_size(a) for a in AXES]
 
@@ -38,38 +37,39 @@
     def device(d):
         return tuple(index[a] + d[a] for a in range(3))
 
-    def source(a, step):
-        s = sizes[a]
+    def source(k, step):
+        s = sizes[k]
         if step == -1:
             return slice(0, width)
         if step == 1:
             return slice(s - width, s)
         return slice(0, s)
 
-    def side(a, step):
-        s = sizes[a]
+    def side(k, step):
+        s = sizes[k]
         if step == -1:
             return slice(0, width)
         if step == 1:
             return slice(s + width, s + 2 * width)
         return slice(width, width + s)
 
+    def window(pick, d, sign):
+        return tuple(pick(k, sign * d[owners[k]]) for k in range(3)) + (slice(None),)
+
     barrier = pltpu.get_barrier_semaphore()
     for d in DIRS:
         @pl.when(exists(d))
         def _():
             pl.semaphore_signal(barrier, inc=1, device_id=device(d), device_id_type=MESH)
 
-    local = pltpu.make_async_copy(
-        f_ref, p_ref.at[width:width + size_z, width:width + size_y, width:width + size_x, :],
-        local_sem.at[0])
+    interior = tuple(slice(width, width + sizes[k]) for k in range(3)) + (slice(None),)
+    local = pltpu.make_async_copy(f_ref, p_ref.at[interior], local_sem.at[0])
     local.start()
 
     for d in DIRS:
         @pl.when(jnp.logical_not(exists(d)))
         def _():
-            sx, sy, sz = (side(a, d[a]) for a in range(3))
-            region = p_ref.at[sz, sy, sx, :]
+            region = p_ref.at[window(side, d, 1)]
             region[...] = jnp.zeros(region.shape, region.dtype)
 
     peers = 1
@@ -81,11 +81,9 @@
 
     copies = []
     for k, d in enumerate(DIRS):
-        sx, sy, sz = (source(a, d[a]) for a in range(3))
-        tx, ty, tz = (side(a, -d[a]) for a in range(3))
         copy = pltpu.make_async_remote_copy(
-            src_ref=f_ref.at[sz, sy, sx, :],
-            dst_ref=p_ref.at[tz, ty, tx, :],
+            src_ref=f_ref.at[window(source, d, 1)],
+            dst_ref=p_ref.at[window(side, d, -1)],
             send_sem=send_sem.at[k],
             recv_sem=recv_sem.at[k],
             device_id=device(d),
@@ -108,12 +106,12 @@
             copy.wait_recv()
 
 
-def with_rim(field, width, collective_id):
-    size_z, size_y, size_x, chans = field.shape
+def with_rim(field, width, owners, collective_id):
+    sizes = field.shape[:3]
     return pl.pallas_call(
-        functools.partial(rim_kernel, width),
+        functools.partial(rim_kernel, width, owners),
         out_shape=jax.ShapeDtypeStruct(
-            (size_z + 2 * width, size_y + 2 * width, size_x + 2 * width, chans), field.dtype),
+            tuple(s + 2 * width for s in sizes) + (field.shape[3],), field.dtype),
         in_specs=[pl.BlockSpec(memory_space=pltpu.VMEM)],
         out_specs=pl.BlockSpec(memory_space=pltpu.VMEM),
         scratch_shapes=[
@@ -123,6 +121,11 @@
         ],
         compiler_params=pltpu.CompilerParams(collective_id=collective_id, has_side_effects=True),
     )(field)
+
+
+def rim_yxz(field, width, collective_id):
+    rimmed = with_rim(field.transpose(1, 2, 0, 3), width, (1, 0, 2), collective_id)
+    return rimmed.transpose(2, 0, 1, 3)
 
 
 def region_mask(tissue, repeats, block_starts, extents, margin):
@@ -186,7 +189,7 @@
     mask_one = region_mask(tissue, (4, 4, 8), first_blocks, (first_x, first_y, first_z), 0)
     mask_one_wide = region_mask(tissue, (4, 4, 8), first_blocks, (first_x, first_y, first_z), 1)
     down_one = finish(down_first(grid_zero, w_down1), b_down1, mask_one)
-    inner_one = finish(conv_taps(with_rim(down_one, 2, 0), w_conv1a), b_conv1a, mask_one_wide)
+    inner_one = finish(conv_taps(rim_yxz(down_one, 2, 0), w_conv1a), b_conv1a, mask_one_wide)
     feat_one = finish(conv_taps(inner_one, w_conv1b), b_conv1b, mask_one)
     second_x = first_x // 2
     second_y = first_y // 2
@@ -195,7 +198,7 @@
     mask_two = region_mask(tissue, (2, 2, 4), second_blocks, (second_x, second_y, second_z), 0)
     mask_two_wide = region_mask(tissue, (2, 2, 4), second_blocks, (second_x, second_y, second_z), 1)
     down_two = finish(down_cells(feat_one, w_down2), b_down2, mask_two)
-    middle = finish(conv_taps(with_rim(down_two, 2, 1), w_conv2a), b_conv2a, mask_two_wide)
+    middle = finish(conv_taps(with_rim(down_two, 2, (2, 1, 0), 1), w_conv2a), b_conv2a, mask_two_wide)
     feat_two = finish(conv_taps(middle, w_conv2b), b_conv2b, mask_two)
     return (packed(feat_one), packed(feat_two))
 

time: 94.9 us -> 103 us (1.085)
  local copies, waits for them, and re-layouts: 24.6 us -> 32.4 us
  matrix products: 32.3 us -> 33.6 us
    slice x4, local copies, waits for them, and re-layouts: 7.28 us -> 11.9 us  [conv_taps(): stacked = jnp.concatenate([padded[k:k + size_z] for k in range(3)], axis=-1)]
    concatenate x3 -> x2, other arithmetic: 4.62 us -> 1.14 us  [conv_taps(): stacked = jnp.concatenate([padded[k:k + size_z] for k in range(3)], axis=-1)]
    convert_element_type x3, other arithmetic: 1.14 us -> 3.13 us  [finish(): (jnp.maximum(summed + offsets, 0.0) * tissue_mask).astype(jnp.bfloat16)]
    transpose x3 -> x4, local copies, waits for them, and re-layouts: 0.33 us -> 1.9 us  [region_mask(): return table.astype(jnp.float32).transpose(2, 1, 0)[..., None]]
    dot_general x1, matrix products: 6.56 us -> 5.1 us  [down_first(): jnp.einsum('abkoi,izkybxa->zyxo', grouped, split, preferred_element_type=...]
    dot_general x1, matrix products: 1.01 us -> 2.43 us  [down_cells(): jnp.einsum('abkoi,zkybxai->zyxo', grouped, split, preferred_element_type=...]
    conv_general_dilated x4, matrix products: 24.7 us -> 26.1 us  [conv_taps(): lax.conv_general_dilated(stacked, kernel, (1, 1), 'VALID', dimension_numb...]
    unnamed x41 -> x35, local copies, waits for them, and re-layouts: 11.6 us -> 12 us
where the time goes in v3:
time: 103 us
  matrix products  33.6 us (33%)
  local copies, waits for them, and re-layouts  32.4 us (31%)
  Pallas kernels  26.5 us (26%)
  other arithmetic  9.12 us (9%)
  between operations  1.06 us (1%)
    pallas_call x2, Pallas kernels, with_rim(): pl.pallas_call(functools.partial(rim_kernel, width, owners), out_shape=ja...  26.5 us
    conv_general_dilated x4, matrix products, conv_taps(): lax.conv_general_dilated(stacked, kernel, (1, 1), 'VALID', dimension_numb...  26.1 us
    unnamed x35, local copies, waits for them, and re-layouts  12 us
    slice x4, local copies, waits for them, and re-layouts, conv_taps(): stacked = jnp.concatenate([padded[k:k + size_z] for k in range(3)], axis=-1)  11.9 us
    dot_general x1, matrix products, down_first(): jnp.einsum('abkoi,izkybxa->zyxo', grouped, split, preferred_element_type=...  5.1 us
    conv_general_dilated x2, other arithmetic, conv_taps(): lax.conv_general_dilated(stacked, kernel, (1, 1), 'VALID', dimension_numb...  3.87 us
    convert_element_type x3, other arithmetic, finish(): (jnp.maximum(summed + offsets, 0.0) * tissue_mask).astype(jnp.bfloat16)  3.13 us
    dot_general x1, matrix products, down_cells(): jnp.einsum('abkoi,zkybxai->zyxo', grouped, split, preferred_element_type=...  2.43 us

profile of v3, /device:TPU:1, one launch (start us, length us, event | category | flops | bytes accessed | tf_op | source)
XLA Modules:
  0.0 102.7 jit_solution(10495735596169409256)
XLA Ops:
  0.6 0.0 copy-start
  0.7 0.9 pad_dynamic-slice_fusion
  1.5 0.1 copy.57
  1.7 0.7 fusion.61
  2.4 0.1 copy.58
  2.5 0.0 copy-start.7
  2.5 8.7 %copy.53 = bf16[48,16,2048]{0,2,1:T(8,128)(2,1)} copy(bf16[48,16,2048]{2,1,0:T(8,128)(2,1)} %param.14) | data formatting | bytes 6291456 | tf_op args[0]
  11.3 0.0 copy-done.7
  11.3 5.1 %fusion.24 = f32[8,16,32,64]{3,2,1,0:T(8,128)S(1)} fusion(bf16[2,2,2,64,48,1,1]{3,4,2,1,0,6,5:T(8,128)(2,1)S(1)} %bitcast.137, bf16[48,8,2,16,2,32,2]{0,6,5,4,3,2,1:T(2,128)(2,1)} %bitcast.118), kind=kOutput, calls=%fused_computation.28 | convolution fusion | flops 201326592 | bytes 4243456 | tf_op jit(solution)/shard_map/abkoi,izkybxa->zyxo/dot_general | solution.py:164
  16.4 0.0 copy-done.6
  16.4 2.7 %fusion.20.f_ref = bf16[16,32,8,64]{3,2,1,0:T(8,128)(2,1)} fusion(f32[8,16,32,64]{3,2,1,0:T(8,128)S(1)} %fusion.24, f32[16,32,8]{2,1,0:T(8,128)S(1)} %copy.58, f32[64]{0:T(128)S(1)} %copy-done.6), kind=kLoop, calls=%fused_computation.24 | loop fusion | flops 1048576 | bytes 1589504 | tf_op jit(solution)/shard_map/convert_element_type | solution.py:147
  19.1 17.6 %shard_map.149 = bf16[20,36,12,64]{3,2,1,0:T(8,128)(2,1)} custom-call(bf16[16,32,8,64]{3,2,1,0:T(8,128)(2,1)} %fusion.20.f_ref), custom_call_target="tpu_custom_call" | custom-call | tf_op jit(solution)/shard_map/pallas_call | solution.py:111
  36.7 0.0 copy-start.8
  36.7 8.5 %fusion.67 = (bf16[10,20,36,64]{3,0,2,1:T(8,128)(2,1)S(1)}, bf16[10,20,36,64]{3,0,2,1:T(8,128)(2,1)}, bf16[10,20,36,64]{3,0,2,1:T(8,128)(2,1)}) fusion(bf16[12,20,36,64]{3,0,2,1:T(8,128)(2,1)} %bitcast.117), kind=kLoop, calls=%fused_computation.66 | loop fusion | bytes 5529600 | tf_op jit(solution)/shard_map/slice | solution.py:152
  45.2 0.1 fusion.60
  45.3 1.0 copy.60
  46.3 1.3 %copy.59 = bf16[3,3,3,64,64]{3,4,2,0,1:T(8,128)(2,1)S(1)} copy(bf16[3,3,3,64,64]{4,3,2,1,0:T(8,128)(2,1)} %bitcast.129) | data formatting | bytes 442368 | tf_op jit(solution)/shard_map/reshape | solution.py:153
  47.6 13.4 %multiply_convert_fusion = bf16[10,18,34,64]{3,0,2,1:T(8,128)(2,1)S(1)} fusion(f32[10,18,34]{0,2,1:T(8,128)} %copy.60, f32[64]{0:T(128)S(1)} %copy-done.8, bf16[3,3,192,64]{3,2,1,0:T(8,128)(2,1)S(1)} %bitcast.131, bf16[10,20,36,64]{3,0,2,1:T(8,128)(2,1)} %get-tuple-element.9, bf16[10,20,36,64]{3,0,2,1:T(8,128)(2,1)} %get-tuple-element.10, ...), kind=kOutput, calls=%fused_computation.10 | convolution fusion | flops 1363507200 | bytes 3794080 | tf_op jit(solution)/shard_map/conv_general_dilated | solution.py:155
  61.0 0.0 copy-start.5
  61.0 0.0 copy-start.4
  61.0 0.0 copy-start.9
  61.1 1.7 %fusion.68 = (bf16[8,18,34,64]{3,0,2,1:T(8,128)(2,1)S(1)}, bf16[8,18,34,64]{3,0,2,1:T(8,128)(2,1)S(1)}, bf16[8,18,34,64]{3,0,2,1:T(8,128)(2,1)}) fusion(bf16[10,18,34,64]{3,0,2,1:T(8,128)(2,1)S(1)} %multiply_convert_fusion), kind=kLoop, calls=%fused_computation.67 | loop fusion | bytes 3760128 | tf_op jit(solution)/shard_map/slice | solution.py:152
  62.8 0.8 copy.62
  63.6 0.2 copy.61
  63.9 0.0 copy-start.10
  63.9 7.1 %multiply_convert_fusion.1 = bf16[8,16,32,64]{3,0,2,1:T(8,128)(2,1)} fusion(bf16[3,3,192,64]{3,2,1,0:T(8,128)(2,1)S(1)} %bitcast.132, bf16[8,18,34,64]{3,0,2,1:T(8,128)(2,1)S(1)} %get-tuple-element.12, bf16[8,18,34,64]{3,0,2,1:T(8,128)(2,1)} %get-tuple-element.13, bf16[8,18,34,64]{3,0,2,1:T(8,128)(2,1)S(1)} %get-tuple-element.11, f32[8,16,32]{0,2,1:T(8,128)} %copy.62, ...), kind=kOutput, calls=%fused_computation.27 | convolution fusion | flops 912658432 | bytes 2642176 | tf_op jit(solution)/shard_map/conv_general_dilated | solution.py:155
  71.1 0.1 copy.65
  71.2 0.1 fusion.64
  71.3 2.4 %fusion.54.f_ref = bf16[4,8,16,96]{3,2,1,0:T(8,128)(2,1)} fusion(bf16[2,2,2,96,64,1,1]{3,4,2,1,0,6,5:T(8,128)(2,1)S(1)} %bitcast.116, bf16[4,2,8,2,16,2,64]{6,1,0,5,4,3,2:T(2,128)(2,1)} %bitcast.122, f32[4,8,16]{2,1,0:T(8,128)S(1)} %fusion.64, f32[96]{0:T(128)S(1)} %copy-done.10), kind=kOutput, calls=%fused_computation.44 | convolution fusion | flops 50528256 | bytes 723328 | tf_op jit(solution)/shard_map/abkoi,zkybxai->zyxo/dot_general | solution.py:171
  73.7 8.9 %shard_map.150 = bf16[8,12,20,96]{3,2,1,0:T(8,128)(2,1)} custom-call(bf16[4,8,16,96]{3,2,1,0:T(8,128)(2,1)} %fusion.54.f_ref), custom_call_target="tpu_custom_call" | custom-call | tf_op jit(solution)/shard_map/pallas_call | solution.py:111
  82.7 1.6 %fusion.69 = (bf16[6,12,20,96]{3,2,1,0:T(8,128)(2,1)S(1)}, bf16[6,12,20,96]{3,2,1,0:T(8,128)(2,1)S(1)}, bf16[6,12,20,96]{3,2,1,0:T(8,128)(2,1)S(1)}) fusion(bf16[8,12,20,96]{3,2,1,0:T(8,128)(2,1)} %shard_map.150), kind=kLoop, calls=%fused_computation.68 | loop fusion | bytes 1658880 | tf_op jit(solution)/shard_map/slice | solution.py:152
  84.3 0.7 maximum_bitcast_fusion
  85.0 0.1 copy.83
  85.2 0.2 pad.8.clone
  85.3 1.0 reshape.98
  86.3 0.5 slice.77
  86.9 0.0 copy-start.2
  86.9 0.0 copy-start.11
  86.9 0.0 copy-start.14
  86.9 3.3 %fusion.9 = bf16[12,6,8,5,288]{4,3,2,1,0:T(8,128)(2,1)} fusion(bf16[12,6,7,2,288]{4,3,2,1,0:T(2,128)(2,1)S(1)} %slice.77, bf16[12,6,8,3,288]{4,3,2,1,0:T(4,128)(2,1)S(1)} %reshape.98), kind=kLoop, calls=%fused_computation.11 | loop fusion | flops 4976640 | bytes 3234816 | tf_op jit(solution)/shard_map/conv_general_dilated | solution.py:155
  90.2 0.3 copy.68
  90.6 0.0 copy-done.11
  90.6 4.3 %fusion.35 = f32[10,48,3,96]{3,1,2,0:T(8,128)S(1)} fusion(bf16[3,3,288,96]{3,2,1,0:T(8,128)(2,1)S(1)} %bitcast.126, bf16[12,6,8,5,288]{4,3,2,1,0:T(8,128)(2,1)} %fusion.9, f32[96]{0:T(128)S(1)} %copy-done.11, pred[48,3]{0,1:T(4,128)(4,1)S(1)} %copy-done.14), kind=kOutput, calls=%fused_computation.32 | convolution fusion | flops 717050880 | bytes 2710032 | tf_op jit(solution)/shard_map/conv_general_dilated | solution.py:155
  94.8 0.4 copy.69
  95.2 0.3 reshape.102
  95.6 0.1 fusion.63
  95.7 0.3 fusion.57
  96.0 0.1 fusion.70
  96.1 0.4 maximum_bitcast_fusion.1
  96.5 0.2 copy.84
  96.7 0.0 copy-start.3
  96.7 0.3 pad.10.clone
  97.0 0.0 copy-start.12
  97.0 0.0 copy-start.13
  97.0 0.1 slice.83
  97.2 0.6 fusion.38
  97.7 0.0 copy-done.3
  97.8 0.3 copy.73
  98.1 1.3 %fusion.48 = f32[8,32,3,96]{3,1,2,0:T(8,128)S(1)} fusion(bf16[3,3,288,96]{3,2,1,0:T(8,128)(2,1)S(1)} %bitcast.127, bf16[10,4,8,5,288]{4,1,3,2,0:T(4,128)(2,1)S(1)} %fusion.38, f32[96]{0:T(128)S(1)} %copy-done.12, pred[32,3]{0,1:T(4,128)(4,1)S(1)} %copy-done.13), kind=kOutput, calls=%fused_computation.39 | convolution fusion | flops 382427136 | bytes 1714656 | tf_op jit(solution)/shard_map/conv_general_dilated | solution.py:155
  99.4 0.2 copy.74
  99.7 0.1 copy.75
  99.7 0.1 fusion.59
  99.9 0.8 copy.78
  100.7 2.1 %copy.77 = bf16[64,8,512]{2,1,0:T(8,128)(2,1)} copy(bf16[64,8,512]{0,1,2:T(8,128)(2,1)S(1)} %bitcast.123) | data formatting | bytes 1048576
  (24 shorter events, 0.2 us)
Async XLA Ops:
  0.6 70.7 %copy-start = (bf16[8,96,64]{1,2,0:T(8,128)(2,1)S(1)}, bf16[8,96,64]{1,2,0:T(8,128)(2,1)}, u32[]{:S(2)}) copy-start(bf16[8,96,64]{1,2,0:T(8,128)(2,1)} %param.22) | copy-start | bytes 294916
  2.5 8.7 %copy-start.7 = (bf16[8,64,48]{1,2,0:T(8,128)(2,1)S(1)}, bf16[8,64,48]{1,2,0:T(8,128)(2,1)}, u32[]{:S(2)}) copy-start(bf16[8,64,48]{1,2,0:T(8,128)(2,1)} %param.16) | copy-start | bytes 147460
  11.3 5.1 %copy-start.6 = (f32[64]{0:T(128)S(1)}, f32[64]{0:T(128)}, u32[]{:S(2)}) copy-start(f32[64]{0:T(128)} %param.17) | copy-start | bytes 772
  36.7 10.9 %copy-start.8 = (f32[64]{0:T(128)S(1)}, f32[64]{0:T(128)}, u32[]{:S(2)}) copy-start(f32[64]{0:T(128)} %param.19) | copy-start | bytes 772
  61.0 1.8 %copy-start.5 = (f32[8,16,32]{2,0,1:T(8,128)S(1)}, f32[8,16,32]{2,0,1:T(8,128)}, u32[]{:S(2)}) copy-start(f32[8,16,32]{2,0,1:T(8,128)} %get-tuple-element.20) | copy-start | bytes 49156
  61.0 2.6 %copy-start.4 = (bf16[27,64,64]{2,1,0:T(8,128)(2,1)S(1)}, bf16[27,64,64]{2,1,0:T(8,128)(2,1)}, u32[]{:S(2)}) copy-start(bf16[27,64,64]{2,1,0:T(8,128)(2,1)} %param.20) | copy-start | bytes 663556
  61.0 2.8 %copy-start.9 = (f32[64]{0:T(128)S(1)}, f32[64]{0:T(128)}, u32[]{:S(2)}) copy-start(f32[64]{0:T(128)} %param.21) | copy-start | bytes 772
  63.9 7.4 %copy-start.10 = (f32[96]{0:T(128)S(1)}, f32[96]{0:T(128)}, u32[]{:S(2)}) copy-start(f32[96]{0:T(128)} %param.23) | copy-start | bytes 1156
  86.9 3.3 %copy-start.2 = (bf16[27,96,96]{2,1,0:T(8,128)(2,1)S(1)}, bf16[27,96,96]{2,1,0:T(8,128)(2,1)}, u32[]{:S(2)}) copy-start(bf16[27,96,96]{2,1,0:T(8,128)(2,1)} %param.24) | copy-start | bytes 1492996
  86.9 3.7 %copy-start.11 = (f32[96]{0:T(128)S(1)}, f32[96]{0:T(128)}, u32[]{:S(2)}) copy-start(f32[96]{0:T(128)} %param.25) | copy-start | bytes 1156
  86.9 3.7 %copy-start.14 = (pred[48,3]{0,1:T(4,128)(4,1)S(1)}, pred[48,3]{0,1:T(4,128)(4,1)}, u32[]{:S(2)}) copy-start(pred[48,3]{0,1:T(4,128)(4,1)} %constant.39) | copy-start | bytes 436
  96.7 1.1 %copy-start.3 = (bf16[27,96,96]{2,1,0:T(8,128)(2,1)S(1)}, bf16[27,96,96]{2,1,0:T(8,128)(2,1)}, u32[]{:S(2)}) copy-start(bf16[27,96,96]{2,1,0:T(8,128)(2,1)} %param.26) | copy-start | bytes 1492996
  97.0 1.1 %copy-start.12 = (f32[96]{0:T(128)S(1)}, f32[96]{0:T(128)}, u32[]{:S(2)}) copy-start(f32[96]{0:T(128)} %param.27) | copy-start | bytes 1156
  97.0 1.1 %copy-start.13 = (pred[32,3]{0,1:T(4,128)(4,1)S(1)}, pred[32,3]{0,1:T(4,128)(4,1)}, u32[]{:S(2)}) copy-start(pred[32,3]{0,1:T(4,128)(4,1)} %constant.38) | copy-start | bytes 292
  98.1 2.5 %copy-start.1 = (bf16[8,16,32,64]{3,0,2,1:T(8,128)(2,1)S(1)}, bf16[8,16,32,64]{3,0,2,1:T(8,128)(2,1)}, u32[]{:S(2)}) copy-start(bf16[8,16,32,64]{3,0,2,1:T(8,128)(2,1)} %multiply_convert_fusion.1) | copy-start | bytes 1572868

commit v4 on v0

--- a/solution.py
+++ b/solution.py
@@ -152,6 +152,14 @@
     return lax.conv_general_dilated(
         stacked, kernel, (1, 1), "VALID",
         dimension_numbers=("NHWC", "HWIO", "NHWC"), preferred_element_type=jnp.float32)
+
+
+def conv_cube(padded, weights):
+    kernel = weights.reshape(3, 3, 3, weights.shape[1], weights.shape[2]).transpose(2, 1, 0, 4, 3)
+    result = lax.conv_general_dilated(
+        padded[None], kernel, (1, 1, 1), "VALID",
+        dimension_numbers=("NDHWC", "DHWIO", "NDHWC"), preferred_element_type=jnp.float32)
+    return result[0]
 
 
 def down_first(grid, weights):
@@ -195,8 +203,8 @@
     mask_two = region_mask(tissue, (2, 2, 4), second_blocks, (second_x, second_y, second_z), 0)
     mask_two_wide = region_mask(tissue, (2, 2, 4), second_blocks, (second_x, second_y, second_z), 1)
     down_two = finish(down_cells(feat_one, w_down2), b_down2, mask_two)
-    middle = finish(conv_taps(with_rim(down_two, 2, 1), w_conv2a), b_conv2a, mask_two_wide)
-    feat_two = finish(conv_taps(middle, w_conv2b), b_conv2b, mask_two)
+    middle = finish(conv_cube(with_rim(down_two, 2, 1), w_conv2a), b_conv2a, mask_two_wide)
+    feat_two = finish(conv_cube(middle, w_conv2b), b_conv2b, mask_two)
     return (packed(feat_one), packed(feat_two))
 
 

time: 94.9 us -> 87.8 us (0.925)
  other arithmetic: 9.98 us -> 4.93 us
  matrix products: 32.3 us -> 31.1 us
    conv_general_dilated x4 -> x2, matrix products: 24.7 us -> 19.1 us  [conv_taps(): lax.conv_general_dilated(stacked, kernel, (1, 1), 'VALID', dimension_numb...]
    conv_general_dilated x0 -> x2, matrix products: none -> 4.37 us  [conv_cube(): lax.conv_general_dilated(padded[None], kernel, (1, 1, 1), 'VALID', dimens...]
    conv_general_dilated x2 -> x0, other arithmetic: 3.87 us -> none  [conv_taps(): lax.conv_general_dilated(stacked, kernel, (1, 1), 'VALID', dimension_numb...]
    reshape x2, local copies, waits for them, and re-layouts: 0.5 us -> 2.21 us  [conv_taps(): weights.reshape(3, 3, 3, weights.shape[1], weights.shape[2])]
    slice x4 -> x2, local copies, waits for them, and re-layouts: 7.28 us -> 5.65 us  [conv_taps(): stacked = jnp.concatenate([padded[k:k + size_z] for k in range(3)], axis=-1)]
    unnamed x41 -> x30, local copies, waits for them, and re-layouts: 11.6 us -> 13.1 us
    concatenate x3 -> x1, other arithmetic: 4.62 us -> 3.46 us  [conv_taps(): stacked = jnp.concatenate([padded[k:k + size_z] for k in range(3)], axis=-1)]
    conv_general_dilated x3 -> x7, local copies, waits for them, and re-layouts: 1.67 us -> 0.62 us  [conv_cube(): lax.conv_general_dilated(padded[None], kernel, (1, 1, 1), 'VALID', dimens...]
where the time goes in v4:
time: 87.8 us; the launch traced here: 87.2 us
  matrix products  31.1 us (35%)
  Pallas kernels  26.4 us (30%)
  local copies, waits for them, and re-layouts  23.9 us (27%)
  other arithmetic  4.93 us (6%)
  between operations  1.02 us (1%)
    pallas_call x2, Pallas kernels, with_rim(): pl.pallas_call(functools.partial(rim_kernel, width), out_shape=jax.ShapeD...  26.4 us
    conv_general_dilated x2, matrix products, conv_taps(): lax.conv_general_dilated(stacked, kernel, (1, 1), 'VALID', dimension_numb...  19.1 us
    unnamed x30, local copies, waits for them, and re-layouts  13.1 us
    dot_general x1, matrix products, down_first(): jnp.einsum('abkoi,izkybxa->zyxo', grouped, split, preferred_element_type=...  6.56 us
    slice x2, local copies, waits for them, and re-layouts, conv_taps(): stacked = jnp.concatenate([padded[k:k + size_z] for k in range(3)], axis=-1)  5.65 us
    conv_general_dilated x2, matrix products, conv_cube(): lax.conv_general_dilated(padded[None], kernel, (1, 1, 1), 'VALID', dimens...  4.37 us
    concatenate x1, other arithmetic, conv_taps(): stacked = jnp.concatenate([padded[k:k + size_z] for k in range(3)], axis=-1)  3.46 us
    reshape x2, local copies, waits for them, and re-layouts, conv_taps(): weights.reshape(3, 3, 3, weights.shape[1], weights.shape[2])  2.21 us

profile of v4, /device:TPU:1, one launch (start us, length us, event | category | flops | bytes accessed | tf_op | source)
XLA Modules:
  0.0 87.2 jit_solution(16370354459303957507)
XLA Ops:
  0.6 0.0 copy-start
  0.7 0.9 %pad_dynamic-slice_fusion = s32[10,6,3]{1,2,0:T(4,128)S(1)} fusion(s32[]{:T(128)S(6)} %select_n.6, s32[]{:T(128)S(6)} %select_n.7, s32[]{:T(128)S(6)} %select_n.8, s32[32,32,4]{1,2,0:T(4,128)} %param.15), kind=kLoop, calls=%fused_computation.55 | loop fusion | bytes 17116 | tf_op jit(solution)/shard_map/dynamic_slice | solution.py:132
  1.6 0.1 copy.35
  1.7 0.1 fusion.51
  1.8 0.0 copy-start.6
  1.8 0.0 copy-start.7
  1.8 8.7 %copy.32 = bf16[48,16,2048]{0,2,1:T(8,128)(2,1)} copy(bf16[48,16,2048]{2,1,0:T(8,128)(2,1)} %param.14) | data formatting | bytes 6291456 | tf_op args[0]
  10.5 0.0 copy-done.6
  10.5 0.0 copy-done.7
  10.5 6.6 %fusion.12.f_ref = bf16[8,16,32,64]{3,2,1,0:T(8,128)(2,1)} fusion(bf16[2,2,2,64,48,1,1]{3,4,2,1,0,6,5:T(8,128)(2,1)S(1)} %bitcast.113, bf16[48,8,2,16,2,32,2]{0,6,5,4,3,2,1:T(2,128)(2,1)} %bitcast.94, f32[8,16,32]{2,1,0:T(8,128)S(1)} %fusion.51, f32[64]{0:T(128)S(1)} %copy-done.7), kind=kOutput, calls=%fused_computation.15 | convolution fusion | flops 202375168 | bytes 3735808 | tf_op jit(solution)/shard_map/abkoi,izkybxa->zyxo/dot_general | solution.py:169
  17.1 17.5 %shard_map.149 = bf16[12,20,36,64]{3,2,1,0:T(8,128)(2,1)} custom-call(bf16[8,16,32,64]{3,2,1,0:T(8,128)(2,1)} %fusion.12.f_ref), custom_call_target="tpu_custom_call" | custom-call | tf_op jit(solution)/shard_map/pallas_call | solution.py:113
  34.6 3.9 %fusion.62 = (bf16[10,20,36,64]{3,2,1,0:T(8,128)(2,1)S(1)}, bf16[10,20,36,64]{3,2,1,0:T(8,128)(2,1)S(1)}, bf16[10,20,36,64]{3,2,1,0:T(8,128)(2,1)S(1)}) fusion(bf16[12,20,36,64]{3,2,1,0:T(8,128)(2,1)} %shard_map.149), kind=kLoop, calls=%fused_computation.72 | loop fusion | bytes 5529600 | tf_op jit(solution)/shard_map/slice | solution.py:149
  38.5 0.0 copy-start.1
  38.5 0.0 copy-start.8
  38.5 3.5 %pad_maximum_fusion = bf16[10,20,36,192]{3,2,1,0:T(8,128)(2,1)} fusion(bf16[10,20,36,64]{3,2,1,0:T(8,128)(2,1)S(1)} %get-tuple-element.10, bf16[10,20,36,64]{3,2,1,0:T(8,128)(2,1)S(1)} %get-tuple-element.11, bf16[10,20,36,64]{3,2,1,0:T(8,128)(2,1)S(1)} %get-tuple-element.9), kind=kLoop, calls=%fused_computation.5 | loop fusion | flops 8294400 | bytes 5529600 | tf_op jit(solution)/shard_map/concatenate | solution.py:149
  42.0 0.1 fusion.50
  42.1 0.2 copy.38
  42.3 0.0 copy-done.1
  42.3 0.2 copy.36
  42.6 0.0 copy-done.8
  42.6 12.4 %multiply_convert_fusion = bf16[10,18,34,64]{3,0,2,1:T(8,128)(2,1)S(1)} fusion(f32[10,18,34]{0,2,1:T(8,128)S(1)} %copy.38, f32[64]{0:T(128)S(1)} %copy-done.8, bf16[3,3,192,64]{3,2,1,0:T(8,128)(2,1)S(1)} %bitcast.106, bf16[10,20,36,192]{3,2,1,0:T(8,128)(2,1)} %pad_maximum_fusion), kind=kOutput, calls=%fused_computation.4 | convolution fusion | flops 1355212800 | bytes 3794080 | tf_op jit(solution)/shard_map/conv_general_dilated | solution.py:152
  54.9 1.7 %fusion.61 = (bf16[8,18,34,64]{3,0,2,1:T(8,128)(2,1)S(1)}, bf16[8,18,34,64]{3,0,2,1:T(8,128)(2,1)S(1)}, bf16[8,18,34,64]{3,0,2,1:T(8,128)(2,1)}) fusion(bf16[10,18,34,64]{3,0,2,1:T(8,128)(2,1)S(1)} %multiply_convert_fusion), kind=kLoop, calls=%fused_computation.71 | loop fusion | bytes 3760128 | tf_op jit(solution)/shard_map/slice | solution.py:149
  56.7 2.0 %copy.39 = bf16[3,3,3,64,64]{3,4,2,0,1:T(8,128)(2,1)} copy(bf16[3,3,3,64,64]{4,3,2,1,0:T(8,128)(2,1)} %bitcast.104) | data formatting | bytes 442368 | tf_op jit(solution)/shard_map/reshape | solution.py:150
  58.7 0.0 copy-start.3
  58.7 6.7 %fusion.4 = f32[8,16,32,64]{3,0,2,1:T(8,128)S(1)} fusion(bf16[3,3,192,64]{3,2,1,0:T(8,128)(2,1)} %bitcast.105, bf16[8,18,34,64]{3,0,2,1:T(8,128)(2,1)S(1)} %get-tuple-element.7, bf16[8,18,34,64]{3,0,2,1:T(8,128)(2,1)} %get-tuple-element.8, bf16[8,18,34,64]{3,0,2,1:T(8,128)(2,1)S(1)} %get-tuple-element.6), kind=kOutput, calls=%fused_computation.6 | convolution fusion | flops 911609856 | bytes 3149824 | tf_op jit(solution)/shard_map/conv_general_dilated | solution.py:152
  65.4 0.0 copy-done.3
  65.4 0.0 copy-start.5
  65.4 0.0 copy-start.9
  65.4 0.7 fusion.15
  66.2 0.1 copy.43
  66.4 0.1 fusion.53
  66.5 0.0 copy-done.5
  66.5 0.0 copy-done.9
  66.5 1.0 %fusion.27.f_ref = bf16[4,8,16,96]{3,2,1,0:T(8,128)(2,1)} fusion(bf16[2,2,2,96,64,1,1]{3,4,2,1,0,6,5:T(8,128)(2,1)S(1)} %bitcast.112, bf16[4,2,8,2,16,2,64]{6,5,4,3,2,1,0:T(2,128)(2,1)S(1)} %bitcast.95, f32[4,8,16]{2,1,0:T(8,128)S(1)} %fusion.53, f32[96]{0:T(128)S(1)} %copy-done.9), kind=kOutput, calls=%fused_computation.32 | convolution fusion | flops 50528256 | bytes 723328 | tf_op jit(solution)/shard_map/abkoi,zkybxai->zyxo/dot_general | solution.py:176
  67.5 8.9 %shard_map.150 = bf16[8,12,20,96]{3,2,1,0:T(8,128)(2,1)} custom-call(bf16[4,8,16,96]{3,2,1,0:T(8,128)(2,1)} %fusion.27.f_ref), custom_call_target="tpu_custom_call" | custom-call | tf_op jit(solution)/shard_map/pallas_call | solution.py:113
  76.4 0.0 copy-start.10
  76.4 0.0 copy-start.12
  76.5 1.3 %copy.61 = bf16[8,12,1,20,96]{4,0,3,1,2:T(8,128)(2,1)S(1)} copy(bf16[8,12,1,20,96]{4,3,1,0,2:T(8,128)(2,1)} %bitcast.97) | data formatting | bytes 737280
  77.7 0.1 pad.8.clone
  77.9 0.1 copy.46
  78.0 0.1 slice.50
  78.1 0.0 copy-done
  78.1 0.0 copy-done.10
  78.1 0.0 copy-done.12
  78.1 2.8 %fusion.22 = f32[6,10,8,3,96]{4,2,3,1,0:T(8,128)S(1)} fusion(bf16[8,12,1,7,2,96]{5,3,4,1,0,2:T(8,128)(2,1)S(1)} %slice.50, bf16[8,12,1,8,3,96]{5,3,4,1,0,2:T(8,128)(2,1)S(1)} %copy.46, bf16[3,3,3,96,96]{4,3,2,1,0:T(8,128)(2,1)S(1)} %bitcast.93, f32[96]{0:T(128)S(1)} %copy-done.10, pred[8,3]{0,1:T(4,128)(4,1)S(1)} %copy-done.12), kind=kOutput, calls=%fused_computation.24 | convolution fusion | flops 719262720 | bytes 1751448 | tf_op jit(solution)/shard_map/conv_general_dilated | solution.py:159
  80.9 0.3 copy.48
  81.2 0.3 reshape.94
  81.6 0.0 copy-start.11
  81.6 0.1 fusion.52
  81.7 0.3 fusion.35
  81.9 0.0 copy-start.4
  81.9 0.1 pad.10
  82.0 0.2 reshape.97
  82.3 0.1 copy.50
  82.3 0.1 slice.53
  82.4 0.0 copy-done.11
  82.4 0.6 copy-done.4
  83.0 0.0 copy-start.2
  83.0 1.5 %convolution_select_fusion.1 = f32[4,8,8,3,96]{4,2,3,1,0:T(8,128)S(1)} fusion(bf16[3,3,3,96,96]{4,3,2,1,0:T(8,128)(2,1)S(1)} %bitcast.111, bf16[6,10,1,7,2,96]{5,3,4,1,0,2:T(8,128)(2,1)S(1)} %slice.53, bf16[6,10,1,8,3,96]{5,3,4,1,0,2:T(8,128)(2,1)S(1)} %copy.50, pred[8,3]{0,1:T(4,128)(4,1)S(1)} %copy-done.11), kind=kOutput, calls=%fused_computation.27 | convolution fusion | flops 383662080 | bytes 1230360 | tf_op jit(solution)/shard_map/conv_general_dilated | solution.py:159
  84.6 0.1 copy.52
  84.7 0.0 copy-done.2
  84.7 0.1 fusion.49
  84.8 0.8 copy.55
  85.6 1.7 %copy.54 = bf16[64,8,512]{2,1,0:T(8,128)(2,1)} copy(bf16[64,8,512]{0,2,1:T(8,128)(2,1)S(1)} %bitcast.96) | data formatting | bytes 1048576
  (10 shorter events, 0.1 us)
Async XLA Ops:
  0.6 77.4 %copy-start = (bf16[27,96,96]{2,1,0:T(8,128)(2,1)S(1)}, bf16[27,96,96]{2,1,0:T(8,128)(2,1)}, u32[]{:S(2)}) copy-start(bf16[27,96,96]{2,1,0:T(8,128)(2,1)} %param.24) | copy-start | bytes 1492996
  1.8 8.7 %copy-start.6 = (bf16[8,64,48]{1,2,0:T(8,128)(2,1)S(1)}, bf16[8,64,48]{1,2,0:T(8,128)(2,1)}, u32[]{:S(2)}) copy-start(bf16[8,64,48]{1,2,0:T(8,128)(2,1)} %param.16) | copy-start | bytes 147460
  1.8 8.7 %copy-start.7 = (f32[64]{0:T(128)S(1)}, f32[64]{0:T(128)}, u32[]{:S(2)}) copy-start(f32[64]{0:T(128)} %param.17) | copy-start | bytes 772
  38.5 3.8 %copy-start.1 = (bf16[27,64,64]{2,1,0:T(8,128)(2,1)S(1)}, bf16[27,64,64]{2,1,0:T(8,128)(2,1)}, u32[]{:S(2)}) copy-start(bf16[27,64,64]{2,1,0:T(8,128)(2,1)} %param.18) | copy-start | bytes 663556
  38.5 4.1 %copy-start.8 = (f32[64]{0:T(128)S(1)}, f32[64]{0:T(128)}, u32[]{:S(2)}) copy-start(f32[64]{0:T(128)} %param.19) | copy-start | bytes 772
  58.7 6.8 %copy-start.3 = (f32[64]{0:T(128)S(1)}, f32[64]{0:T(128)}, u32[]{:S(2)}) copy-start(f32[64]{0:T(128)} %param.21) | copy-start | bytes 772
  65.4 1.1 %copy-start.5 = (bf16[8,96,64]{1,2,0:T(8,128)(2,1)S(1)}, bf16[8,96,64]{1,2,0:T(8,128)(2,1)}, u32[]{:S(2)}) copy-start(bf16[8,96,64]{1,2,0:T(8,128)(2,1)} %param.22) | copy-start | bytes 294916
  65.4 1.0 %copy-start.9 = (f32[96]{0:T(128)S(1)}, f32[96]{0:T(128)}, u32[]{:S(2)}) copy-start(f32[96]{0:T(128)} %param.23) | copy-start | bytes 1156
  76.4 1.7 %copy-start.10 = (f32[96]{0:T(128)S(1)}, f32[96]{0:T(128)}, u32[]{:S(2)}) copy-start(f32[96]{0:T(128)} %param.25) | copy-start | bytes 1156
  76.4 1.7 %copy-start.12 = (pred[8,3]{0,1:T(4,128)(4,1)S(1)}, pred[8,3]{0,1:T(4,128)(4,1)}, u32[]{:S(2)}) copy-start(pred[8,3]{0,1:T(4,128)(4,1)} %constant.39) | copy-start | bytes 76
  81.6 0.8 copy-start.11
  81.9 1.1 %copy-start.4 = (bf16[27,96,96]{2,1,0:T(8,128)(2,1)S(1)}, bf16[27,96,96]{2,1,0:T(8,128)(2,1)}, u32[]{:S(2)}) copy-start(bf16[27,96,96]{2,1,0:T(8,128)(2,1)} %param.26) | copy-start | bytes 1492996
  83.0 1.7 %copy-start.2 = (f32[96]{0:T(128)S(1)}, f32[96]{0:T(128)}, u32[]{:S(2)}) copy-start(f32[96]{0:T(128)} %param.27) | copy-start | bytes 1156

commit v5 on v4

--- a/solution.py
+++ b/solution.py
@@ -20,9 +20,10 @@
 ]
 
 
-def rim_kernel(width, f_ref, p_ref, local_sem, send_sem, recv_sem):
+def rim_kernel(widths, f_ref, p_ref, local_sem, send_sem, recv_sem):
     size_z, size_y, size_x, _ = f_ref.shape
     sizes = (size_x, size_y, size_z)
+    reach = (widths[2], widths[1], widths[0])
     index = [lax.axis_index(a) for a in AXES]
     count = [lax.axis_size(a) for a in AXES]
 
@@ -39,20 +40,20 @@
         return tuple(index[a] + d[a] for a in range(3))
 
     def source(a, step):
-        s = sizes[a]
+        s, w = sizes[a], reach[a]
         if step == -1:
-            return slice(0, width)
+            return slice(0, w)
         if step == 1:
-            return slice(s - width, s)
+            return slice(s - w, s)
         return slice(0, s)
 
     def side(a, step):
-        s = sizes[a]
+        s, w = sizes[a], reach[a]
         if step == -1:
-            return slice(0, width)
+            return slice(0, w)
         if step == 1:
-            return slice(s + width, s + 2 * width)
-        return slice(width, width + s)
+            return slice(s + w, s + 2 * w)
+        return slice(w, w + s)
 
     barrier = pltpu.get_barrier_semaphore()
     for d in DIRS:
@@ -61,7 +62,8 @@
             pl.semaphore_signal(barrier, inc=1, device_id=device(d), device_id_type=MESH)
 
     local = pltpu.make_async_copy(
-        f_ref, p_ref.at[width:width + size_z, width:width + size_y, width:width + size_x, :],
+        f_ref, p_ref.at[widths[0]:widths[0] + size_z, widths[1]:widths[1] + size_y,
+                        widths[2]:widths[2] + size_x, :],
         local_sem.at[0])
     local.start()
 
@@ -108,12 +110,13 @@
             copy.wait_recv()
 
 
-def with_rim(field, width, collective_id):
+def with_rim(field, widths, collective_id):
     size_z, size_y, size_x, chans = field.shape
     return pl.pallas_call(
-        functools.partial(rim_kernel, width),
+        functools.partial(rim_kernel, widths),
         out_shape=jax.ShapeDtypeStruct(
-            (size_z + 2 * width, size_y + 2 * width, size_x + 2 * width, chans), field.dtype),
+            (size_z + 2 * widths[0], size_y + 2 * widths[1], size_x + 2 * widths[2], chans),
+            field.dtype),
         in_specs=[pl.BlockSpec(memory_space=pltpu.VMEM)],
         out_specs=pl.BlockSpec(memory_space=pltpu.VMEM),
         scratch_shapes=[
@@ -194,7 +197,10 @@
     mask_one = region_mask(tissue, (4, 4, 8), first_blocks, (first_x, first_y, first_z), 0)
     mask_one_wide = region_mask(tissue, (4, 4, 8), first_blocks, (first_x, first_y, first_z), 1)
     down_one = finish(down_first(grid_zero, w_down1), b_down1, mask_one)
-    inner_one = finish(conv_taps(with_rim(down_one, 2, 0), w_conv1a), b_conv1a, mask_one_wide)
+    paired = down_one.reshape(first_z, first_y, first_x // 2, 2 * down_one.shape[3])
+    rimmed = with_rim(paired, (2, 2, 2), 0)
+    rimmed = rimmed.reshape(first_z + 4, first_y + 4, first_x + 8, down_one.shape[3])[:, :, 2:-2]
+    inner_one = finish(conv_taps(rimmed, w_conv1a), b_conv1a, mask_one_wide)
     feat_one = finish(conv_taps(inner_one, w_conv1b), b_conv1b, mask_one)
     second_x = first_x // 2
     second_y = first_y // 2
@@ -203,7 +209,7 @@
     mask_two = region_mask(tissue, (2, 2, 4), second_blocks, (second_x, second_y, second_z), 0)
     mask_two_wide = region_mask(tissue, (2, 2, 4), second_blocks, (second_x, second_y, second_z), 1)
     down_two = finish(down_cells(feat_one, w_down2), b_down2, mask_two)
-    middle = finish(conv_cube(with_rim(down_two, 2, 1), w_conv2a), b_conv2a, mask_two_wide)
+    middle = finish(conv_cube(with_rim(down_two, (2, 2, 2), 1), w_conv2a), b_conv2a, mask_two_wide)
     feat_two = finish(conv_cube(middle, w_conv2b), b_conv2b, mask_two)
     return (packed(feat_one), packed(feat_two))
 

time: 87.8 us -> 90.4 us (1.030)
  local copies, waits for them, and re-layouts: 23.9 us -> 33.3 us
  Pallas kernels: 26.4 us -> 22.5 us
  other arithmetic: 4.93 us -> 1.47 us
    unnamed x30 -> x33, local copies, waits for them, and re-layouts: 13.1 us -> 20.7 us
    reshape x0 -> x2, local copies, waits for them, and re-layouts: none -> 4.36 us  [the longest x1 3.06 us: local(): rimmed.reshape(first_z + 4, first_y + 4, first_x + 8, down_one.shape[3])]
    pallas_call x2, Pallas kernels: 26.4 us -> 22.5 us  [with_rim(): pl.pallas_call(functools.partial(rim_kernel, widths), out_shape=jax.Shape...]
    concatenate x1 -> x0, other arithmetic: 3.46 us -> none  [conv_taps(): stacked = jnp.concatenate([padded[k:k + size_z] for k in range(3)], axis=-1)]
    slice x2, local copies, waits for them, and re-layouts: 5.65 us -> 3.11 us  [conv_taps(): stacked = jnp.concatenate([padded[k:k + size_z] for k in range(3)], axis=-1)]
    conv_general_dilated x2, matrix products: 19.1 us -> 20.7 us  [conv_taps(): lax.conv_general_dilated(stacked, kernel, (1, 1), 'VALID', dimension_numb...]
    dot_general x1, matrix products: 6.56 us -> 5.5 us  [down_first(): jnp.einsum('abkoi,izkybxa->zyxo', grouped, split, preferred_element_type=...]
where the time goes in v5:
time: 90.4 us; the launch traced here: 89.9 us
  local copies, waits for them, and re-layouts  33.3 us (37%)
  matrix products  31.6 us (35%)
  Pallas kernels  22.5 us (25%)
  other arithmetic  1.47 us (2%)
  between operations  1.01 us (1%)
    pallas_call x2, Pallas kernels, with_rim(): pl.pallas_call(functools.partial(rim_kernel, widths), out_shape=jax.Shape...  22.5 us
    unnamed x33, local copies, waits for them, and re-layouts  20.7 us
    conv_general_dilated x2, matrix products, conv_taps(): lax.conv_general_dilated(stacked, kernel, (1, 1), 'VALID', dimension_numb...  20.7 us
    dot_general x1, matrix products, down_first(): jnp.einsum('abkoi,izkybxa->zyxo', grouped, split, preferred_element_type=...  5.5 us
    conv_general_dilated x2, matrix products, conv_cube(): lax.conv_general_dilated(padded[None], kernel, (1, 1, 1), 'VALID', dimens...  4.37 us
    slice x2, local copies, waits for them, and re-layouts, conv_taps(): stacked = jnp.concatenate([padded[k:k + size_z] for k in range(3)], axis=-1)  3.11 us
    reshape x1, local copies, waits for them, and re-layouts, local(): rimmed.reshape(first_z + 4, first_y + 4, first_x + 8, down_one.shape[3])  3.06 us
    reshape x2, local copies, waits for them, and re-layouts, conv_taps(): weights.reshape(3, 3, 3, weights.shape[1], weights.shape[2])  2.21 us

profile of v5, /device:TPU:1, one launch (start us, length us, event | category | flops | bytes accessed | tf_op | source)
XLA Modules:
  0.0 89.9 jit_solution(11895148359850753561)
XLA Ops:
  0.6 0.0 copy-start
  0.7 0.9 %pad_dynamic-slice_fusion = s32[10,6,3]{1,2,0:T(4,128)S(1)} fusion(s32[]{:T(128)S(6)} %select_n.6, s32[]{:T(128)S(6)} %select_n.7, s32[]{:T(128)S(6)} %select_n.8, s32[32,32,4]{1,2,0:T(4,128)} %param.15), kind=kLoop, calls=%fused_computation.58 | loop fusion | bytes 17116 | tf_op jit(solution)/shard_map/dynamic_slice | solution.py:135
  1.6 0.1 copy.37
  1.7 0.1 fusion.55
  1.8 0.0 copy-start.6
  1.8 0.0 copy-start.7
  1.8 8.7 %copy.34 = bf16[48,16,2048]{0,2,1:T(8,128)(2,1)} copy(bf16[48,16,2048]{2,1,0:T(8,128)(2,1)} %param.14) | data formatting | bytes 6291456 | tf_op args[0]
  10.5 0.0 copy-done.6
  10.5 0.0 copy-done.7
  10.5 5.5 %fusion.16 = bf16[8,16,32,64]{3,2,1,0:T(8,128)(2,1)S(1)} fusion(bf16[2,2,2,64,48,1,1]{3,4,2,1,0,6,5:T(8,128)(2,1)S(1)} %bitcast.115, bf16[48,8,2,16,2,32,2]{0,6,5,4,3,2,1:T(2,128)(2,1)} %bitcast.96, f32[8,16,32]{2,1,0:T(8,128)S(1)} %fusion.55, f32[64]{0:T(128)S(1)} %copy-done.7), kind=kOutput, calls=%fused_computation.18 | convolution fusion | flops 202375168 | bytes 3735808 | tf_op jit(solution)/shard_map/abkoi,izkybxa->zyxo/dot_general | solution.py:172
  16.0 1.3 %reshape.81.f_ref = bf16[8,16,16,128]{3,2,1,0:T(8,128)(2,1)} reshape(bf16[8,16,32,64]{3,2,1,0:T(8,128)(2,1)S(1)} %fusion.16) | data formatting | bytes 1048576 | tf_op jit(solution)/shard_map/reshape | solution.py:200
  17.4 13.6 %shard_map.149 = bf16[12,20,20,128]{3,2,1,0:T(8,128)(2,1)} custom-call(bf16[8,16,16,128]{3,2,1,0:T(8,128)(2,1)} %reshape.81.f_ref), custom_call_target="tpu_custom_call" | custom-call | tf_op jit(solution)/shard_map/pallas_call | solution.py:115
  31.0 3.1 %reshape.82 = bf16[12,20,40,64]{3,2,1,0:T(8,128)(2,1)S(1)} reshape(bf16[12,20,20,128]{3,2,1,0:T(8,128)(2,1)} %shard_map.149) | data formatting | bytes 2457600 | tf_op jit(solution)/shard_map/reshape | solution.py:202
  34.0 1.4 %fusion.67 = (bf16[10,20,36,64]{3,2,1,0:T(8,128)(2,1)S(1)}, bf16[10,20,36,64]{3,2,1,0:T(8,128)(2,1)S(1)}, bf16[10,20,36,64]{3,2,1,0:T(8,128)(2,1)S(1)}) fusion(bf16[12,20,40,64]{3,2,1,0:T(8,128)(2,1)S(1)} %reshape.82), kind=kLoop, calls=%fused_computation.76 | loop fusion | bytes 5529600 | tf_op jit(solution)/shard_map/slice | solution.py:152
  35.4 2.6 %copy.64 = bf16[10,20,36,64]{3,0,2,1:T(8,128)(2,1)} copy(bf16[10,20,36,64]{3,2,1,0:T(8,128)(2,1)S(1)} %get-tuple-element.9) | data formatting | bytes 1843200
  38.0 2.5 %copy.65 = bf16[10,20,36,64]{3,0,2,1:T(8,128)(2,1)} copy(bf16[10,20,36,64]{3,2,1,0:T(8,128)(2,1)S(1)} %get-tuple-element.10) | data formatting | bytes 1843200
  40.5 0.0 copy-start.1
  40.5 0.0 copy-start.8
  40.5 2.5 %copy.66 = bf16[10,20,36,64]{3,0,2,1:T(8,128)(2,1)} copy(bf16[10,20,36,64]{3,2,1,0:T(8,128)(2,1)S(1)} %get-tuple-element.11) | data formatting | bytes 1843200
  43.1 0.1 fusion.54
  43.2 0.2 copy.42
  43.4 0.0 copy-done.1
  43.4 0.2 copy.41
  43.7 0.0 copy-done.8
  43.7 13.9 %multiply_convert_fusion = bf16[10,18,34,64]{3,0,2,1:T(8,128)(2,1)S(1)} fusion(f32[10,18,34]{0,2,1:T(8,128)S(1)} %copy.42, f32[64]{0:T(128)S(1)} %copy-done.8, bf16[3,3,192,64]{3,2,1,0:T(8,128)(2,1)S(1)} %bitcast.107, bf16[10,20,36,64]{3,0,2,1:T(8,128)(2,1)} %copy.66, bf16[10,20,36,64]{3,0,2,1:T(8,128)(2,1)} %copy.65, bf16[10,20,36,64]{3,0,2,1:T(8,128)(2,1)} %copy.64), kind=kOutput, calls=%fused_computation.8 | convolution fusion | flops 1363507200 | bytes 3794080 | tf_op jit(solution)/shard_map/conv_general_dilated | solution.py:155
  57.6 1.7 %fusion.66 = (bf16[8,18,34,64]{3,0,2,1:T(8,128)(2,1)S(1)}, bf16[8,18,34,64]{3,0,2,1:T(8,128)(2,1)S(1)}, bf16[8,18,34,64]{3,0,2,1:T(8,128)(2,1)}) fusion(bf16[10,18,34,64]{3,0,2,1:T(8,128)(2,1)S(1)} %multiply_convert_fusion), kind=kLoop, calls=%fused_computation.75 | loop fusion | bytes 3760128 | tf_op jit(solution)/shard_map/slice | solution.py:152
  59.3 2.0 %copy.43 = bf16[3,3,3,64,64]{3,4,2,0,1:T(8,128)(2,1)} copy(bf16[3,3,3,64,64]{4,3,2,1,0:T(8,128)(2,1)} %bitcast.106) | data formatting | bytes 442368 | tf_op jit(solution)/shard_map/reshape | solution.py:153
  61.3 6.8 %fusion.8 = f32[8,16,32,64]{3,0,2,1:T(8,128)S(1)} fusion(bf16[3,3,192,64]{3,2,1,0:T(8,128)(2,1)} %bitcast.108, bf16[8,18,34,64]{3,0,2,1:T(8,128)(2,1)S(1)} %get-tuple-element.7, bf16[8,18,34,64]{3,0,2,1:T(8,128)(2,1)} %get-tuple-element.8, bf16[8,18,34,64]{3,0,2,1:T(8,128)(2,1)S(1)} %get-tuple-element.6), kind=kOutput, calls=%fused_computation.9 | convolution fusion | flops 911609856 | bytes 3149824 | tf_op jit(solution)/shard_map/conv_general_dilated | solution.py:155
  68.1 0.0 copy-done.3
  68.1 0.0 copy-start.5
  68.1 0.0 copy-start.9
  68.1 0.7 fusion.19
  68.9 0.1 copy.47
  69.0 0.1 fusion.57
  69.1 0.0 copy-done.5
  69.1 0.0 copy-done.9
  69.1 1.0 %fusion.31.f_ref = bf16[4,8,16,96]{3,2,1,0:T(8,128)(2,1)} fusion(bf16[2,2,2,96,64,1,1]{3,4,2,1,0,6,5:T(8,128)(2,1)S(1)} %bitcast.114, bf16[4,2,8,2,16,2,64]{6,5,4,3,2,1,0:T(2,128)(2,1)S(1)} %bitcast.97, f32[4,8,16]{2,1,0:T(8,128)S(1)} %fusion.57, f32[96]{0:T(128)S(1)} %copy-done.9), kind=kOutput, calls=%fused_computation.35 | convolution fusion | flops 50528256 | bytes 723328 | tf_op jit(solution)/shard_map/abkoi,zkybxai->zyxo/dot_general | solution.py:179
  70.1 8.9 %shard_map.150 = bf16[8,12,20,96]{3,2,1,0:T(8,128)(2,1)} custom-call(bf16[4,8,16,96]{3,2,1,0:T(8,128)(2,1)} %fusion.31.f_ref), custom_call_target="tpu_custom_call" | custom-call | tf_op jit(solution)/shard_map/pallas_call | solution.py:115
  79.1 1.3 %copy.68 = bf16[8,12,1,20,96]{4,0,3,1,2:T(8,128)(2,1)S(1)} copy(bf16[8,12,1,20,96]{4,3,1,0,2:T(8,128)(2,1)} %bitcast.99) | data formatting | bytes 737280
  80.3 0.1 pad.8.clone
  80.5 0.1 copy.50
  80.6 0.1 slice.57
  80.7 0.0 copy-done
  80.7 0.0 copy-done.10
  80.7 0.0 copy-done.12
  80.7 2.8 %fusion.26 = f32[6,10,8,3,96]{4,2,3,1,0:T(8,128)S(1)} fusion(bf16[8,12,1,7,2,96]{5,3,4,1,0,2:T(8,128)(2,1)S(1)} %slice.57, bf16[8,12,1,8,3,96]{5,3,4,1,0,2:T(8,128)(2,1)S(1)} %copy.50, bf16[3,3,3,96,96]{4,3,2,1,0:T(8,128)(2,1)S(1)} %bitcast.95, f32[96]{0:T(128)S(1)} %copy-done.10, pred[8,3]{0,1:T(4,128)(4,1)S(1)} %copy-done.12), kind=kOutput, calls=%fused_computation.27 | convolution fusion | flops 719262720 | bytes 1751448 | tf_op jit(solution)/shard_map/conv_general_dilated | solution.py:162
  83.5 0.3 copy.52
  83.8 0.3 reshape.102
  84.2 0.0 copy-start.11
  84.2 0.1 fusion.56
  84.3 0.3 fusion.39
  84.5 0.0 copy-start.4
  84.5 0.1 pad.10
  84.6 0.2 reshape.105
  84.9 0.1 copy.54
  84.9 0.1 slice.60
  85.0 0.0 copy-done.11
  85.0 0.6 copy-done.4
  85.6 1.5 %convolution_select_fusion.1 = f32[4,8,8,3,96]{4,2,3,1,0:T(8,128)S(1)} fusion(bf16[3,3,3,96,96]{4,3,2,1,0:T(8,128)(2,1)S(1)} %bitcast.113, bf16[6,10,1,7,2,96]{5,3,4,1,0,2:T(8,128)(2,1)S(1)} %slice.60, bf16[6,10,1,8,3,96]{5,3,4,1,0,2:T(8,128)(2,1)S(1)} %copy.54, pred[8,3]{0,1:T(4,128)(4,1)S(1)} %copy-done.11), kind=kOutput, calls=%fused_computation.30 | convolution fusion | flops 383662080 | bytes 1230360 | tf_op jit(solution)/shard_map/conv_general_dilated | solution.py:162
  87.2 0.1 copy.56
  87.3 0.0 copy-done.2
  87.3 0.1 fusion.53
  87.4 0.8 copy.59
  88.2 1.7 %copy.58 = bf16[64,8,512]{2,1,0:T(8,128)(2,1)} copy(bf16[64,8,512]{0,2,1:T(8,128)(2,1)S(1)} %bitcast.98) | data formatting | bytes 1048576
  (14 shorter events, 0.2 us)
Async XLA Ops:
  0.6 80.0 %copy-start = (bf16[27,96,96]{2,1,0:T(8,128)(2,1)S(1)}, bf16[27,96,96]{2,1,0:T(8,128)(2,1)}, u32[]{:S(2)}) copy-start(bf16[27,96,96]{2,1,0:T(8,128)(2,1)} %param.24) | copy-start | bytes 1492996
  1.8 8.7 %copy-start.6 = (bf16[8,64,48]{1,2,0:T(8,128)(2,1)S(1)}, bf16[8,64,48]{1,2,0:T(8,128)(2,1)}, u32[]{:S(2)}) copy-start(bf16[8,64,48]{1,2,0:T(8,128)(2,1)} %param.16) | copy-start | bytes 147460
  1.8 8.7 %copy-start.7 = (f32[64]{0:T(128)S(1)}, f32[64]{0:T(128)}, u32[]{:S(2)}) copy-start(f32[64]{0:T(128)} %param.17) | copy-start | bytes 772
  40.5 2.9 %copy-start.1 = (bf16[27,64,64]{2,1,0:T(8,128)(2,1)S(1)}, bf16[27,64,64]{2,1,0:T(8,128)(2,1)}, u32[]{:S(2)}) copy-start(bf16[27,64,64]{2,1,0:T(8,128)(2,1)} %param.18) | copy-start | bytes 663556
  40.5 3.1 %copy-start.8 = (f32[64]{0:T(128)S(1)}, f32[64]{0:T(128)}, u32[]{:S(2)}) copy-start(f32[64]{0:T(128)} %param.19) | copy-start | bytes 772
  61.3 6.8 %copy-start.3 = (f32[64]{0:T(128)S(1)}, f32[64]{0:T(128)}, u32[]{:S(2)}) copy-start(f32[64]{0:T(128)} %param.21) | copy-start | bytes 772
  68.1 1.1 %copy-start.5 = (bf16[8,96,64]{1,2,0:T(8,128)(2,1)S(1)}, bf16[8,96,64]{1,2,0:T(8,128)(2,1)}, u32[]{:S(2)}) copy-start(bf16[8,96,64]{1,2,0:T(8,128)(2,1)} %param.22) | copy-start | bytes 294916
  68.1 1.0 %copy-start.9 = (f32[96]{0:T(128)S(1)}, f32[96]{0:T(128)}, u32[]{:S(2)}) copy-start(f32[96]{0:T(128)} %param.23) | copy-start | bytes 1156
  70.1 10.5 %copy-start.10 = (f32[96]{0:T(128)S(1)}, f32[96]{0:T(128)}, u32[]{:S(2)}) copy-start(f32[96]{0:T(128)} %param.25) | copy-start | bytes 1156
  70.1 10.5 %copy-start.12 = (pred[8,3]{0,1:T(4,128)(4,1)S(1)}, pred[8,3]{0,1:T(4,128)(4,1)}, u32[]{:S(2)}) copy-start(pred[8,3]{0,1:T(4,128)(4,1)} %constant.39) | copy-start | bytes 76
  84.2 0.8 copy-start.11
  84.5 1.1 %copy-start.4 = (bf16[27,96,96]{2,1,0:T(8,128)(2,1)S(1)}, bf16[27,96,96]{2,1,0:T(8,128)(2,1)}, u32[]{:S(2)}) copy-start(bf16[27,96,96]{2,1,0:T(8,128)(2,1)} %param.26) | copy-start | bytes 1492996
  85.6 1.7 %copy-start.2 = (f32[96]{0:T(128)S(1)}, f32[96]{0:T(128)}, u32[]{:S(2)}) copy-start(f32[96]{0:T(128)} %param.27) | copy-start | bytes 1156

commit v6 on v4

--- a/solution.py
+++ b/solution.py
@@ -20,7 +20,11 @@
 ]
 
 
-def rim_kernel(width, f_ref, p_ref, local_sem, send_sem, recv_sem):
+def rim_kernel(width, stack, f_ref, *refs):
+    if stack:
+        s_ref, p_ref, local_sem, send_sem, recv_sem = refs
+    else:
+        p_ref, local_sem, send_sem, recv_sem = refs
     size_z, size_y, size_x, _ = f_ref.shape
     sizes = (size_x, size_y, size_z)
     index = [lax.axis_index(a) for a in AXES]
@@ -107,22 +111,43 @@
         def _():
             copy.wait_recv()
 
-
-def with_rim(field, width, collective_id):
+    if stack:
+        chans = f_ref.shape[3]
+        depth = s_ref.shape[0]
+        for k in range(3):
+            s_ref[:, :, :, k * chans:(k + 1) * chans] = p_ref[k:k + depth]
+
+
+def with_rim(field, width, collective_id, stack):
     size_z, size_y, size_x, chans = field.shape
+    padded = (size_z + 2 * width, size_y + 2 * width, size_x + 2 * width, chans)
+    sems = [
+        pltpu.SemaphoreType.DMA((1,)),
+        pltpu.SemaphoreType.DMA((len(DIRS),)),
+        pltpu.SemaphoreType.DMA((len(DIRS),)),
+    ]
+    if stack:
+        shape = (padded[0] - 2, padded[1], padded[2], 3 * chans)
+        scratch = [pltpu.VMEM(padded, field.dtype)] + sems
+    else:
+        shape = padded
+        scratch = sems
     return pl.pallas_call(
-        functools.partial(rim_kernel, width),
-        out_shape=jax.ShapeDtypeStruct(
-            (size_z + 2 * width, size_y + 2 * width, size_x + 2 * width, chans), field.dtype),
+        functools.partial(rim_kernel, width, stack),
+        out_shape=jax.ShapeDtypeStruct(shape, field.dtype),
         in_specs=[pl.BlockSpec(memory_space=pltpu.VMEM)],
         out_specs=pl.BlockSpec(memory_space=pltpu.VMEM),
-        scratch_shapes=[
-            pltpu.SemaphoreType.DMA((1,)),
-            pltpu.SemaphoreType.DMA((len(DIRS),)),
-            pltpu.SemaphoreType.DMA((len(DIRS),)),
-        ],
+        scratch_shapes=scratch,
         compiler_params=pltpu.CompilerParams(collective_id=collective_id, has_side_effects=True),
     )(field)
+
+
+def conv_stacked(stacked, weights):
+    kernel = weights.reshape(3, 3, 3, weights.shape[1], weights.shape[2]).transpose(1, 0, 2, 4, 3)
+    kernel = kernel.reshape(3, 3, 3 * weights.shape[2], weights.shape[1])
+    return lax.conv_general_dilated(
+        stacked, kernel, (1, 1), "VALID",
+        dimension_numbers=("NHWC", "HWIO", "NHWC"), preferred_element_type=jnp.float32)
 
 
 def region_mask(tissue, repeats, block_starts, extents, margin):
@@ -194,7 +219,7 @@
     mask_one = region_mask(tissue, (4, 4, 8), first_blocks, (first_x, first_y, first_z), 0)
     mask_one_wide = region_mask(tissue, (4, 4, 8), first_blocks, (first_x, first_y, first_z), 1)
     down_one = finish(down_first(grid_zero, w_down1), b_down1, mask_one)
-    inner_one = finish(conv_taps(with_rim(down_one, 2, 0), w_conv1a), b_conv1a, mask_one_wide)
+    inner_one = finish(conv_stacked(with_rim(down_one, 2, 0, True), w_conv1a), b_conv1a, mask_one_wide)
     feat_one = finish(conv_taps(inner_one, w_conv1b), b_conv1b, mask_one)
     second_x = first_x // 2
     second_y = first_y // 2
@@ -203,7 +228,7 @@
     mask_two = region_mask(tissue, (2, 2, 4), second_blocks, (second_x, second_y, second_z), 0)
     mask_two_wide = region_mask(tissue, (2, 2, 4), second_blocks, (second_x, second_y, second_z), 1)
     down_two = finish(down_cells(feat_one, w_down2), b_down2, mask_two)
-    middle = finish(conv_cube(with_rim(down_two, 2, 1), w_conv2a), b_conv2a, mask_two_wide)
+    middle = finish(conv_cube(with_rim(down_two, 2, 1, False), w_conv2a), b_conv2a, mask_two_wide)
     feat_two = finish(conv_cube(middle, w_conv2b), b_conv2b, mask_two)
     return (packed(feat_one), packed(feat_two))
 

time: 87.8 us -> 82.1 us (0.935)
  local copies, waits for them, and re-layouts: 23.9 us -> 19.6 us
  other arithmetic: 4.93 us -> 1.69 us
  Pallas kernels: 26.4 us -> 28.3 us
    conv_general_dilated x2 -> x1, matrix products: 19.1 us -> 6.75 us  [conv_taps(): lax.conv_general_dilated(stacked, kernel, (1, 1), 'VALID', dimension_numb...]
    conv_general_dilated x0 -> x1, matrix products: none -> 12.3 us  [conv_stacked(): lax.conv_general_dilated(stacked, kernel, (1, 1), 'VALID', dimension_numb...]
    slice x2 -> x1, local copies, waits for them, and re-layouts: 5.65 us -> 1.75 us  [conv_taps(): stacked = jnp.concatenate([padded[k:k + size_z] for k in range(3)], axis=-1)]
    concatenate x1 -> x0, other arithmetic: 3.46 us -> none  [conv_taps(): stacked = jnp.concatenate([padded[k:k + size_z] for k in range(3)], axis=-1)]
    pallas_call x2, Pallas kernels: 26.4 us -> 28.3 us  [with_rim(): pl.pallas_call(functools.partial(rim_kernel, width, stack), out_shape=jax...]
    reshape x2 -> x1, local copies, waits for them, and re-layouts: 2.21 us -> 1.96 us  [conv_taps(): weights.reshape(3, 3, 3, weights.shape[1], weights.shape[2])]
where the time goes in v6:
time: 82.1 us; the launch traced here: 81.6 us
  matrix products  31 us (38%)
  Pallas kernels  28.3 us (34%)
  local copies, waits for them, and re-layouts  19.6 us (24%)
  other arithmetic  1.69 us (2%)
  between operations  0.99 us (1%)
    pallas_call x2, Pallas kernels, with_rim(): pl.pallas_call(functools.partial(rim_kernel, width, stack), out_shape=jax...  28.3 us
    unnamed x30, local copies, waits for them, and re-layouts  12.7 us
    conv_general_dilated x1, matrix products, conv_stacked(): lax.conv_general_dilated(stacked, kernel, (1, 1), 'VALID', dimension_numb...  12.3 us
    conv_general_dilated x1, matrix products, conv_taps(): lax.conv_general_dilated(stacked, kernel, (1, 1), 'VALID', dimension_numb...  6.75 us
    dot_general x1, matrix products, down_first(): jnp.einsum('abkoi,izkybxa->zyxo', grouped, split, preferred_element_type=...  6.57 us
    conv_general_dilated x2, matrix products, conv_cube(): lax.conv_general_dilated(padded[None], kernel, (1, 1, 1), 'VALID', dimens...  4.37 us
    reshape x1, local copies, waits for them, and re-layouts, conv_taps(): weights.reshape(3, 3, 3, weights.shape[1], weights.shape[2])  1.96 us
    slice x1, local copies, waits for them, and re-layouts, conv_taps(): stacked = jnp.concatenate([padded[k:k + size_z] for k in range(3)], axis=-1)  1.75 us

profile of v6, /device:TPU:1, one launch (start us, length us, event | category | flops | bytes accessed | tf_op | source)
XLA Modules:
  0.0 81.6 jit_solution(9101814595908367766)
XLA Ops:
  0.6 0.0 copy-start
  0.7 0.9 %pad_dynamic-slice_fusion = s32[10,6,3]{1,2,0:T(4,128)S(1)} fusion(s32[]{:T(128)S(6)} %select_n.6, s32[]{:T(128)S(6)} %select_n.7, s32[]{:T(128)S(6)} %select_n.8, s32[32,32,4]{1,2,0:T(4,128)} %param.15), kind=kLoop, calls=%fused_computation.54 | loop fusion | bytes 17116 | tf_op jit(solution)/shard_map/dynamic_slice | solution.py:157
  1.6 0.1 copy.35
  1.7 0.1 fusion.51
  1.8 0.0 copy-start.6
  1.8 0.0 copy-start.7
  1.8 8.7 %copy.32 = bf16[48,16,2048]{0,2,1:T(8,128)(2,1)} copy(bf16[48,16,2048]{2,1,0:T(8,128)(2,1)} %param.14) | data formatting | bytes 6291456 | tf_op args[0]
  10.5 0.0 copy-done.6
  10.5 0.0 copy-done.7
  10.5 6.6 %fusion.12.f_ref = bf16[8,16,32,64]{3,2,1,0:T(8,128)(2,1)} fusion(bf16[2,2,2,64,48,1,1]{3,4,2,1,0,6,5:T(8,128)(2,1)S(1)} %bitcast.113, bf16[48,8,2,16,2,32,2]{0,6,5,4,3,2,1:T(2,128)(2,1)} %bitcast.94, f32[8,16,32]{2,1,0:T(8,128)S(1)} %fusion.51, f32[64]{0:T(128)S(1)} %copy-done.7), kind=kOutput, calls=%fused_computation.14 | convolution fusion | flops 202375168 | bytes 3735808 | tf_op jit(solution)/shard_map/abkoi,izkybxa->zyxo/dot_general | solution.py:194
  17.1 0.0 copy-start.1
  17.1 0.0 copy-start.8
  17.1 19.4 %shard_map.149 = bf16[10,20,36,192]{3,2,1,0:T(8,128)(2,1)} custom-call(bf16[8,16,32,64]{3,2,1,0:T(8,128)(2,1)} %fusion.12.f_ref), custom_call_target="tpu_custom_call" | custom-call | tf_op jit(solution)/shard_map/pallas_call | solution.py:135
  36.5 0.1 fusion.50
  36.6 0.2 copy.38
  36.8 0.0 copy-done.1
  36.8 0.2 copy.36
  37.1 0.0 copy-done.8
  37.1 12.3 %multiply_convert_fusion = bf16[10,18,34,64]{3,0,2,1:T(8,128)(2,1)S(1)} fusion(f32[10,18,34]{0,2,1:T(8,128)S(1)} %copy.38, f32[64]{0:T(128)S(1)} %copy-done.8, bf16[3,3,192,64]{3,2,1,0:T(8,128)(2,1)S(1)} %bitcast.106, bf16[10,20,36,192]{3,2,1,0:T(8,128)(2,1)} %shard_map.149), kind=kOutput, calls=%fused_computation.4 | convolution fusion | flops 1355212800 | bytes 3794080 | tf_op jit(solution)/shard_map/conv_general_dilated | solution.py:148
  49.4 1.7 %fusion.61 = (bf16[8,18,34,64]{3,0,2,1:T(8,128)(2,1)S(1)}, bf16[8,18,34,64]{3,0,2,1:T(8,128)(2,1)S(1)}, bf16[8,18,34,64]{3,0,2,1:T(8,128)(2,1)}) fusion(bf16[10,18,34,64]{3,0,2,1:T(8,128)(2,1)S(1)} %multiply_convert_fusion), kind=kLoop, calls=%fused_computation.70 | loop fusion | bytes 3760128 | tf_op jit(solution)/shard_map/slice | solution.py:174
  51.2 2.0 %copy.39 = bf16[3,3,3,64,64]{3,4,2,0,1:T(8,128)(2,1)} copy(bf16[3,3,3,64,64]{4,3,2,1,0:T(8,128)(2,1)} %bitcast.104) | data formatting | bytes 442368 | tf_op jit(solution)/shard_map/reshape | solution.py:175
  53.1 0.0 copy-start.3
  53.1 6.7 %fusion.4 = f32[8,16,32,64]{3,0,2,1:T(8,128)S(1)} fusion(bf16[3,3,192,64]{3,2,1,0:T(8,128)(2,1)} %bitcast.105, bf16[8,18,34,64]{3,0,2,1:T(8,128)(2,1)S(1)} %get-tuple-element.7, bf16[8,18,34,64]{3,0,2,1:T(8,128)(2,1)} %get-tuple-element.8, bf16[8,18,34,64]{3,0,2,1:T(8,128)(2,1)S(1)} %get-tuple-element.6), kind=kOutput, calls=%fused_computation.5 | convolution fusion | flops 911609856 | bytes 3149824 | tf_op jit(solution)/shard_map/conv_general_dilated | solution.py:177
  59.9 0.0 copy-done.3
  59.9 0.0 copy-start.5
  59.9 0.0 copy-start.9
  59.9 1.0 %fusion.15 = bf16[8,16,32,64]{3,2,1,0:T(8,128)(2,1)S(1)} fusion(f32[8,16,32,64]{3,0,2,1:T(8,128)S(1)} %fusion.4, f32[64]{0:T(128)S(1)} %copy-done.3, f32[8,16,32]{2,1,0:T(8,128)S(1)} %fusion.51), kind=kLoop, calls=%fused_computation.18 | loop fusion | flops 1048576 | bytes 1589504 | tf_op jit(solution)/shard_map/convert_element_type | solution.py:169
  60.9 0.1 copy.43
  61.1 0.1 fusion.53
  61.2 0.0 copy-done.5
  61.2 0.0 copy-done.9
  61.2 1.0 %fusion.27.f_ref = bf16[4,8,16,96]{3,2,1,0:T(8,128)(2,1)} fusion(bf16[2,2,2,96,64,1,1]{3,4,2,1,0,6,5:T(8,128)(2,1)S(1)} %bitcast.112, bf16[4,2,8,2,16,2,64]{6,5,4,3,2,1,0:T(2,128)(2,1)S(1)} %bitcast.95, f32[4,8,16]{2,1,0:T(8,128)S(1)} %fusion.53, f32[96]{0:T(128)S(1)} %copy-done.9), kind=kOutput, calls=%fused_computation.31 | convolution fusion | flops 50528256 | bytes 723328 | tf_op jit(solution)/shard_map/abkoi,zkybxai->zyxo/dot_general | solution.py:201
  62.2 8.9 %shard_map.150 = bf16[8,12,20,96]{3,2,1,0:T(8,128)(2,1)} custom-call(bf16[4,8,16,96]{3,2,1,0:T(8,128)(2,1)} %fusion.27.f_ref), custom_call_target="tpu_custom_call" | custom-call | tf_op jit(solution)/shard_map/pallas_call | solution.py:135
  71.1 0.0 copy-start.10
  71.1 0.0 copy-start.12
  71.1 1.3 %copy.61 = bf16[8,12,1,20,96]{4,0,3,1,2:T(8,128)(2,1)S(1)} copy(bf16[8,12,1,20,96]{4,3,1,0,2:T(8,128)(2,1)} %bitcast.97) | data formatting | bytes 737280
  72.4 0.1 pad.8.clone
  72.6 0.1 copy.46
  72.6 0.1 slice.38
  72.8 0.0 copy-done
  72.8 0.0 copy-done.10
  72.8 0.0 copy-done.12
  72.8 2.8 %fusion.22 = f32[6,10,8,3,96]{4,2,3,1,0:T(8,128)S(1)} fusion(bf16[8,12,1,7,2,96]{5,3,4,1,0,2:T(8,128)(2,1)S(1)} %slice.38, bf16[8,12,1,8,3,96]{5,3,4,1,0,2:T(8,128)(2,1)S(1)} %copy.46, bf16[3,3,3,96,96]{4,3,2,1,0:T(8,128)(2,1)S(1)} %bitcast.93, f32[96]{0:T(128)S(1)} %copy-done.10, pred[8,3]{0,1:T(4,128)(4,1)S(1)} %copy-done.12), kind=kOutput, calls=%fused_computation.23 | convolution fusion | flops 719262720 | bytes 1751448 | tf_op jit(solution)/shard_map/conv_general_dilated | solution.py:184
  75.6 0.3 copy.48
  75.9 0.3 reshape.94
  76.2 0.0 copy-start.4
  76.3 0.0 copy-start.11
  76.3 0.1 fusion.52
  76.4 0.3 fusion.35
  76.6 0.1 pad.10
  76.7 0.2 reshape.97
  76.9 0.1 copy.50
  77.0 0.1 slice.41
  77.1 0.3 copy-done.4
  77.3 0.0 copy-done.11
  77.3 0.0 copy-start.2
  77.3 1.5 %convolution_select_fusion.1 = f32[4,8,8,3,96]{4,2,3,1,0:T(8,128)S(1)} fusion(bf16[3,3,3,96,96]{4,3,2,1,0:T(8,128)(2,1)S(1)} %bitcast.111, bf16[6,10,1,7,2,96]{5,3,4,1,0,2:T(8,128)(2,1)S(1)} %slice.41, bf16[6,10,1,8,3,96]{5,3,4,1,0,2:T(8,128)(2,1)S(1)} %copy.50, pred[8,3]{0,1:T(4,128)(4,1)S(1)} %copy-done.11), kind=kOutput, calls=%fused_computation.26 | convolution fusion | flops 383662080 | bytes 1230360 | tf_op jit(solution)/shard_map/conv_general_dilated | solution.py:184
  78.9 0.1 copy.52
  79.0 0.0 copy-done.2
  79.0 0.1 fusion.49
  79.1 0.8 copy.55
  79.9 1.7 %copy.54 = bf16[64,8,512]{2,1,0:T(8,128)(2,1)} copy(bf16[64,8,512]{0,2,1:T(8,128)(2,1)S(1)} %bitcast.96) | data formatting | bytes 1048576
  (10 shorter events, 0.1 us)
Async XLA Ops:
  0.6 72.1 %copy-start = (bf16[27,96,96]{2,1,0:T(8,128)(2,1)S(1)}, bf16[27,96,96]{2,1,0:T(8,128)(2,1)}, u32[]{:S(2)}) copy-start(bf16[27,96,96]{2,1,0:T(8,128)(2,1)} %param.24) | copy-start | bytes 1492996
  1.8 8.7 %copy-start.6 = (bf16[8,64,48]{1,2,0:T(8,128)(2,1)S(1)}, bf16[8,64,48]{1,2,0:T(8,128)(2,1)}, u32[]{:S(2)}) copy-start(bf16[8,64,48]{1,2,0:T(8,128)(2,1)} %param.16) | copy-start | bytes 147460
  1.8 8.7 %copy-start.7 = (f32[64]{0:T(128)S(1)}, f32[64]{0:T(128)}, u32[]{:S(2)}) copy-start(f32[64]{0:T(128)} %param.17) | copy-start | bytes 772
  17.1 19.7 %copy-start.1 = (bf16[27,64,64]{2,1,0:T(8,128)(2,1)S(1)}, bf16[27,64,64]{2,1,0:T(8,128)(2,1)}, u32[]{:S(2)}) copy-start(bf16[27,64,64]{2,1,0:T(8,128)(2,1)} %param.18) | copy-start | bytes 663556
  17.1 20.0 %copy-start.8 = (f32[64]{0:T(128)S(1)}, f32[64]{0:T(128)}, u32[]{:S(2)}) copy-start(f32[64]{0:T(128)} %param.19) | copy-start | bytes 772
  53.1 6.8 %copy-start.3 = (f32[64]{0:T(128)S(1)}, f32[64]{0:T(128)}, u32[]{:S(2)}) copy-start(f32[64]{0:T(128)} %param.21) | copy-start | bytes 772
  59.9 1.3 %copy-start.5 = (bf16[8,96,64]{1,2,0:T(8,128)(2,1)S(1)}, bf16[8,96,64]{1,2,0:T(8,128)(2,1)}, u32[]{:S(2)}) copy-start(bf16[8,96,64]{1,2,0:T(8,128)(2,1)} %param.22) | copy-start | bytes 294916
  59.9 1.3 %copy-start.9 = (f32[96]{0:T(128)S(1)}, f32[96]{0:T(128)}, u32[]{:S(2)}) copy-start(f32[96]{0:T(128)} %param.23) | copy-start | bytes 1156
  71.1 1.7 %copy-start.10 = (f32[96]{0:T(128)S(1)}, f32[96]{0:T(128)}, u32[]{:S(2)}) copy-start(f32[96]{0:T(128)} %param.25) | copy-start | bytes 1156
  71.1 1.7 %copy-start.12 = (pred[8,3]{0,1:T(4,128)(4,1)S(1)}, pred[8,3]{0,1:T(4,128)(4,1)}, u32[]{:S(2)}) copy-start(pred[8,3]{0,1:T(4,128)(4,1)} %constant.39) | copy-start | bytes 76
  76.2 1.1 %copy-start.4 = (bf16[27,96,96]{2,1,0:T(8,128)(2,1)S(1)}, bf16[27,96,96]{2,1,0:T(8,128)(2,1)}, u32[]{:S(2)}) copy-start(bf16[27,96,96]{2,1,0:T(8,128)(2,1)} %param.26) | copy-start | bytes 1492996
  76.3 1.1 %copy-start.11 = (pred[8,3]{0,1:T(4,128)(4,1)S(1)}, pred[8,3]{0,1:T(4,128)(4,1)}, u32[]{:S(2)}) copy-start(pred[8,3]{0,1:T(4,128)(4,1)} %constant.38) | copy-start | bytes 76
  77.3 1.7 %copy-start.2 = (f32[96]{0:T(128)S(1)}, f32[96]{0:T(128)}, u32[]{:S(2)}) copy-start(f32[96]{0:T(128)} %param.27) | copy-start | bytes 1156

commit v7 on v6

--- a/solution.py
+++ b/solution.py
@@ -143,11 +143,11 @@
 
 
 def conv_stacked(stacked, weights):
-    kernel = weights.reshape(3, 3, 3, weights.shape[1], weights.shape[2]).transpose(1, 0, 2, 4, 3)
-    kernel = kernel.reshape(3, 3, 3 * weights.shape[2], weights.shape[1])
+    kernel = weights.reshape(3, 3, 3, weights.shape[1], weights.shape[2]).transpose(0, 1, 3, 2, 4)
+    kernel = kernel.reshape(3, 3, weights.shape[1], 3 * weights.shape[2])
     return lax.conv_general_dilated(
         stacked, kernel, (1, 1), "VALID",
-        dimension_numbers=("NHWC", "HWIO", "NHWC"), preferred_element_type=jnp.float32)
+        dimension_numbers=("NHWC", "WHOI", "NHWC"), preferred_element_type=jnp.float32)
 
 
 def region_mask(tissue, repeats, block_starts, extents, margin):
@@ -172,11 +172,11 @@
 def conv_taps(padded, weights):
     size_z = padded.shape[0] - 2
     stacked = jnp.concatenate([padded[k:k + size_z] for k in range(3)], axis=-1)
-    kernel = weights.reshape(3, 3, 3, weights.shape[1], weights.shape[2]).transpose(1, 0, 2, 4, 3)
-    kernel = kernel.reshape(3, 3, 3 * weights.shape[2], weights.shape[1])
+    kernel = weights.reshape(3, 3, 3, weights.shape[1], weights.shape[2]).transpose(0, 1, 3, 2, 4)
+    kernel = kernel.reshape(3, 3, weights.shape[1], 3 * weights.shape[2])
     return lax.conv_general_dilated(
         stacked, kernel, (1, 1), "VALID",
-        dimension_numbers=("NHWC", "HWIO", "NHWC"), preferred_element_type=jnp.float32)
+        dimension_numbers=("NHWC", "WHOI", "NHWC"), preferred_element_type=jnp.float32)
 
 
 def conv_cube(padded, weights):

time: 82.1 us -> 83.6 us (1.018)
  no operation moved by 1% of the time
where the time goes in v7:
time: 83.6 us; the launch traced here: 83.1 us
  matrix products  31.7 us (38%)
  Pallas kernels  28.3 us (34%)
  local copies, waits for them, and re-layouts  19.6 us (23%)
  other arithmetic  2.49 us (3%)
  between operations  0.99 us (1%)
    pallas_call x2, Pallas kernels, with_rim(): pl.pallas_call(functools.partial(rim_kernel, width, stack), out_shape=jax...  28.3 us
    unnamed x30, local copies, waits for them, and re-layouts  12.7 us
    conv_general_dilated x1, matrix products, conv_stacked(): lax.conv_general_dilated(stacked, kernel, (1, 1), 'VALID', dimension_numb...  12.7 us
    conv_general_dilated x1, matrix products, conv_taps(): lax.conv_general_dilated(stacked, kernel, (1, 1), 'VALID', dimension_numb...  7.03 us
    dot_general x1, matrix products, down_first(): jnp.einsum('abkoi,izkybxa->zyxo', grouped, split, preferred_element_type=...  6.57 us
    conv_general_dilated x2, matrix products, conv_cube(): lax.conv_general_dilated(padded[None], kernel, (1, 1, 1), 'VALID', dimens...  4.37 us
    convert_element_type x3, other arithmetic, finish(): (jnp.maximum(summed + offsets, 0.0) * tissue_mask).astype(jnp.bfloat16)  2.16 us
    reshape x1, local copies, waits for them, and re-layouts, conv_taps(): weights.reshape(3, 3, 3, weights.shape[1], weights.shape[2])  1.96 us

profile of v7, /device:TPU:1, one launch (start us, length us, event | category | flops | bytes accessed | tf_op | source)
XLA Modules:
  0.0 83.1 jit_solution(16916259095308588936)
XLA Ops:
  0.6 0.0 copy-start
  0.7 0.9 %pad_dynamic-slice_fusion = s32[10,6,3]{1,2,0:T(4,128)S(1)} fusion(s32[]{:T(128)S(6)} %select_n.6, s32[]{:T(128)S(6)} %select_n.7, s32[]{:T(128)S(6)} %select_n.8, s32[32,32,4]{1,2,0:T(4,128)} %param.15), kind=kLoop, calls=%fused_computation.54 | loop fusion | bytes 17116 | tf_op jit(solution)/shard_map/dynamic_slice | solution.py:157
  1.6 0.1 copy.35
  1.7 0.1 fusion.51
  1.8 0.0 copy-start.6
  1.8 0.0 copy-start.7
  1.8 8.7 %copy.32 = bf16[48,16,2048]{0,2,1:T(8,128)(2,1)} copy(bf16[48,16,2048]{2,1,0:T(8,128)(2,1)} %param.14) | data formatting | bytes 6291456 | tf_op args[0]
  10.5 0.0 copy-done.6
  10.5 0.0 copy-done.7
  10.5 6.6 %fusion.12.f_ref = bf16[8,16,32,64]{3,2,1,0:T(8,128)(2,1)} fusion(bf16[2,2,2,64,48,1,1]{3,4,2,1,0,6,5:T(8,128)(2,1)S(1)} %bitcast.113, bf16[48,8,2,16,2,32,2]{0,6,5,4,3,2,1:T(2,128)(2,1)} %bitcast.94, f32[8,16,32]{2,1,0:T(8,128)S(1)} %fusion.51, f32[64]{0:T(128)S(1)} %copy-done.7), kind=kOutput, calls=%fused_computation.14 | convolution fusion | flops 202375168 | bytes 3735808 | tf_op jit(solution)/shard_map/abkoi,izkybxa->zyxo/dot_general | solution.py:194
  17.1 0.0 copy-start.1
  17.1 0.0 copy-start.8
  17.1 19.4 %shard_map.149 = bf16[10,20,36,192]{3,2,1,0:T(8,128)(2,1)} custom-call(bf16[8,16,32,64]{3,2,1,0:T(8,128)(2,1)} %fusion.12.f_ref), custom_call_target="tpu_custom_call" | custom-call | tf_op jit(solution)/shard_map/pallas_call | solution.py:135
  36.5 0.1 fusion.50
  36.6 0.3 copy.38
  36.9 0.0 copy-done.1
  36.9 0.2 copy.36
  37.1 0.0 copy-done.8
  37.1 12.7 %multiply_convert_fusion = bf16[10,18,34,64]{3,0,1,2:T(8,128)(2,1)S(1)} fusion(f32[10,18,34]{0,1,2:T(8,128)S(1)} %copy.38, f32[64]{0:T(128)S(1)} %copy-done.8, bf16[3,3,64,192]{2,3,1,0:T(8,128)(2,1)S(1)} %bitcast.106, bf16[10,20,36,192]{3,2,1,0:T(8,128)(2,1)} %shard_map.149), kind=kOutput, calls=%fused_computation.4 | convolution fusion | flops 1355212800 | bytes 3794080 | tf_op jit(solution)/shard_map/conv_general_dilated | solution.py:148
  49.9 1.7 %fusion.61 = (bf16[8,18,34,64]{3,0,1,2:T(8,128)(2,1)S(1)}, bf16[8,18,34,64]{3,0,1,2:T(8,128)(2,1)S(1)}, bf16[8,18,34,64]{3,0,1,2:T(8,128)(2,1)}) fusion(bf16[10,18,34,64]{3,0,1,2:T(8,128)(2,1)S(1)} %multiply_convert_fusion), kind=kLoop, calls=%fused_computation.70 | loop fusion | bytes 3760128 | tf_op jit(solution)/shard_map/slice | solution.py:174
  51.6 2.0 %copy.39 = bf16[3,3,3,64,64]{3,4,2,1,0:T(8,128)(2,1)} copy(bf16[3,3,3,64,64]{4,3,2,1,0:T(8,128)(2,1)} %bitcast.104) | data formatting | bytes 442368 | tf_op jit(solution)/shard_map/reshape | solution.py:175
  53.6 0.0 copy-start.3
  53.6 7.0 %fusion.4 = f32[8,16,32,64]{3,0,1,2:T(8,128)S(1)} fusion(bf16[3,3,64,192]{2,3,1,0:T(8,128)(2,1)} %bitcast.105, bf16[8,18,34,64]{3,0,1,2:T(8,128)(2,1)S(1)} %get-tuple-element.7, bf16[8,18,34,64]{3,0,1,2:T(8,128)(2,1)} %get-tuple-element.8, bf16[8,18,34,64]{3,0,1,2:T(8,128)(2,1)S(1)} %get-tuple-element.6), kind=kOutput, calls=%fused_computation.5 | convolution fusion | flops 911609856 | bytes 3149824 | tf_op jit(solution)/shard_map/conv_general_dilated | solution.py:177
  60.6 0.0 copy-done.3
  60.6 0.0 copy-start.5
  60.6 0.0 copy-start.9
  60.7 1.8 %fusion.15 = bf16[8,16,32,64]{3,2,1,0:T(8,128)(2,1)S(1)} fusion(f32[8,16,32,64]{3,0,1,2:T(8,128)S(1)} %fusion.4, f32[64]{0:T(128)S(1)} %copy-done.3, f32[8,16,32]{2,1,0:T(8,128)S(1)} %fusion.51), kind=kLoop, calls=%fused_computation.18 | loop fusion | flops 1048576 | bytes 1589504 | tf_op jit(solution)/shard_map/convert_element_type | solution.py:169
  62.5 0.1 copy.43
  62.6 0.1 fusion.53
  62.7 0.0 copy-done.5
  62.7 0.0 copy-done.9
  62.7 1.0 %fusion.27.f_ref = bf16[4,8,16,96]{3,2,1,0:T(8,128)(2,1)} fusion(bf16[2,2,2,96,64,1,1]{3,4,2,1,0,6,5:T(8,128)(2,1)S(1)} %bitcast.112, bf16[4,2,8,2,16,2,64]{6,5,4,3,2,1,0:T(2,128)(2,1)S(1)} %bitcast.95, f32[4,8,16]{2,1,0:T(8,128)S(1)} %fusion.53, f32[96]{0:T(128)S(1)} %copy-done.9), kind=kOutput, calls=%fused_computation.31 | convolution fusion | flops 50528256 | bytes 723328 | tf_op jit(solution)/shard_map/abkoi,zkybxai->zyxo/dot_general | solution.py:201
  63.7 8.9 %shard_map.150 = bf16[8,12,20,96]{3,2,1,0:T(8,128)(2,1)} custom-call(bf16[4,8,16,96]{3,2,1,0:T(8,128)(2,1)} %fusion.27.f_ref), custom_call_target="tpu_custom_call" | custom-call | tf_op jit(solution)/shard_map/pallas_call | solution.py:135
  72.7 0.0 copy-start.10
  72.7 0.0 copy-start.12
  72.7 1.3 %copy.61 = bf16[8,12,1,20,96]{4,0,3,1,2:T(8,128)(2,1)S(1)} copy(bf16[8,12,1,20,96]{4,3,1,0,2:T(8,128)(2,1)} %bitcast.97) | data formatting | bytes 737280
  74.0 0.1 pad.8.clone
  74.1 0.1 copy.46
  74.2 0.1 slice.38
  74.3 0.0 copy-done
  74.3 0.0 copy-done.10
  74.3 0.0 copy-done.12
  74.3 2.8 %fusion.22 = f32[6,10,8,3,96]{4,2,3,1,0:T(8,128)S(1)} fusion(bf16[8,12,1,7,2,96]{5,3,4,1,0,2:T(8,128)(2,1)S(1)} %slice.38, bf16[8,12,1,8,3,96]{5,3,4,1,0,2:T(8,128)(2,1)S(1)} %copy.46, bf16[3,3,3,96,96]{4,3,2,1,0:T(8,128)(2,1)S(1)} %bitcast.93, f32[96]{0:T(128)S(1)} %copy-done.10, pred[8,3]{0,1:T(4,128)(4,1)S(1)} %copy-done.12), kind=kOutput, calls=%fused_computation.23 | convolution fusion | flops 719262720 | bytes 1751448 | tf_op jit(solution)/shard_map/conv_general_dilated | solution.py:184
  77.2 0.3 copy.48
  77.4 0.3 reshape.94
  77.8 0.0 copy-start.4
  77.8 0.0 copy-start.11
  77.8 0.1 fusion.52
  77.9 0.3 fusion.35
  78.2 0.1 pad.10
  78.3 0.2 reshape.97
  78.5 0.1 copy.50
  78.5 0.1 slice.41
  78.6 0.3 copy-done.4
  78.9 0.0 copy-done.11
  78.9 0.0 copy-start.2
  78.9 1.5 %convolution_select_fusion.1 = f32[4,8,8,3,96]{4,2,3,1,0:T(8,128)S(1)} fusion(bf16[3,3,3,96,96]{4,3,2,1,0:T(8,128)(2,1)S(1)} %bitcast.111, bf16[6,10,1,7,2,96]{5,3,4,1,0,2:T(8,128)(2,1)S(1)} %slice.41, bf16[6,10,1,8,3,96]{5,3,4,1,0,2:T(8,128)(2,1)S(1)} %copy.50, pred[8,3]{0,1:T(4,128)(4,1)S(1)} %copy-done.11), kind=kOutput, calls=%fused_computation.26 | convolution fusion | flops 383662080 | bytes 1230360 | tf_op jit(solution)/shard_map/conv_general_dilated | solution.py:184
  80.4 0.1 copy.52
  80.6 0.0 copy-done.2
  80.6 0.1 fusion.49
  80.7 0.8 copy.55
  81.5 1.7 %copy.54 = bf16[64,8,512]{2,1,0:T(8,128)(2,1)} copy(bf16[64,8,512]{0,2,1:T(8,128)(2,1)S(1)} %bitcast.96) | data formatting | bytes 1048576
  (10 shorter events, 0.1 us)
Async XLA Ops:
  0.6 73.7 %copy-start = (bf16[27,96,96]{2,1,0:T(8,128)(2,1)S(1)}, bf16[27,96,96]{2,1,0:T(8,128)(2,1)}, u32[]{:S(2)}) copy-start(bf16[27,96,96]{2,1,0:T(8,128)(2,1)} %param.24) | copy-start | bytes 1492996
  1.8 8.7 %copy-start.6 = (bf16[8,64,48]{1,2,0:T(8,128)(2,1)S(1)}, bf16[8,64,48]{1,2,0:T(8,128)(2,1)}, u32[]{:S(2)}) copy-start(bf16[8,64,48]{1,2,0:T(8,128)(2,1)} %param.16) | copy-start | bytes 147460
  1.8 8.7 %copy-start.7 = (f32[64]{0:T(128)S(1)}, f32[64]{0:T(128)}, u32[]{:S(2)}) copy-start(f32[64]{0:T(128)} %param.17) | copy-start | bytes 772
  17.1 19.8 %copy-start.1 = (bf16[27,64,64]{2,1,0:T(8,128)(2,1)S(1)}, bf16[27,64,64]{2,1,0:T(8,128)(2,1)}, u32[]{:S(2)}) copy-start(bf16[27,64,64]{2,1,0:T(8,128)(2,1)} %param.18) | copy-start | bytes 663556
  17.1 20.0 %copy-start.8 = (f32[64]{0:T(128)S(1)}, f32[64]{0:T(128)}, u32[]{:S(2)}) copy-start(f32[64]{0:T(128)} %param.19) | copy-start | bytes 772
  53.6 7.0 %copy-start.3 = (f32[64]{0:T(128)S(1)}, f32[64]{0:T(128)}, u32[]{:S(2)}) copy-start(f32[64]{0:T(128)} %param.21) | copy-start | bytes 772
  60.6 2.1 %copy-start.5 = (bf16[8,96,64]{1,2,0:T(8,128)(2,1)S(1)}, bf16[8,96,64]{1,2,0:T(8,128)(2,1)}, u32[]{:S(2)}) copy-start(bf16[8,96,64]{1,2,0:T(8,128)(2,1)} %param.22) | copy-start | bytes 294916
  60.6 2.1 %copy-start.9 = (f32[96]{0:T(128)S(1)}, f32[96]{0:T(128)}, u32[]{:S(2)}) copy-start(f32[96]{0:T(128)} %param.23) | copy-start | bytes 1156
  72.7 1.7 %copy-start.10 = (f32[96]{0:T(128)S(1)}, f32[96]{0:T(128)}, u32[]{:S(2)}) copy-start(f32[96]{0:T(128)} %param.25) | copy-start | bytes 1156
  72.7 1.7 %copy-start.12 = (pred[8,3]{0,1:T(4,128)(4,1)S(1)}, pred[8,3]{0,1:T(4,128)(4,1)}, u32[]{:S(2)}) copy-start(pred[8,3]{0,1:T(4,128)(4,1)} %constant.39) | copy-start | bytes 76
  77.8 1.1 %copy-start.4 = (bf16[27,96,96]{2,1,0:T(8,128)(2,1)S(1)}, bf16[27,96,96]{2,1,0:T(8,128)(2,1)}, u32[]{:S(2)}) copy-start(bf16[27,96,96]{2,1,0:T(8,128)(2,1)} %param.26) | copy-start | bytes 1492996
  77.8 1.1 %copy-start.11 = (pred[8,3]{0,1:T(4,128)(4,1)S(1)}, pred[8,3]{0,1:T(4,128)(4,1)}, u32[]{:S(2)}) copy-start(pred[8,3]{0,1:T(4,128)(4,1)} %constant.38) | copy-start | bytes 76
  78.9 1.7 %copy-start.2 = (f32[96]{0:T(128)S(1)}, f32[96]{0:T(128)}, u32[]{:S(2)}) copy-start(f32[96]{0:T(128)} %param.27) | copy-start | bytes 1156

commit v8 on v6

--- a/solution.py
+++ b/solution.py
@@ -142,6 +142,114 @@
     )(field)
 
 
+def rim_any_kernel(width, owners, f_ref, p_ref, local_sem, send_sem, recv_sem):
+    sizes = f_ref.shape[:3]
+    index = [lax.axis_index(a) for a in AXES]
+    count = [lax.axis_size(a) for a in AXES]
+
+    def exists(d):
+        ok = True
+        for a in range(3):
+            if d[a] == -1:
+                ok = jnp.logical_and(ok, index[a] > 0)
+            elif d[a] == 1:
+                ok = jnp.logical_and(ok, index[a] < count[a] - 1)
+        return ok
+
+    def device(d):
+        return tuple(index[a] + d[a] for a in range(3))
+
+    def source(k, step):
+        s = sizes[k]
+        if step == -1:
+            return slice(0, width)
+        if step == 1:
+            return slice(s - width, s)
+        return slice(0, s)
+
+    def side(k, step):
+        s = sizes[k]
+        if step == -1:
+            return slice(0, width)
+        if step == 1:
+            return slice(s + width, s + 2 * width)
+        return slice(width, width + s)
+
+    def window(pick, d, sign):
+        return tuple(pick(k, sign * d[owners[k]]) for k in range(3)) + (slice(None),)
+
+    barrier = pltpu.get_barrier_semaphore()
+    for d in DIRS:
+        @pl.when(exists(d))
+        def _():
+            pl.semaphore_signal(barrier, inc=1, device_id=device(d), device_id_type=MESH)
+
+    interior = tuple(slice(width, width + sizes[k]) for k in range(3)) + (slice(None),)
+    local = pltpu.make_async_copy(f_ref, p_ref.at[interior], local_sem.at[0])
+    local.start()
+
+    for d in DIRS:
+        @pl.when(jnp.logical_not(exists(d)))
+        def _():
+            region = p_ref.at[window(side, d, 1)]
+            region[...] = jnp.zeros(region.shape, region.dtype)
+
+    peers = 1
+    for a in range(3):
+        below = (index[a] + count[a] - 1) // count[a]
+        above = (2 * count[a] - 2 - index[a]) // count[a]
+        peers = peers * (1 + below + above)
+    pl.semaphore_wait(barrier, peers - 1)
+
+    copies = []
+    for k, d in enumerate(DIRS):
+        copy = pltpu.make_async_remote_copy(
+            src_ref=f_ref.at[window(source, d, 1)],
+            dst_ref=p_ref.at[window(side, d, -1)],
+            send_sem=send_sem.at[k],
+            recv_sem=recv_sem.at[k],
+            device_id=device(d),
+            device_id_type=MESH,
+        )
+        copies.append((d, copy))
+
+        @pl.when(exists(d))
+        def _():
+            copy.start()
+
+    local.wait()
+    for d, copy in copies:
+        @pl.when(exists(d))
+        def _():
+            copy.wait_send()
+
+        @pl.when(exists(tuple(-v for v in d)))
+        def _():
+            copy.wait_recv()
+
+
+def with_rim_any(field, width, owners, collective_id):
+    sizes = field.shape[:3]
+    return pl.pallas_call(
+        functools.partial(rim_any_kernel, width, owners),
+        out_shape=jax.ShapeDtypeStruct(
+            tuple(s + 2 * width for s in sizes) + (field.shape[3],), field.dtype),
+        in_specs=[pl.BlockSpec(memory_space=pltpu.VMEM)],
+        out_specs=pl.BlockSpec(memory_space=pltpu.VMEM),
+        scratch_shapes=[
+            pltpu.SemaphoreType.DMA((1,)),
+            pltpu.SemaphoreType.DMA((len(DIRS),)),
+            pltpu.SemaphoreType.DMA((len(DIRS),)),
+        ],
+        compiler_params=pltpu.CompilerParams(collective_id=collective_id, has_side_effects=True),
+    )(field)
+
+
+def rim_yxz(field, width, collective_id):
+    rimmed = with_rim_any(field.transpose(1, 2, 0, 3), width, (1, 0, 2), collective_id)
+    return rimmed.transpose(2, 0, 1, 3)
+
+
 def conv_stacked(stacked, weights):
     kernel = weights.reshape(3, 3, 3, weights.shape[1], weights.shape[2]).transpose(1, 0, 2, 4, 3)
     kernel = kernel.reshape(3, 3, 3 * weights.shape[2], weights.shape[1])
@@ -228,7 +336,7 @@
     mask_two = region_mask(tissue, (2, 2, 4), second_blocks, (second_x, second_y, second_z), 0)
     mask_two_wide = region_mask(tissue, (2, 2, 4), second_blocks, (second_x, second_y, second_z), 1)
     down_two = finish(down_cells(feat_one, w_down2), b_down2, mask_two)
-    middle = finish(conv_cube(with_rim(down_two, 2, 1, False), w_conv2a), b_conv2a, mask_two_wide)
+    middle = finish(conv_cube(rim_yxz(down_two, 2, 1), w_conv2a), b_conv2a, mask_two_wide)
     feat_two = finish(conv_cube(middle, w_conv2b), b_conv2b, mask_two)
     return (packed(feat_one), packed(feat_two))
 

time: 82.1 us -> 82.6 us (level)
  other arithmetic: 1.69 us -> 2.65 us
    pallas_call x2 -> x1, Pallas kernels: 28.3 us -> 19.4 us  [with_rim(): pl.pallas_call(functools.partial(rim_kernel, width, stack), out_shape=jax...]
    pallas_call x0 -> x1, Pallas kernels: none -> 8.89 us  [with_rim_any(): pl.pallas_call(functools.partial(rim_any_kernel, width, owners), out_shap...]
    unnamed x30 -> x29, local copies, waits for them, and re-layouts: 12.7 us -> 11.5 us
    broadcast_in_dim x1, local copies, waits for them, and re-layouts: 0.14 us -> 1.16 us  [conv_cube(): padded[None]]
    convert_element_type x3 -> x4, other arithmetic: 1.35 us -> 2.31 us  [finish(): (jnp.maximum(summed + offsets, 0.0) * tissue_mask).astype(jnp.bfloat16)]
where the time goes in v8:
time: 82.6 us; the launch traced here: 82.1 us
  matrix products  30.4 us (37%)
  Pallas kernels  28.2 us (34%)
  local copies, waits for them, and re-layouts  19.9 us (24%)
  other arithmetic  2.65 us (3%)
  between operations  1 us (1%)
    pallas_call x1, Pallas kernels, with_rim(): pl.pallas_call(functools.partial(rim_kernel, width, stack), out_shape=jax...  19.4 us
    conv_general_dilated x1, matrix products, conv_stacked(): lax.conv_general_dilated(stacked, kernel, (1, 1), 'VALID', dimension_numb...  12.3 us
    unnamed x29, local copies, waits for them, and re-layouts  11.5 us
    pallas_call x1, Pallas kernels, with_rim_any(): pl.pallas_call(functools.partial(rim_any_kernel, width, owners), out_shap...  8.89 us
    conv_general_dilated x1, matrix products, conv_taps(): lax.conv_general_dilated(stacked, kernel, (1, 1), 'VALID', dimension_numb...  6.76 us
    dot_general x1, matrix products, down_first(): jnp.einsum('abkoi,izkybxa->zyxo', grouped, split, preferred_element_type=...  6.56 us
    conv_general_dilated x2, matrix products, conv_cube(): lax.conv_general_dilated(padded[None], kernel, (1, 1, 1), 'VALID', dimens...  4.37 us
    convert_element_type x4, other arithmetic, finish(): (jnp.maximum(summed + offsets, 0.0) * tissue_mask).astype(jnp.bfloat16)  2.31 us

profile of v8, /device:TPU:1, one launch (start us, length us, event | category | flops | bytes accessed | tf_op | source)
XLA Modules:
  0.0 82.1 jit_solution(18263952314999634848)
XLA Ops:
  0.6 0.0 copy-start
  0.7 0.9 %pad_dynamic-slice_fusion = s32[10,6,3]{1,2,0:T(4,128)S(1)} fusion(s32[]{:T(128)S(6)} %select_n.6, s32[]{:T(128)S(6)} %select_n.7, s32[]{:T(128)S(6)} %select_n.8, s32[32,32,4]{1,2,0:T(4,128)} %param.15), kind=kLoop, calls=%fused_computation.54 | loop fusion | bytes 17116 | tf_op jit(solution)/shard_map/dynamic_slice | solution.py:265
  1.6 0.1 copy.63
  1.7 0.1 fusion.49
  1.8 0.0 copy-start.7
  1.8 0.0 copy-start.8
  1.8 8.7 %copy.60 = bf16[48,16,2048]{0,2,1:T(8,128)(2,1)} copy(bf16[48,16,2048]{2,1,0:T(8,128)(2,1)} %param.14) | data formatting | bytes 6291456 | tf_op args[0]
  10.5 0.0 copy-done.7
  10.5 0.0 copy-done.8
  10.5 6.6 %fusion.12.f_ref = bf16[8,16,32,64]{3,2,1,0:T(8,128)(2,1)} fusion(bf16[2,2,2,64,48,1,1]{3,4,2,1,0,6,5:T(8,128)(2,1)S(1)} %bitcast.112, bf16[48,8,2,16,2,32,2]{0,6,5,4,3,2,1:T(2,128)(2,1)} %bitcast.94, f32[8,16,32]{2,1,0:T(8,128)S(1)} %fusion.49, f32[64]{0:T(128)S(1)} %copy-done.8), kind=kOutput, calls=%fused_computation.14 | convolution fusion | flops 202375168 | bytes 3735808 | tf_op jit(solution)/shard_map/abkoi,izkybxa->zyxo/dot_general | solution.py:302
  17.1 0.0 copy-start.1
  17.1 0.0 copy-start.9
  17.1 19.4 %shard_map.149 = bf16[10,20,36,192]{3,2,1,0:T(8,128)(2,1)} custom-call(bf16[8,16,32,64]{3,2,1,0:T(8,128)(2,1)} %fusion.12.f_ref), custom_call_target="tpu_custom_call" | custom-call | tf_op jit(solution)/shard_map/pallas_call | solution.py:135
  36.5 0.1 fusion.48
  36.6 0.2 copy.66
  36.8 0.0 copy-done.1
  36.8 0.2 copy.64
  37.1 0.0 copy-done.9
  37.1 12.3 %multiply_convert_fusion = bf16[10,18,34,64]{3,0,2,1:T(8,128)(2,1)S(1)} fusion(f32[10,18,34]{0,2,1:T(8,128)S(1)} %copy.66, f32[64]{0:T(128)S(1)} %copy-done.9, bf16[3,3,192,64]{3,2,1,0:T(8,128)(2,1)S(1)} %bitcast.106, bf16[10,20,36,192]{3,2,1,0:T(8,128)(2,1)} %shard_map.149), kind=kOutput, calls=%fused_computation.4 | convolution fusion | flops 1355212800 | bytes 3794080 | tf_op jit(solution)/shard_map/conv_general_dilated | solution.py:256
  49.4 1.7 %fusion.60 = (bf16[8,18,34,64]{3,0,2,1:T(8,128)(2,1)S(1)}, bf16[8,18,34,64]{3,0,2,1:T(8,128)(2,1)S(1)}, bf16[8,18,34,64]{3,0,2,1:T(8,128)(2,1)}) fusion(bf16[10,18,34,64]{3,0,2,1:T(8,128)(2,1)S(1)} %multiply_convert_fusion), kind=kLoop, calls=%fused_computation.71 | loop fusion | bytes 3760128 | tf_op jit(solution)/shard_map/slice | solution.py:282
  51.2 2.0 %copy.67 = bf16[3,3,3,64,64]{3,4,2,0,1:T(8,128)(2,1)} copy(bf16[3,3,3,64,64]{4,3,2,1,0:T(8,128)(2,1)} %bitcast.104) | data formatting | bytes 442368 | tf_op jit(solution)/shard_map/reshape | solution.py:283
  53.1 0.0 copy-start.4
  53.1 6.8 %fusion.4 = f32[8,16,32,64]{3,0,2,1:T(8,128)S(1)} fusion(bf16[3,3,192,64]{3,2,1,0:T(8,128)(2,1)} %bitcast.105, bf16[8,18,34,64]{3,0,2,1:T(8,128)(2,1)S(1)} %get-tuple-element.9, bf16[8,18,34,64]{3,0,2,1:T(8,128)(2,1)} %get-tuple-element.10, bf16[8,18,34,64]{3,0,2,1:T(8,128)(2,1)S(1)} %get-tuple-element.8), kind=kOutput, calls=%fused_computation.5 | convolution fusion | flops 911609856 | bytes 3149824 | tf_op jit(solution)/shard_map/conv_general_dilated | solution.py:285
  59.9 0.0 copy-done.4
  59.9 0.0 copy-start.6
  59.9 0.0 copy-start.2
  59.9 1.0 %fusion.15 = bf16[8,16,32,64]{3,2,1,0:T(8,128)(2,1)S(1)} fusion(f32[8,16,32,64]{3,0,2,1:T(8,128)S(1)} %fusion.4, f32[64]{0:T(128)S(1)} %copy-done.4, f32[8,16,32]{2,1,0:T(8,128)S(1)} %fusion.49), kind=kLoop, calls=%fused_computation.18 | loop fusion | flops 1048576 | bytes 1589504 | tf_op jit(solution)/shard_map/convert_element_type | solution.py:277
  60.9 0.0 copy-done.6
  60.9 0.4 convolution_bitcast_fusion
  61.3 0.1 copy.73
  61.5 0.1 fusion.51
  61.6 0.0 copy-start.10
  61.6 0.0 copy-start.12
  61.6 0.1 copy.74
  61.7 0.0 copy-done.2
  61.7 0.9 %fusion.46.f_ref = bf16[8,16,4,96]{3,2,1,0:T(4,128)(2,1)} fusion(f32[4,8,16,96]{3,2,1,0:T(8,128)S(1)} %convolution_bitcast_fusion, f32[96]{0:T(128)S(1)} %copy-done.2, f32[8,16,4]{2,1,0:T(8,128)S(1)} %copy.74), kind=kLoop, calls=%fused_computation.51 | loop fusion | flops 196608 | bytes 297344 | tf_op jit(solution)/shard_map/convert_element_type | solution.py:277
  62.6 8.9 %shard_map.150 = bf16[12,20,8,96]{3,2,1,0:T(8,128)(2,1)} custom-call(bf16[8,16,4,96]{3,2,1,0:T(4,128)(2,1)} %fusion.46.f_ref), custom_call_target="tpu_custom_call" | custom-call | tf_op jit(solution)/shard_map/pallas_call | solution.py:233
  71.5 1.2 %pad.8 = bf16[8,12,1,24,96]{4,0,3,1,2:T(8,128)(2,1)S(1)} pad(bf16[8,12,1,20,96]{4,0,3,1,2:T(8,128)(2,1)} %bitcast.98, bf16[]{:T(256)} %constant.30), padding=0_0x0_0x0_0x0_4x0_0 | pad | bytes 811010 | tf_op jit(solution)/shard_map/broadcast_in_dim | solution.py:293
  72.7 0.1 copy.76
  72.8 0.1 slice.38
  72.9 0.0 copy-done
  72.9 0.0 copy-done.10
  72.9 0.0 copy-done.12
  72.9 2.8 %fusion.22 = f32[6,10,8,3,96]{4,2,3,1,0:T(8,128)S(1)} fusion(bf16[8,12,1,7,2,96]{5,3,4,1,0,2:T(8,128)(2,1)S(1)} %slice.38, bf16[8,12,1,8,3,96]{5,3,4,1,0,2:T(8,128)(2,1)S(1)} %copy.76, bf16[3,3,3,96,96]{4,3,2,1,0:T(8,128)(2,1)S(1)} %bitcast.93, f32[96]{0:T(128)S(1)} %copy-done.10, pred[8,3]{0,1:T(4,128)(4,1)S(1)} %copy-done.12), kind=kOutput, calls=%fused_computation.23 | convolution fusion | flops 719262720 | bytes 1751448 | tf_op jit(solution)/shard_map/conv_general_dilated | solution.py:292
  75.7 0.3 copy.78
  76.0 0.3 reshape.94
  76.4 0.1 fusion.50
  76.5 0.0 copy-start.5
  76.5 0.0 copy-start.11
  76.5 0.3 fusion.31
  76.8 0.1 pad.10
  76.8 0.2 reshape.97
  77.1 0.1 copy.81
  77.1 0.1 slice.41
  77.2 0.3 copy-done.5
  77.5 0.0 copy-done.11
  77.5 0.0 copy-start.3
  77.5 1.5 %convolution_select_fusion.1 = f32[4,8,8,3,96]{4,2,3,1,0:T(8,128)S(1)} fusion(bf16[3,3,3,96,96]{4,3,2,1,0:T(8,128)(2,1)S(1)} %bitcast.110, bf16[6,10,1,7,2,96]{5,3,4,1,0,2:T(8,128)(2,1)S(1)} %slice.41, bf16[6,10,1,8,3,96]{5,3,4,1,0,2:T(8,128)(2,1)S(1)} %copy.81, pred[8,3]{0,1:T(4,128)(4,1)S(1)} %copy-done.11), kind=kOutput, calls=%fused_computation.26 | convolution fusion | flops 383662080 | bytes 1230360 | tf_op jit(solution)/shard_map/conv_general_dilated | solution.py:292
  79.1 0.3 copy.83
  79.4 0.1 copy.84
  79.5 0.0 copy-done.3
  79.5 0.2 fusion.45
  79.7 0.8 copy.86
  80.5 1.7 %copy.85 = bf16[64,8,512]{2,1,0:T(8,128)(2,1)} copy(bf16[64,8,512]{0,2,1:T(8,128)(2,1)S(1)} %bitcast.96) | data formatting | bytes 1048576
  (10 shorter events, 0.1 us)
Async XLA Ops:
  0.6 72.2 %copy-start = (bf16[27,96,96]{2,1,0:T(8,128)(2,1)S(1)}, bf16[27,96,96]{2,1,0:T(8,128)(2,1)}, u32[]{:S(2)}) copy-start(bf16[27,96,96]{2,1,0:T(8,128)(2,1)} %param.24) | copy-start | bytes 1492996
  1.8 8.7 %copy-start.7 = (bf16[8,64,48]{1,2,0:T(8,128)(2,1)S(1)}, bf16[8,64,48]{1,2,0:T(8,128)(2,1)}, u32[]{:S(2)}) copy-start(bf16[8,64,48]{1,2,0:T(8,128)(2,1)} %param.16) | copy-start | bytes 147460
  1.8 8.7 %copy-start.8 = (f32[64]{0:T(128)S(1)}, f32[64]{0:T(128)}, u32[]{:S(2)}) copy-start(f32[64]{0:T(128)} %param.17) | copy-start | bytes 772
  17.1 19.7 %copy-start.1 = (bf16[27,64,64]{2,1,0:T(8,128)(2,1)S(1)}, bf16[27,64,64]{2,1,0:T(8,128)(2,1)}, u32[]{:S(2)}) copy-start(bf16[27,64,64]{2,1,0:T(8,128)(2,1)} %param.18) | copy-start | bytes 663556
  17.1 20.0 %copy-start.9 = (f32[64]{0:T(128)S(1)}, f32[64]{0:T(128)}, u32[]{:S(2)}) copy-start(f32[64]{0:T(128)} %param.19) | copy-start | bytes 772
  53.1 6.8 %copy-start.4 = (f32[64]{0:T(128)S(1)}, f32[64]{0:T(128)}, u32[]{:S(2)}) copy-start(f32[64]{0:T(128)} %param.21) | copy-start | bytes 772
  59.9 1.0 %copy-start.6 = (bf16[8,96,64]{1,2,0:T(8,128)(2,1)S(1)}, bf16[8,96,64]{1,2,0:T(8,128)(2,1)}, u32[]{:S(2)}) copy-start(bf16[8,96,64]{1,2,0:T(8,128)(2,1)} %param.22) | copy-start | bytes 294916
  59.9 1.8 %copy-start.2 = (f32[96]{0:T(128)S(1)}, f32[96]{0:T(128)}, u32[]{:S(2)}) copy-start(f32[96]{0:T(128)} %param.23) | copy-start | bytes 1156
  61.6 11.3 %copy-start.10 = (f32[96]{0:T(128)S(1)}, f32[96]{0:T(128)}, u32[]{:S(2)}) copy-start(f32[96]{0:T(128)} %param.25) | copy-start | bytes 1156
  61.6 11.3 %copy-start.12 = (pred[8,3]{0,1:T(4,128)(4,1)S(1)}, pred[8,3]{0,1:T(4,128)(4,1)}, u32[]{:S(2)}) copy-start(pred[8,3]{0,1:T(4,128)(4,1)} %constant.39) | copy-start | bytes 76
  76.5 1.1 %copy-start.5 = (bf16[27,96,96]{2,1,0:T(8,128)(2,1)S(1)}, bf16[27,96,96]{2,1,0:T(8,128)(2,1)}, u32[]{:S(2)}) copy-start(bf16[27,96,96]{2,1,0:T(8,128)(2,1)} %param.26) | copy-start | bytes 1492996
  76.5 1.1 %copy-start.11 = (pred[8,3]{0,1:T(4,128)(4,1)S(1)}, pred[8,3]{0,1:T(4,128)(4,1)}, u32[]{:S(2)}) copy-start(pred[8,3]{0,1:T(4,128)(4,1)} %constant.38) | copy-start | bytes 76
  77.5 1.9 %copy-start.3 = (f32[96]{0:T(128)S(1)}, f32[96]{0:T(128)}, u32[]{:S(2)}) copy-start(f32[96]{0:T(128)} %param.27) | copy-start | bytes 1156

commit v9 on v6

--- a/solution.py
+++ b/solution.py
@@ -169,14 +169,14 @@
     return (jnp.maximum(summed + offsets, 0.0) * tissue_mask).astype(jnp.bfloat16)
 
 
-def conv_taps(padded, weights):
+def conv_taps(padded, weights, out_spec="NHWC"):
     size_z = padded.shape[0] - 2
     stacked = jnp.concatenate([padded[k:k + size_z] for k in range(3)], axis=-1)
     kernel = weights.reshape(3, 3, 3, weights.shape[1], weights.shape[2]).transpose(1, 0, 2, 4, 3)
     kernel = kernel.reshape(3, 3, 3 * weights.shape[2], weights.shape[1])
     return lax.conv_general_dilated(
         stacked, kernel, (1, 1), "VALID",
-        dimension_numbers=("NHWC", "HWIO", "NHWC"), preferred_element_type=jnp.float32)
+        dimension_numbers=("NHWC", "HWIO", out_spec), preferred_element_type=jnp.float32)
 
 
 def conv_cube(padded, weights):
@@ -220,17 +220,19 @@
     mask_one_wide = region_mask(tissue, (4, 4, 8), first_blocks, (first_x, first_y, first_z), 1)
     down_one = finish(down_first(grid_zero, w_down1), b_down1, mask_one)
     inner_one = finish(conv_stacked(with_rim(down_one, 2, 0, True), w_conv1a), b_conv1a, mask_one_wide)
-    feat_one = finish(conv_taps(inner_one, w_conv1b), b_conv1b, mask_one)
+    summed = conv_taps(inner_one, w_conv1b, "CNHW")
+    feat_one = (jnp.maximum(summed + b_conv1b[:, None, None, None], 0.0) * mask_one[None, ..., 0]).astype(
+        jnp.bfloat16)
     second_x = first_x // 2
     second_y = first_y // 2
     second_z = first_z // 2
     second_blocks = (index_x * (second_x // 2), index_y * (second_y // 2), index_z * (second_z // 4))
     mask_two = region_mask(tissue, (2, 2, 4), second_blocks, (second_x, second_y, second_z), 0)
     mask_two_wide = region_mask(tissue, (2, 2, 4), second_blocks, (second_x, second_y, second_z), 1)
-    down_two = finish(down_cells(feat_one, w_down2), b_down2, mask_two)
+    down_two = finish(down_first(feat_one, w_down2), b_down2, mask_two)
     middle = finish(conv_cube(with_rim(down_two, 2, 1, False), w_conv2a), b_conv2a, mask_two_wide)
     feat_two = finish(conv_cube(middle, w_conv2b), b_conv2b, mask_two)
-    return (packed(feat_one), packed(feat_two))
+    return (feat_one.reshape(feat_one.shape[0], feat_one.shape[1], -1), packed(feat_two))
 
 
 def solution(mesh):

time: 82.1 us -> 83.8 us (1.021)
  matrix products: 31 us -> 33 us
  other arithmetic: 1.69 us -> 0.73 us
    dot_general x1 -> x2, matrix products: 6.57 us -> 9 us  [down_first(): jnp.einsum('abkoi,izkybxa->zyxo', grouped, split, preferred_element_type=...]
    dot_general x1 -> x0, matrix products: 1.02 us -> none  [down_cells(): jnp.einsum('abkoi,zkybxai->zyxo', grouped, split, preferred_element_type=...]
    convert_element_type x3 -> x2, other arithmetic: 1.35 us -> 0.39 us  [finish(): (jnp.maximum(summed + offsets, 0.0) * tissue_mask).astype(jnp.bfloat16)]
where the time goes in v9:
time: 83.8 us; the launch traced here: 83.3 us
  matrix products  33 us (39%)
  Pallas kernels  28.3 us (34%)
  local copies, waits for them, and re-layouts  20.3 us (24%)
  between operations  0.97 us (1%)
    pallas_call x2, Pallas kernels, with_rim(): pl.pallas_call(functools.partial(rim_kernel, width, stack), out_shape=jax...  28.3 us
    unnamed x30, local copies, waits for them, and re-layouts  13.3 us
    conv_general_dilated x1, matrix products, conv_stacked(): lax.conv_general_dilated(stacked, kernel, (1, 1), 'VALID', dimension_numb...  12.3 us
    dot_general x2, matrix products, down_first(): jnp.einsum('abkoi,izkybxa->zyxo', grouped, split, preferred_element_type=...  9 us
    conv_general_dilated x1, matrix products, conv_taps(): lax.conv_general_dilated(stacked, kernel, (1, 1), 'VALID', dimension_numb...  7.29 us
    conv_general_dilated x2, matrix products, conv_cube(): lax.conv_general_dilated(padded[None], kernel, (1, 1, 1), 'VALID', dimens...  4.38 us
    reshape x1, local copies, waits for them, and re-layouts, conv_taps(): weights.reshape(3, 3, 3, weights.shape[1], weights.shape[2])  1.97 us
    slice x1, local copies, waits for them, and re-layouts, conv_taps(): stacked = jnp.concatenate([padded[k:k + size_z] for k in range(3)], axis=-1)  1.75 us

profile of v9, /device:TPU:1, one launch (start us, length us, event | category | flops | bytes accessed | tf_op | source)
XLA Modules:
  0.0 83.3 jit_solution(10251708360524173223)
XLA Ops:
  0.6 0.0 copy-start
  0.7 0.9 %pad_dynamic-slice_fusion = s32[10,6,3]{1,2,0:T(4,128)S(1)} fusion(s32[]{:T(128)S(6)} %select_n.6, s32[]{:T(128)S(6)} %select_n.7, s32[]{:T(128)S(6)} %select_n.8, s32[32,32,4]{1,2,0:T(4,128)} %param.15), kind=kLoop, calls=%fused_computation.51 | loop fusion | bytes 17116 | tf_op jit(solution)/shard_map/dynamic_slice | solution.py:157
  1.6 0.1 copy.35
  1.7 0.1 fusion.50
  1.8 0.0 copy-start.5
  1.8 0.0 copy-start.6
  1.8 8.7 %copy.32 = bf16[48,16,2048]{0,2,1:T(8,128)(2,1)} copy(bf16[48,16,2048]{2,1,0:T(8,128)(2,1)} %param.14) | data formatting | bytes 6291456 | tf_op args[0]
  10.5 0.0 copy-done.5
  10.5 0.0 copy-done.6
  10.5 6.6 %fusion.12.f_ref = bf16[8,16,32,64]{3,2,1,0:T(8,128)(2,1)} fusion(bf16[2,2,2,64,48,1,1]{3,4,2,1,0,6,5:T(8,128)(2,1)S(1)} %bitcast.111, bf16[48,8,2,16,2,32,2]{0,6,5,4,3,2,1:T(2,128)(2,1)} %bitcast.92, f32[8,16,32]{2,1,0:T(8,128)S(1)} %fusion.50, f32[64]{0:T(128)S(1)} %copy-done.6), kind=kOutput, calls=%fused_computation.14 | convolution fusion | flops 202375168 | bytes 3735808 | tf_op jit(solution)/shard_map/abkoi,izkybxa->zyxo/dot_general | solution.py:194
  17.1 0.0 copy-start.2
  17.1 0.0 copy-start.7
  17.1 19.4 %shard_map.149 = bf16[10,20,36,192]{3,2,1,0:T(8,128)(2,1)} custom-call(bf16[8,16,32,64]{3,2,1,0:T(8,128)(2,1)} %fusion.12.f_ref), custom_call_target="tpu_custom_call" | custom-call | tf_op jit(solution)/shard_map/pallas_call | solution.py:135
  36.5 0.1 fusion.49
  36.6 0.2 copy.38
  36.8 0.0 copy-done.2
  36.8 0.2 copy.36
  37.1 0.0 copy-done.7
  37.1 12.3 %multiply_convert_fusion = bf16[10,18,34,64]{3,0,2,1:T(8,128)(2,1)S(1)} fusion(f32[10,18,34]{0,2,1:T(8,128)S(1)} %copy.38, f32[64]{0:T(128)S(1)} %copy-done.7, bf16[3,3,192,64]{3,2,1,0:T(8,128)(2,1)S(1)} %bitcast.104, bf16[10,20,36,192]{3,2,1,0:T(8,128)(2,1)} %shard_map.149), kind=kOutput, calls=%fused_computation.4 | convolution fusion | flops 1355212800 | bytes 3794080 | tf_op jit(solution)/shard_map/conv_general_dilated | solution.py:148
  49.4 0.0 copy-start.8
  49.4 1.7 %fusion.60 = (bf16[8,18,34,64]{3,0,2,1:T(8,128)(2,1)S(1)}, bf16[8,18,34,64]{3,0,2,1:T(8,128)(2,1)S(1)}, bf16[8,18,34,64]{3,0,2,1:T(8,128)(2,1)}) fusion(bf16[10,18,34,64]{3,0,2,1:T(8,128)(2,1)S(1)} %multiply_convert_fusion), kind=kLoop, calls=%fused_computation.67 | loop fusion | bytes 3760128 | tf_op jit(solution)/shard_map/slice | solution.py:174
  51.2 0.1 copy.40
  51.3 2.0 %copy.39 = bf16[3,3,3,64,64]{3,4,2,0,1:T(8,128)(2,1)} copy(bf16[3,3,3,64,64]{4,3,2,1,0:T(8,128)(2,1)} %bitcast.102) | data formatting | bytes 442368 | tf_op jit(solution)/shard_map/reshape | solution.py:175
  53.3 0.0 copy-done.8
  53.3 0.0 copy-start.9
  53.3 7.3 %multiply_convert_fusion.1 = bf16[64,8,16,32]{0,1,3,2:T(8,128)(2,1)} fusion(bf16[3,3,192,64]{3,2,1,0:T(8,128)(2,1)} %bitcast.103, bf16[8,18,34,64]{3,0,2,1:T(8,128)(2,1)S(1)} %get-tuple-element.7, bf16[8,18,34,64]{3,0,2,1:T(8,128)(2,1)} %get-tuple-element.8, bf16[8,18,34,64]{3,0,2,1:T(8,128)(2,1)S(1)} %get-tuple-element.6, f32[8,16,32]{0,2,1:T(8,128)S(1)} %copy.40, ...), kind=kOutput, calls=%fused_computation.15 | convolution fusion | flops 912658432 | bytes 2642176 | tf_op jit(solution)/shard_map/conv_general_dilated | solution.py:177
  60.6 0.1 copy.43
  60.8 0.1 fusion.52
  60.8 0.0 copy-done.9
  60.9 2.4 %fusion.26.f_ref = bf16[4,8,16,96]{3,2,1,0:T(8,128)(2,1)} fusion(bf16[2,2,2,96,64,1,1]{3,4,2,1,0,6,5:T(8,128)(2,1)} %bitcast.110, bf16[64,4,2,8,2,16,2]{0,2,1,6,5,4,3:T(2,128)(2,1)} %bitcast.96, f32[4,8,16]{2,1,0:T(8,128)S(1)} %fusion.52, f32[96]{0:T(128)S(1)} %copy-done.9), kind=kOutput, calls=%fused_computation.28 | convolution fusion | flops 50528256 | bytes 723328 | tf_op jit(solution)/shard_map/abkoi,izkybxa->zyxo/dot_general | solution.py:194
  63.3 8.9 %shard_map.150 = bf16[8,12,20,96]{3,2,1,0:T(8,128)(2,1)} custom-call(bf16[4,8,16,96]{3,2,1,0:T(8,128)(2,1)} %fusion.26.f_ref), custom_call_target="tpu_custom_call" | custom-call | tf_op jit(solution)/shard_map/pallas_call | solution.py:135
  72.2 0.0 copy-start.10
  72.2 0.0 copy-start.12
  72.2 1.3 %copy.61 = bf16[8,12,1,20,96]{4,0,3,1,2:T(8,128)(2,1)S(1)} copy(bf16[8,12,1,20,96]{4,3,1,0,2:T(8,128)(2,1)} %bitcast.93) | data formatting | bytes 737280
  73.5 0.1 pad.8.clone
  73.6 0.1 copy.46
  73.7 0.1 slice.38
  73.8 0.0 copy-done
  73.9 0.0 copy-done.10
  73.9 0.0 copy-done.12
  73.9 2.8 %fusion.21 = f32[6,10,8,3,96]{4,2,3,1,0:T(8,128)S(1)} fusion(bf16[8,12,1,7,2,96]{5,3,4,1,0,2:T(8,128)(2,1)S(1)} %slice.38, bf16[8,12,1,8,3,96]{5,3,4,1,0,2:T(8,128)(2,1)S(1)} %copy.46, bf16[3,3,3,96,96]{4,3,2,1,0:T(8,128)(2,1)S(1)} %bitcast.91, f32[96]{0:T(128)S(1)} %copy-done.10, pred[8,3]{0,1:T(4,128)(4,1)S(1)} %copy-done.12), kind=kOutput, calls=%fused_computation.20 | convolution fusion | flops 719262720 | bytes 1751448 | tf_op jit(solution)/shard_map/conv_general_dilated | solution.py:184
  76.7 0.3 copy.48
  77.0 0.3 reshape.95
  77.3 0.0 copy-start.4
  77.4 0.0 copy-start.11
  77.4 0.1 fusion.51
  77.5 0.3 fusion.34
  77.7 0.1 pad.10
  77.8 0.2 reshape.98
  78.0 0.1 copy.50
  78.1 0.1 slice.41
  78.2 0.3 copy-done.4
  78.4 0.0 copy-done.11
  78.4 0.0 copy-start.3
  78.4 1.5 %convolution_select_fusion.1 = f32[4,8,8,3,96]{4,2,3,1,0:T(8,128)S(1)} fusion(bf16[3,3,3,96,96]{4,3,2,1,0:T(8,128)(2,1)S(1)} %bitcast.109, bf16[6,10,1,7,2,96]{5,3,4,1,0,2:T(8,128)(2,1)S(1)} %slice.41, bf16[6,10,1,8,3,96]{5,3,4,1,0,2:T(8,128)(2,1)S(1)} %copy.50, pred[8,3]{0,1:T(4,128)(4,1)S(1)} %copy-done.11), kind=kOutput, calls=%fused_computation.23 | convolution fusion | flops 383662080 | bytes 1230360 | tf_op jit(solution)/shard_map/conv_general_dilated | solution.py:184
  80.0 0.0 copy-start.1
  80.0 0.1 copy.52
  80.1 0.0 copy-done.3
  80.1 0.1 fusion.48
  80.3 0.8 copy.55
  81.0 0.2 copy-done.1
  81.2 2.1 %copy.54 = bf16[64,8,512]{2,1,0:T(8,128)(2,1)} copy(bf16[64,8,512]{0,1,2:T(8,128)(2,1)S(1)} %bitcast.97) | data formatting | bytes 1048576
  (10 shorter events, 0.1 us)
Async XLA Ops:
  0.6 73.2 %copy-start = (bf16[27,96,96]{2,1,0:T(8,128)(2,1)S(1)}, bf16[27,96,96]{2,1,0:T(8,128)(2,1)}, u32[]{:S(2)}) copy-start(bf16[27,96,96]{2,1,0:T(8,128)(2,1)} %param.24) | copy-start | bytes 1492996
  1.8 8.7 %copy-start.5 = (bf16[8,64,48]{1,2,0:T(8,128)(2,1)S(1)}, bf16[8,64,48]{1,2,0:T(8,128)(2,1)}, u32[]{:S(2)}) copy-start(bf16[8,64,48]{1,2,0:T(8,128)(2,1)} %param.16) | copy-start | bytes 147460
  1.8 8.7 %copy-start.6 = (f32[64]{0:T(128)S(1)}, f32[64]{0:T(128)}, u32[]{:S(2)}) copy-start(f32[64]{0:T(128)} %param.17) | copy-start | bytes 772
  17.1 19.7 %copy-start.2 = (bf16[27,64,64]{2,1,0:T(8,128)(2,1)S(1)}, bf16[27,64,64]{2,1,0:T(8,128)(2,1)}, u32[]{:S(2)}) copy-start(bf16[27,64,64]{2,1,0:T(8,128)(2,1)} %param.18) | copy-start | bytes 663556
  17.1 20.0 %copy-start.7 = (f32[64]{0:T(128)S(1)}, f32[64]{0:T(128)}, u32[]{:S(2)}) copy-start(f32[64]{0:T(128)} %param.19) | copy-start | bytes 772
  49.4 3.9 %copy-start.8 = (f32[64]{0:T(128)S(1)}, f32[64]{0:T(128)}, u32[]{:S(2)}) copy-start(f32[64]{0:T(128)} %param.21) | copy-start | bytes 772
  53.3 7.6 %copy-start.9 = (f32[96]{0:T(128)S(1)}, f32[96]{0:T(128)}, u32[]{:S(2)}) copy-start(f32[96]{0:T(128)} %param.23) | copy-start | bytes 1156
  72.2 1.7 %copy-start.10 = (f32[96]{0:T(128)S(1)}, f32[96]{0:T(128)}, u32[]{:S(2)}) copy-start(f32[96]{0:T(128)} %param.25) | copy-start | bytes 1156
  72.2 1.7 %copy-start.12 = (pred[8,3]{0,1:T(4,128)(4,1)S(1)}, pred[8,3]{0,1:T(4,128)(4,1)}, u32[]{:S(2)}) copy-start(pred[8,3]{0,1:T(4,128)(4,1)} %constant.40) | copy-start | bytes 76
  77.3 1.1 %copy-start.4 = (bf16[27,96,96]{2,1,0:T(8,128)(2,1)S(1)}, bf16[27,96,96]{2,1,0:T(8,128)(2,1)}, u32[]{:S(2)}) copy-start(bf16[27,96,96]{2,1,0:T(8,128)(2,1)} %param.26) | copy-start | bytes 1492996
  77.4 1.1 %copy-start.11 = (pred[8,3]{0,1:T(4,128)(4,1)S(1)}, pred[8,3]{0,1:T(4,128)(4,1)}, u32[]{:S(2)}) copy-start(pred[8,3]{0,1:T(4,128)(4,1)} %constant.39) | copy-start | bytes 76
  78.4 1.7 %copy-start.3 = (f32[96]{0:T(128)S(1)}, f32[96]{0:T(128)}, u32[]{:S(2)}) copy-start(f32[96]{0:T(128)} %param.27) | copy-start | bytes 1156
  80.0 1.2 %copy-start.1 = (bf16[64,8,16,32]{0,1,3,2:T(8,128)(2,1)S(1)}, bf16[64,8,16,32]{0,1,3,2:T(8,128)(2,1)}, u32[]{:S(2)}) copy-start(bf16[64,8,16,32]{0,1,3,2:T(8,128)(2,1)} %multiply_convert_fusion.1) | copy-start | bytes 1572868

commit v10 on v6

--- a/solution.py
+++ b/solution.py
@@ -18,6 +18,7 @@
     for dz in (-1, 0, 1)
     if (dx, dy, dz) != (0, 0, 0)
 ]
+DIRS.sort(key=lambda d: sum(abs(v) for v in d))
 
 
 def rim_kernel(width, stack, f_ref, *refs):

time: 82.1 us -> 83.4 us (1.016)
  Pallas kernels: 28.3 us -> 29.6 us
    pallas_call x2, Pallas kernels: 28.3 us -> 29.6 us  [with_rim(): pl.pallas_call(functools.partial(rim_kernel, width, stack), out_shape=jax...]
where the time goes in v10:
time: 83.4 us; the launch traced here: 82.9 us
  matrix products  31 us (37%)
  Pallas kernels  29.6 us (35%)
  local copies, waits for them, and re-layouts  19.6 us (24%)
  other arithmetic  1.69 us (2%)
  between operations  0.99 us (1%)
    pallas_call x2, Pallas kernels, with_rim(): pl.pallas_call(functools.partial(rim_kernel, width, stack), out_shape=jax...  29.6 us
    unnamed x30, local copies, waits for them, and re-layouts  12.7 us
    conv_general_dilated x1, matrix products, conv_stacked(): lax.conv_general_dilated(stacked, kernel, (1, 1), 'VALID', dimension_numb...  12.3 us
    conv_general_dilated x1, matrix products, conv_taps(): lax.conv_general_dilated(stacked, kernel, (1, 1), 'VALID', dimension_numb...  6.74 us
    dot_general x1, matrix products, down_first(): jnp.einsum('abkoi,izkybxa->zyxo', grouped, split, preferred_element_type=...  6.57 us
    conv_general_dilated x2, matrix products, conv_cube(): lax.conv_general_dilated(padded[None], kernel, (1, 1, 1), 'VALID', dimens...  4.37 us
    reshape x1, local copies, waits for them, and re-layouts, conv_taps(): weights.reshape(3, 3, 3, weights.shape[1], weights.shape[2])  1.96 us
    slice x1, local copies, waits for them, and re-layouts, conv_taps(): stacked = jnp.concatenate([padded[k:k + size_z] for k in range(3)], axis=-1)  1.75 us

profile of v10, /device:TPU:1, one launch (start us, length us, event | category | flops | bytes accessed | tf_op | source)
XLA Modules:
  0.0 82.9 jit_solution(14029967887311620994)
XLA Ops:
  0.6 0.0 copy-start
  0.7 0.9 %pad_dynamic-slice_fusion = s32[10,6,3]{1,2,0:T(4,128)S(1)} fusion(s32[]{:T(128)S(6)} %select_n.6, s32[]{:T(128)S(6)} %select_n.7, s32[]{:T(128)S(6)} %select_n.8, s32[32,32,4]{1,2,0:T(4,128)} %param.15), kind=kLoop, calls=%fused_computation.54 | loop fusion | bytes 17116 | tf_op jit(solution)/shard_map/dynamic_slice | solution.py:158
  1.6 0.1 copy.35
  1.7 0.1 fusion.51
  1.8 0.0 copy-start.6
  1.8 0.0 copy-start.7
  1.8 8.7 %copy.32 = bf16[48,16,2048]{0,2,1:T(8,128)(2,1)} copy(bf16[48,16,2048]{2,1,0:T(8,128)(2,1)} %param.14) | data formatting | bytes 6291456 | tf_op args[0]
  10.5 0.0 copy-done.6
  10.5 0.0 copy-done.7
  10.5 6.6 %fusion.12.f_ref = bf16[8,16,32,64]{3,2,1,0:T(8,128)(2,1)} fusion(bf16[2,2,2,64,48,1,1]{3,4,2,1,0,6,5:T(8,128)(2,1)S(1)} %bitcast.113, bf16[48,8,2,16,2,32,2]{0,6,5,4,3,2,1:T(2,128)(2,1)} %bitcast.94, f32[8,16,32]{2,1,0:T(8,128)S(1)} %fusion.51, f32[64]{0:T(128)S(1)} %copy-done.7), kind=kOutput, calls=%fused_computation.14 | convolution fusion | flops 202375168 | bytes 3735808 | tf_op jit(solution)/shard_map/abkoi,izkybxa->zyxo/dot_general | solution.py:195
  17.1 0.0 copy-start.1
  17.1 0.0 copy-start.8
  17.1 19.4 %shard_map.149 = bf16[10,20,36,192]{3,2,1,0:T(8,128)(2,1)} custom-call(bf16[8,16,32,64]{3,2,1,0:T(8,128)(2,1)} %fusion.12.f_ref), custom_call_target="tpu_custom_call" | custom-call | tf_op jit(solution)/shard_map/pallas_call | solution.py:136
  36.5 0.1 fusion.50
  36.6 0.2 copy.38
  36.8 0.0 copy-done.1
  36.8 0.2 copy.36
  37.1 0.0 copy-done.8
  37.1 12.3 %multiply_convert_fusion = bf16[10,18,34,64]{3,0,2,1:T(8,128)(2,1)S(1)} fusion(f32[10,18,34]{0,2,1:T(8,128)S(1)} %copy.38, f32[64]{0:T(128)S(1)} %copy-done.8, bf16[3,3,192,64]{3,2,1,0:T(8,128)(2,1)S(1)} %bitcast.106, bf16[10,20,36,192]{3,2,1,0:T(8,128)(2,1)} %shard_map.149), kind=kOutput, calls=%fused_computation.4 | convolution fusion | flops 1355212800 | bytes 3794080 | tf_op jit(solution)/shard_map/conv_general_dilated | solution.py:149
  49.4 1.7 %fusion.61 = (bf16[8,18,34,64]{3,0,2,1:T(8,128)(2,1)S(1)}, bf16[8,18,34,64]{3,0,2,1:T(8,128)(2,1)S(1)}, bf16[8,18,34,64]{3,0,2,1:T(8,128)(2,1)}) fusion(bf16[10,18,34,64]{3,0,2,1:T(8,128)(2,1)S(1)} %multiply_convert_fusion), kind=kLoop, calls=%fused_computation.70 | loop fusion | bytes 3760128 | tf_op jit(solution)/shard_map/slice | solution.py:175
  51.2 2.0 %copy.39 = bf16[3,3,3,64,64]{3,4,2,0,1:T(8,128)(2,1)} copy(bf16[3,3,3,64,64]{4,3,2,1,0:T(8,128)(2,1)} %bitcast.104) | data formatting | bytes 442368 | tf_op jit(solution)/shard_map/reshape | solution.py:176
  53.1 0.0 copy-start.3
  53.1 6.7 %fusion.4 = f32[8,16,32,64]{3,0,2,1:T(8,128)S(1)} fusion(bf16[3,3,192,64]{3,2,1,0:T(8,128)(2,1)} %bitcast.105, bf16[8,18,34,64]{3,0,2,1:T(8,128)(2,1)S(1)} %get-tuple-element.7, bf16[8,18,34,64]{3,0,2,1:T(8,128)(2,1)} %get-tuple-element.8, bf16[8,18,34,64]{3,0,2,1:T(8,128)(2,1)S(1)} %get-tuple-element.6), kind=kOutput, calls=%fused_computation.5 | convolution fusion | flops 911609856 | bytes 3149824 | tf_op jit(solution)/shard_map/conv_general_dilated | solution.py:178
  59.9 0.0 copy-done.3
  59.9 0.0 copy-start.5
  59.9 0.0 copy-start.9
  59.9 1.0 %fusion.15 = bf16[8,16,32,64]{3,2,1,0:T(8,128)(2,1)S(1)} fusion(f32[8,16,32,64]{3,0,2,1:T(8,128)S(1)} %fusion.4, f32[64]{0:T(128)S(1)} %copy-done.3, f32[8,16,32]{2,1,0:T(8,128)S(1)} %fusion.51), kind=kLoop, calls=%fused_computation.18 | loop fusion | flops 1048576 | bytes 1589504 | tf_op jit(solution)/shard_map/convert_element_type | solution.py:170
  60.9 0.1 copy.43
  61.1 0.1 fusion.53
  61.2 0.0 copy-done.5
  61.2 0.0 copy-done.9
  61.2 1.0 %fusion.27.f_ref = bf16[4,8,16,96]{3,2,1,0:T(8,128)(2,1)} fusion(bf16[2,2,2,96,64,1,1]{3,4,2,1,0,6,5:T(8,128)(2,1)S(1)} %bitcast.112, bf16[4,2,8,2,16,2,64]{6,5,4,3,2,1,0:T(2,128)(2,1)S(1)} %bitcast.95, f32[4,8,16]{2,1,0:T(8,128)S(1)} %fusion.53, f32[96]{0:T(128)S(1)} %copy-done.9), kind=kOutput, calls=%fused_computation.31 | convolution fusion | flops 50528256 | bytes 723328 | tf_op jit(solution)/shard_map/abkoi,zkybxai->zyxo/dot_general | solution.py:202
  62.2 10.2 %shard_map.150 = bf16[8,12,20,96]{3,2,1,0:T(8,128)(2,1)} custom-call(bf16[4,8,16,96]{3,2,1,0:T(8,128)(2,1)} %fusion.27.f_ref), custom_call_target="tpu_custom_call" | custom-call | tf_op jit(solution)/shard_map/pallas_call | solution.py:136
  72.4 0.0 copy-start.10
  72.5 0.0 copy-start.12
  72.5 1.3 %copy.61 = bf16[8,12,1,20,96]{4,0,3,1,2:T(8,128)(2,1)S(1)} copy(bf16[8,12,1,20,96]{4,3,1,0,2:T(8,128)(2,1)} %bitcast.97) | data formatting | bytes 737280
  73.7 0.1 pad.8.clone
  73.9 0.1 copy.46
  74.0 0.1 slice.38
  74.1 0.0 copy-done
  74.1 0.0 copy-done.10
  74.1 0.0 copy-done.12
  74.1 2.8 %fusion.22 = f32[6,10,8,3,96]{4,2,3,1,0:T(8,128)S(1)} fusion(bf16[8,12,1,7,2,96]{5,3,4,1,0,2:T(8,128)(2,1)S(1)} %slice.38, bf16[8,12,1,8,3,96]{5,3,4,1,0,2:T(8,128)(2,1)S(1)} %copy.46, bf16[3,3,3,96,96]{4,3,2,1,0:T(8,128)(2,1)S(1)} %bitcast.93, f32[96]{0:T(128)S(1)} %copy-done.10, pred[8,3]{0,1:T(4,128)(4,1)S(1)} %copy-done.12), kind=kOutput, calls=%fused_computation.23 | convolution fusion | flops 719262720 | bytes 1751448 | tf_op jit(solution)/shard_map/conv_general_dilated | solution.py:185
  76.9 0.3 copy.48
  77.2 0.3 reshape.94
  77.6 0.0 copy-start.4
  77.6 0.0 copy-start.11
  77.6 0.1 fusion.52
  77.7 0.3 fusion.35
  78.0 0.1 pad.10
  78.0 0.2 reshape.97
  78.3 0.1 copy.50
  78.3 0.1 slice.41
  78.4 0.3 copy-done.4
  78.7 0.0 copy-done.11
  78.7 0.0 copy-start.2
  78.7 1.5 %convolution_select_fusion.1 = f32[4,8,8,3,96]{4,2,3,1,0:T(8,128)S(1)} fusion(bf16[3,3,3,96,96]{4,3,2,1,0:T(8,128)(2,1)S(1)} %bitcast.111, bf16[6,10,1,7,2,96]{5,3,4,1,0,2:T(8,128)(2,1)S(1)} %slice.41, bf16[6,10,1,8,3,96]{5,3,4,1,0,2:T(8,128)(2,1)S(1)} %copy.50, pred[8,3]{0,1:T(4,128)(4,1)S(1)} %copy-done.11), kind=kOutput, calls=%fused_computation.26 | convolution fusion | flops 383662080 | bytes 1230360 | tf_op jit(solution)/shard_map/conv_general_dilated | solution.py:185
  80.2 0.1 copy.52
  80.3 0.0 copy-done.2
  80.3 0.1 fusion.49
  80.5 0.8 copy.55
  81.2 1.7 %copy.54 = bf16[64,8,512]{2,1,0:T(8,128)(2,1)} copy(bf16[64,8,512]{0,2,1:T(8,128)(2,1)S(1)} %bitcast.96) | data formatting | bytes 1048576
  (10 shorter events, 0.1 us)
Async XLA Ops:
  0.6 73.5 %copy-start = (bf16[27,96,96]{2,1,0:T(8,128)(2,1)S(1)}, bf16[27,96,96]{2,1,0:T(8,128)(2,1)}, u32[]{:S(2)}) copy-start(bf16[27,96,96]{2,1,0:T(8,128)(2,1)} %param.24) | copy-start | bytes 1492996
  1.8 8.7 %copy-start.6 = (bf16[8,64,48]{1,2,0:T(8,128)(2,1)S(1)}, bf16[8,64,48]{1,2,0:T(8,128)(2,1)}, u32[]{:S(2)}) copy-start(bf16[8,64,48]{1,2,0:T(8,128)(2,1)} %param.16) | copy-start | bytes 147460
  1.8 8.7 %copy-start.7 = (f32[64]{0:T(128)S(1)}, f32[64]{0:T(128)}, u32[]{:S(2)}) copy-start(f32[64]{0:T(128)} %param.17) | copy-start | bytes 772
  17.1 19.7 %copy-start.1 = (bf16[27,64,64]{2,1,0:T(8,128)(2,1)S(1)}, bf16[27,64,64]{2,1,0:T(8,128)(2,1)}, u32[]{:S(2)}) copy-start(bf16[27,64,64]{2,1,0:T(8,128)(2,1)} %param.18) | copy-start | bytes 663556
  17.1 20.0 %copy-start.8 = (f32[64]{0:T(128)S(1)}, f32[64]{0:T(128)}, u32[]{:S(2)}) copy-start(f32[64]{0:T(128)} %param.19) | copy-start | bytes 772
  53.1 6.8 %copy-start.3 = (f32[64]{0:T(128)S(1)}, f32[64]{0:T(128)}, u32[]{:S(2)}) copy-start(f32[64]{0:T(128)} %param.21) | copy-start | bytes 772
  59.9 1.3 %copy-start.5 = (bf16[8,96,64]{1,2,0:T(8,128)(2,1)S(1)}, bf16[8,96,64]{1,2,0:T(8,128)(2,1)}, u32[]{:S(2)}) copy-start(bf16[8,96,64]{1,2,0:T(8,128)(2,1)} %param.22) | copy-start | bytes 294916
  59.9 1.3 %copy-start.9 = (f32[96]{0:T(128)S(1)}, f32[96]{0:T(128)}, u32[]{:S(2)}) copy-start(f32[96]{0:T(128)} %param.23) | copy-start | bytes 1156
  72.4 1.7 %copy-start.10 = (f32[96]{0:T(128)S(1)}, f32[96]{0:T(128)}, u32[]{:S(2)}) copy-start(f32[96]{0:T(128)} %param.25) | copy-start | bytes 1156
  72.5 1.7 %copy-start.12 = (pred[8,3]{0,1:T(4,128)(4,1)S(1)}, pred[8,3]{0,1:T(4,128)(4,1)}, u32[]{:S(2)}) copy-start(pred[8,3]{0,1:T(4,128)(4,1)} %constant.39) | copy-start | bytes 76
  77.6 1.1 %copy-start.4 = (bf16[27,96,96]{2,1,0:T(8,128)(2,1)S(1)}, bf16[27,96,96]{2,1,0:T(8,128)(2,1)}, u32[]{:S(2)}) copy-start(bf16[27,96,96]{2,1,0:T(8,128)(2,1)} %param.26) | copy-start | bytes 1492996
  77.6 1.1 %copy-start.11 = (pred[8,3]{0,1:T(4,128)(4,1)S(1)}, pred[8,3]{0,1:T(4,128)(4,1)}, u32[]{:S(2)}) copy-start(pred[8,3]{0,1:T(4,128)(4,1)} %constant.38) | copy-start | bytes 76
  78.7 1.7 %copy-start.2 = (f32[96]{0:T(128)S(1)}, f32[96]{0:T(128)}, u32[]{:S(2)}) copy-start(f32[96]{0:T(128)} %param.27) | copy-start | bytes 1156

commit v11 on v6

--- a/solution.py
+++ b/solution.py
@@ -216,8 +216,8 @@
     first_y = CY // 2
     first_z = volume.shape[1] // 2
     first_blocks = (index_x * (first_x // 4), index_y * (first_y // 4), index_z * (first_z // 8))
-    mask_one = region_mask(tissue, (4, 4, 8), first_blocks, (first_x, first_y, first_z), 0)
     mask_one_wide = region_mask(tissue, (4, 4, 8), first_blocks, (first_x, first_y, first_z), 1)
+    mask_one = mask_one_wide[1:-1, 1:-1, 1:-1]
     down_one = finish(down_first(grid_zero, w_down1), b_down1, mask_one)
     inner_one = finish(conv_stacked(with_rim(down_one, 2, 0, True), w_conv1a), b_conv1a, mask_one_wide)
     feat_one = finish(conv_taps(inner_one, w_conv1b), b_conv1b, mask_one)
@@ -225,8 +225,8 @@
     second_y = first_y // 2
     second_z = first_z // 2
     second_blocks = (index_x * (second_x // 2), index_y * (second_y // 2), index_z * (second_z // 4))
-    mask_two = region_mask(tissue, (2, 2, 4), second_blocks, (second_x, second_y, second_z), 0)
     mask_two_wide = region_mask(tissue, (2, 2, 4), second_blocks, (second_x, second_y, second_z), 1)
+    mask_two = mask_two_wide[1:-1, 1:-1, 1:-1]
     down_two = finish(down_cells(feat_one, w_down2), b_down2, mask_two)
     middle = finish(conv_cube(with_rim(down_two, 2, 1, False), w_conv2a), b_conv2a, mask_two_wide)
     feat_two = finish(conv_cube(middle, w_conv2b), b_conv2b, mask_two)

time: 82.1 us -> 82.1 us (level)
  no operation moved by 1% of the time
where the time goes in v11:
time: 82.1 us; the launch traced here: 81.6 us
  matrix products  31 us (38%)
  Pallas kernels  28.3 us (34%)
  local copies, waits for them, and re-layouts  19.8 us (24%)
  other arithmetic  1.53 us (2%)
  between operations  0.98 us (1%)
    pallas_call x2, Pallas kernels, with_rim(): pl.pallas_call(functools.partial(rim_kernel, width, stack), out_shape=jax...  28.3 us
    unnamed x30, local copies, waits for them, and re-layouts  12.8 us
    conv_general_dilated x1, matrix products, conv_stacked(): lax.conv_general_dilated(stacked, kernel, (1, 1), 'VALID', dimension_numb...  12.3 us
    conv_general_dilated x1, matrix products, conv_taps(): lax.conv_general_dilated(stacked, kernel, (1, 1), 'VALID', dimension_numb...  6.76 us
    dot_general x1, matrix products, down_first(): jnp.einsum('abkoi,izkybxa->zyxo', grouped, split, preferred_element_type=...  6.55 us
    conv_general_dilated x2, matrix products, conv_cube(): lax.conv_general_dilated(padded[None], kernel, (1, 1, 1), 'VALID', dimens...  4.38 us
    reshape x1, local copies, waits for them, and re-layouts, conv_taps(): weights.reshape(3, 3, 3, weights.shape[1], weights.shape[2])  1.96 us
    slice x1, local copies, waits for them, and re-layouts, conv_taps(): stacked = jnp.concatenate([padded[k:k + size_z] for k in range(3)], axis=-1)  1.74 us

profile of v11, /device:TPU:1, one launch (start us, length us, event | category | flops | bytes accessed | tf_op | source)
XLA Modules:
  0.0 81.6 jit_solution(11563893157687733635)
XLA Ops:
  0.6 0.0 copy-start
  0.7 0.9 %pad_dynamic-slice_fusion = s32[10,6,3]{1,2,0:T(4,128)S(1)} fusion(s32[]{:T(128)S(6)} %select_n.12, s32[]{:T(128)S(6)} %select_n.13, s32[]{:T(128)S(6)} %select_n.14, s32[32,32,4]{1,2,0:T(4,128)} %param.15), kind=kLoop, calls=%fused_computation.54 | loop fusion | bytes 17116 | tf_op jit(solution)/shard_map/dynamic_slice | solution.py:157
  1.6 0.1 copy.35
  1.7 0.1 fusion.50
  1.8 0.1 slice_bitcast_fusion
  1.9 0.0 copy-start.6
  1.9 0.0 copy-start.7
  1.9 8.7 %copy.32 = bf16[48,16,2048]{0,2,1:T(8,128)(2,1)} copy(bf16[48,16,2048]{2,1,0:T(8,128)(2,1)} %param.14) | data formatting | bytes 6291456 | tf_op args[0]
  10.6 0.0 copy-done.6
  10.6 0.0 copy-done.7
  10.6 6.6 %fusion.12.f_ref = bf16[8,16,32,64]{3,2,1,0:T(8,128)(2,1)} fusion(bf16[2,2,2,64,48,1,1]{3,4,2,1,0,6,5:T(8,128)(2,1)S(1)} %bitcast.117, bf16[48,8,2,16,2,32,2]{0,6,5,4,3,2,1:T(2,128)(2,1)} %bitcast.100, f32[8,16,32]{2,1,0:T(8,128)S(1)} %slice_bitcast_fusion, f32[64]{0:T(128)S(1)} %copy-done.7), kind=kOutput, calls=%fused_computation.14 | convolution fusion | flops 202375168 | bytes 3735808 | tf_op jit(solution)/shard_map/abkoi,izkybxa->zyxo/dot_general | solution.py:194
  17.1 0.0 copy-start.1
  17.1 0.0 copy-start.8
  17.2 19.4 %shard_map.149 = bf16[10,20,36,192]{3,2,1,0:T(8,128)(2,1)} custom-call(bf16[8,16,32,64]{3,2,1,0:T(8,128)(2,1)} %fusion.12.f_ref), custom_call_target="tpu_custom_call" | custom-call | tf_op jit(solution)/shard_map/pallas_call | solution.py:135
  36.5 0.2 copy.38
  36.8 0.0 copy-done.1
  36.8 0.2 copy.36
  37.0 0.0 copy-done.8
  37.0 12.3 %multiply_convert_fusion = bf16[10,18,34,64]{3,0,2,1:T(8,128)(2,1)S(1)} fusion(f32[10,18,34]{0,2,1:T(8,128)S(1)} %copy.38, f32[64]{0:T(128)S(1)} %copy-done.8, bf16[3,3,192,64]{3,2,1,0:T(8,128)(2,1)S(1)} %bitcast.111, bf16[10,20,36,192]{3,2,1,0:T(8,128)(2,1)} %shard_map.149), kind=kOutput, calls=%fused_computation.4 | convolution fusion | flops 1355212800 | bytes 3794080 | tf_op jit(solution)/shard_map/conv_general_dilated | solution.py:148
  49.4 1.7 %fusion.61 = (bf16[8,18,34,64]{3,0,2,1:T(8,128)(2,1)S(1)}, bf16[8,18,34,64]{3,0,2,1:T(8,128)(2,1)S(1)}, bf16[8,18,34,64]{3,0,2,1:T(8,128)(2,1)}) fusion(bf16[10,18,34,64]{3,0,2,1:T(8,128)(2,1)S(1)} %multiply_convert_fusion), kind=kLoop, calls=%fused_computation.70 | loop fusion | bytes 3760128 | tf_op jit(solution)/shard_map/slice | solution.py:174
  51.1 2.0 %copy.39 = bf16[3,3,3,64,64]{3,4,2,0,1:T(8,128)(2,1)} copy(bf16[3,3,3,64,64]{4,3,2,1,0:T(8,128)(2,1)} %bitcast.109) | data formatting | bytes 442368 | tf_op jit(solution)/shard_map/reshape | solution.py:175
  53.1 0.0 copy-start.3
  53.1 6.8 %fusion.4 = f32[8,16,32,64]{3,0,2,1:T(8,128)S(1)} fusion(bf16[3,3,192,64]{3,2,1,0:T(8,128)(2,1)} %bitcast.110, bf16[8,18,34,64]{3,0,2,1:T(8,128)(2,1)S(1)} %get-tuple-element.7, bf16[8,18,34,64]{3,0,2,1:T(8,128)(2,1)} %get-tuple-element.8, bf16[8,18,34,64]{3,0,2,1:T(8,128)(2,1)S(1)} %get-tuple-element.6), kind=kOutput, calls=%fused_computation.5 | convolution fusion | flops 911609856 | bytes 3149824 | tf_op jit(solution)/shard_map/conv_general_dilated | solution.py:177
  59.8 0.0 copy-done.3
  59.8 0.0 copy-start.5
  59.8 0.0 copy-start.9
  59.9 1.0 %fusion.15 = bf16[8,16,32,64]{3,2,1,0:T(8,128)(2,1)S(1)} fusion(f32[8,16,32,64]{3,0,2,1:T(8,128)S(1)} %fusion.4, f32[64]{0:T(128)S(1)} %copy-done.3, f32[8,16,32]{2,1,0:T(8,128)S(1)} %slice_bitcast_fusion), kind=kLoop, calls=%fused_computation.18 | loop fusion | flops 1048576 | bytes 1589504 | tf_op jit(solution)/shard_map/convert_element_type | solution.py:169
  60.9 0.1 copy.43
  61.0 0.1 fusion.53
  61.1 0.1 slice_bitcast_fusion.1
  61.2 0.0 copy-done.5
  61.2 0.0 copy-done.9
  61.2 1.0 %fusion.27.f_ref = bf16[4,8,16,96]{3,2,1,0:T(8,128)(2,1)} fusion(bf16[2,2,2,96,64,1,1]{3,4,2,1,0,6,5:T(8,128)(2,1)S(1)} %bitcast.116, bf16[4,2,8,2,16,2,64]{6,5,4,3,2,1,0:T(2,128)(2,1)S(1)} %bitcast.101, f32[4,8,16]{2,1,0:T(8,128)S(1)} %slice_bitcast_fusion.1, f32[96]{0:T(128)S(1)} %copy-done.9), kind=kOutput, calls=%fused_computation.31 | convolution fusion | flops 50528256 | bytes 723328 | tf_op jit(solution)/shard_map/abkoi,zkybxai->zyxo/dot_general | solution.py:201
  62.2 8.9 %shard_map.150 = bf16[8,12,20,96]{3,2,1,0:T(8,128)(2,1)} custom-call(bf16[4,8,16,96]{3,2,1,0:T(8,128)(2,1)} %fusion.27.f_ref), custom_call_target="tpu_custom_call" | custom-call | tf_op jit(solution)/shard_map/pallas_call | solution.py:135
  71.1 0.0 copy-start.10
  71.2 0.0 copy-start.12
  71.2 1.3 %copy.61 = bf16[8,12,1,20,96]{4,0,3,1,2:T(8,128)(2,1)S(1)} copy(bf16[8,12,1,20,96]{4,3,1,0,2:T(8,128)(2,1)} %bitcast.103) | data formatting | bytes 737280
  72.4 0.1 pad.6.clone
  72.6 0.1 copy.46
  72.7 0.1 slice.39
  72.8 0.0 copy-done
  72.8 0.0 copy-done.10
  72.8 0.0 copy-done.12
  72.8 2.8 %fusion.22 = f32[6,10,8,3,96]{4,2,3,1,0:T(8,128)S(1)} fusion(bf16[8,12,1,7,2,96]{5,3,4,1,0,2:T(8,128)(2,1)S(1)} %slice.39, bf16[8,12,1,8,3,96]{5,3,4,1,0,2:T(8,128)(2,1)S(1)} %copy.46, bf16[3,3,3,96,96]{4,3,2,1,0:T(8,128)(2,1)S(1)} %bitcast.99, f32[96]{0:T(128)S(1)} %copy-done.10, pred[8,3]{0,1:T(4,128)(4,1)S(1)} %copy-done.12), kind=kOutput, calls=%fused_computation.23 | convolution fusion | flops 719262720 | bytes 1751448 | tf_op jit(solution)/shard_map/conv_general_dilated | solution.py:184
  75.7 0.3 copy.48
  75.9 0.3 reshape.86
  76.3 0.0 copy-start.4
  76.3 0.0 copy-start.11
  76.3 0.3 fusion.35
  76.6 0.1 pad.8
  76.7 0.2 reshape.89
  76.9 0.1 copy.50
  76.9 0.1 slice.41
  77.0 0.4 copy-done.4
  77.4 0.0 copy-done.11
  77.4 0.0 copy-start.2
  77.4 1.5 %convolution_select_fusion.1 = f32[4,8,8,3,96]{4,2,3,1,0:T(8,128)S(1)} fusion(bf16[3,3,3,96,96]{4,3,2,1,0:T(8,128)(2,1)S(1)} %bitcast.115, bf16[6,10,1,7,2,96]{5,3,4,1,0,2:T(8,128)(2,1)S(1)} %slice.41, bf16[6,10,1,8,3,96]{5,3,4,1,0,2:T(8,128)(2,1)S(1)} %copy.50, pred[8,3]{0,1:T(4,128)(4,1)S(1)} %copy-done.11), kind=kOutput, calls=%fused_computation.26 | convolution fusion | flops 383662080 | bytes 1230360 | tf_op jit(solution)/shard_map/conv_general_dilated | solution.py:184
  78.9 0.1 copy.52
  79.0 0.0 copy-done.2
  79.1 0.1 fusion.49
  79.2 0.8 copy.55
  80.0 1.7 %copy.54 = bf16[64,8,512]{2,1,0:T(8,128)(2,1)} copy(bf16[64,8,512]{0,2,1:T(8,128)(2,1)S(1)} %bitcast.102) | data formatting | bytes 1048576
  (10 shorter events, 0.1 us)
Async XLA Ops:
  0.6 72.2 %copy-start = (bf16[27,96,96]{2,1,0:T(8,128)(2,1)S(1)}, bf16[27,96,96]{2,1,0:T(8,128)(2,1)}, u32[]{:S(2)}) copy-start(bf16[27,96,96]{2,1,0:T(8,128)(2,1)} %param.24) | copy-start | bytes 1492996
  1.9 8.7 %copy-start.6 = (bf16[8,64,48]{1,2,0:T(8,128)(2,1)S(1)}, bf16[8,64,48]{1,2,0:T(8,128)(2,1)}, u32[]{:S(2)}) copy-start(bf16[8,64,48]{1,2,0:T(8,128)(2,1)} %param.16) | copy-start | bytes 147460
  1.9 8.7 %copy-start.7 = (f32[64]{0:T(128)S(1)}, f32[64]{0:T(128)}, u32[]{:S(2)}) copy-start(f32[64]{0:T(128)} %param.17) | copy-start | bytes 772
  17.1 19.6 %copy-start.1 = (bf16[27,64,64]{2,1,0:T(8,128)(2,1)S(1)}, bf16[27,64,64]{2,1,0:T(8,128)(2,1)}, u32[]{:S(2)}) copy-start(bf16[27,64,64]{2,1,0:T(8,128)(2,1)} %param.18) | copy-start | bytes 663556
  17.1 19.9 %copy-start.8 = (f32[64]{0:T(128)S(1)}, f32[64]{0:T(128)}, u32[]{:S(2)}) copy-start(f32[64]{0:T(128)} %param.19) | copy-start | bytes 772
  53.1 6.8 %copy-start.3 = (f32[64]{0:T(128)S(1)}, f32[64]{0:T(128)}, u32[]{:S(2)}) copy-start(f32[64]{0:T(128)} %param.21) | copy-start | bytes 772
  59.8 1.4 %copy-start.5 = (bf16[8,96,64]{1,2,0:T(8,128)(2,1)S(1)}, bf16[8,96,64]{1,2,0:T(8,128)(2,1)}, u32[]{:S(2)}) copy-start(bf16[8,96,64]{1,2,0:T(8,128)(2,1)} %param.22) | copy-start | bytes 294916
  59.8 1.3 %copy-start.9 = (f32[96]{0:T(128)S(1)}, f32[96]{0:T(128)}, u32[]{:S(2)}) copy-start(f32[96]{0:T(128)} %param.23) | copy-start | bytes 1156
  71.1 1.7 %copy-start.10 = (f32[96]{0:T(128)S(1)}, f32[96]{0:T(128)}, u32[]{:S(2)}) copy-start(f32[96]{0:T(128)} %param.25) | copy-start | bytes 1156
  71.2 1.7 %copy-start.12 = (pred[8,3]{0,1:T(4,128)(4,1)S(1)}, pred[8,3]{0,1:T(4,128)(4,1)}, u32[]{:S(2)}) copy-start(pred[8,3]{0,1:T(4,128)(4,1)} %constant.39) | copy-start | bytes 76
  76.3 1.1 %copy-start.4 = (bf16[27,96,96]{2,1,0:T(8,128)(2,1)S(1)}, bf16[27,96,96]{2,1,0:T(8,128)(2,1)}, u32[]{:S(2)}) copy-start(bf16[27,96,96]{2,1,0:T(8,128)(2,1)} %param.26) | copy-start | bytes 1492996
  76.3 1.1 %copy-start.11 = (pred[8,3]{0,1:T(4,128)(4,1)S(1)}, pred[8,3]{0,1:T(4,128)(4,1)}, u32[]{:S(2)}) copy-start(pred[8,3]{0,1:T(4,128)(4,1)} %constant.38) | copy-start | bytes 76
  77.4 1.7 %copy-start.2 = (f32[96]{0:T(128)S(1)}, f32[96]{0:T(128)}, u32[]{:S(2)}) copy-start(f32[96]{0:T(128)} %param.27) | copy-start | bytes 1156
